TPU v7x, 256 devices: a whole 4x4x8 slice. The times are simulated.
256 devices in a mesh: grp: 8 (over x, core), dev: 32 (over y, z).
Axes of the slice: x: 4, y: 4, z: 8, core: 2. Of those that a mesh axis runs over, the one named last changes fastest.
Arguments:
- energies: bfloat16 [32768, 32768], P(('grp', 'dev')), may hold values from -48 to 48
- triples: int32 [32768, 3], P(('grp', 'dev')), may hold values from 0 to 113, as said below
- pair_surfaces: float32 [8192, 1024], P('dev'), may hold values from -24 to 24
- pair_slot: int32 [114, 114], replicated, may hold values from 0 to 8191, as said below
- single_surfaces: float32 [128, 32], P('dev'), may hold values from -12 to 12
- modals: float32 [128, 512], P('dev'), may hold values from -1 to 1
- mode_slot: int32 [114], replicated, may hold values from 0 to 127, as said below
Outputs:
- coefficients: bfloat16 [32768, 4096], P(('grp', 'dev'))
- triple_energy: float32 [32768], P(('grp', 'dev'))
- mean_field: float32 [128, 256], P('dev')
Inputs may be any that keep to these rules, and one draw needn't show every extreme that they name: The three modes of a row are distinct. Rows come in blocks of 128, one block to each device in the order of the triples' placement; all rows of a block share their first mode m, and m * (number of groups along grp) // 114 is the block's index along grp. Counting one need for each row and each of its three pairs, the rows of one block need exactly 12 surfaces from each owner along dev, the owner of pair_slot row q being q // 256. `pair_slot`: Symmetric; for two distinct modes it names the row of pair_surfaces that holds their surface, distinct pairs naming distinct rows; the diagonal is 0. `mode_slot`: distinct modes name distinct rows.
All inputs are finite; a program needn't handle non-finite values.
Results may differ from a plain program's by a relative error of at most 0.001.
Values sent between devices are 32-bit elements; how exact they have to be, the bound alone decides.
No kernel may reach another device: no remote copies, remote signals or barrier semaphores. Data moves between devices by JAX's collectives and lax.ppermute only.
A program may use at most 128 MiB of HBM per device.

v0:
```python
import jax
import jax.numpy as jnp
from jax import lax
from jax.sharding import PartitionSpec as P

G = 32
KEEP = 16
S = 16


highest = lax.Precision.HIGHEST


def in_one_piece(arrays, axis, dim, along):
    both = jnp.concatenate(arrays, axis=along)
    out, at, gathered = (lax.all_gather(both, axis, axis=dim, tiled=True), 0, [])
    for a in arrays:
        gathered.append(lax.slice_in_dim(out, at, at + a.shape[along], axis=along))
        at += a.shape[along]
    return tuple(gathered)


def copy_for_each(shard, axis):
    length = lax.axis_size(axis)
    return lax.all_to_all(
        jnp.broadcast_to(shard[None], (length, *shard.shape)), axis, 0, 0, tiled=True
    )


def over_copies(shard, axis):
    everything = copy_for_each(shard, axis)
    return jnp.sum(everything, axis=0)


def split_up(shard, dim, length):
    dims = shard.shape
    tiles = shard.reshape(*dims[:dim], length, dims[dim] // length, *dims[dim + 1 :])
    return jnp.moveaxis(tiles, dim, 0)


def sum_at_owner(shard, axis, dim):
    length = lax.axis_size(axis)
    tiles = lax.all_to_all(split_up(shard, dim, length), axis, 0, 0, tiled=True)
    return jnp.sum(tiles, axis=0)


def tables():
    orders = jnp.arange(KEEP, dtype=jnp.float32)
    points = jnp.arange(G, dtype=jnp.float32) + 0.5
    cosines = jnp.cos(jnp.pi * orders[:, None] * points[None, :] / G)
    weights = jnp.where(orders == 0, 1.0, 2.0) / G
    return (cosines, weights[:, None] * cosines)


def chebyshev_fit(values, fitter):
    number = values.shape[0]
    section_one = jnp.einsum(
        "cg,bgx->bcx", fitter, values.reshape(number, G, G * G), precision=highest
    )
    section_one = section_one.reshape(number, KEEP, G, G)
    section_two = jnp.einsum("dh,bchl->bcdl", fitter, section_one, precision=highest)
    return jnp.einsum("el,bcdl->bcde", fitter, section_two, precision=highest)


def oriented(picked, lower_ends, upper_ends, width):
    square = picked.reshape(-1, width, width)
    return jnp.where((lower_ends < upper_ends)[:, None, None], square, jnp.swapaxes(square, 1, 2))


def body(energies, triples, pair_surfaces, pair_slot, single_surfaces, modals, mode_slot):
    cosines, fitter = tables()
    devices = lax.axis_size("dev")
    number = triples.shape[0]
    pair_rows = pair_surfaces.shape[0]
    mode_rows = modals.shape[0]
    capacity = 3 * number // devices
    shaped = modals.reshape(mode_rows, G, S)
    local_ground = jnp.einsum("mg,cg->mc", shaped[:, :, 0] ** 2, cosines, precision=highest)
    ground, singles = in_one_piece((local_ground, single_surfaces), "dev", 0, 1)
    lead_mode = triples[:, 0]
    second = triples[:, 1]
    third_mode = triples[:, 2]
    lower_ends = jnp.concatenate([lead_mode, lead_mode, second])
    upper_ends = jnp.concatenate([second, third_mode, third_mode])
    pair_ids = pair_slot[lower_ends, upper_ends]
    owners = pair_ids // pair_rows
    local_rows = pair_ids % pair_rows
    owner_hits = (owners[:, None] == jnp.arange(devices, dtype=jnp.int32)[None, :]).astype(
        jnp.int32
    )
    before = jnp.cumsum(owner_hits, axis=0) - owner_hits
    places = owners * capacity + jnp.sum(before * owner_hits, axis=1)
    requests = (
        jnp.zeros((devices * capacity,), jnp.int32)
        .at[places]
        .set(local_rows)
        .reshape(devices, capacity)
    )
    slot_first = mode_slot[lead_mode]
    slot_second = mode_slot[second]
    slot_third = mode_slot[third_mode]
    single_first = singles[slot_first]
    single_second = singles[slot_second]
    single_third = singles[slot_third]
    energy_block = (
        energies.astype(jnp.float32).reshape(number, G, G, G)
        - single_first[:, :, None, None]
        - single_second[:, None, :, None]
        - single_third[:, None, None, :]
    )
    wanted = lax.all_to_all(requests, "dev", split_axis=0, concat_axis=0, tiled=True)
    picked = pair_surfaces[wanted].reshape(wanted.shape + (G, G))
    reduced = jnp.einsum("cg,dh,xygh->xycd", fitter, fitter, picked, precision=highest)
    arrived = lax.all_to_all(
        reduced.reshape(wanted.shape + (KEEP * KEEP,)),
        "dev",
        split_axis=0,
        concat_axis=0,
        tiled=True,
    )
    pair_terms = oriented(
        arrived.reshape(devices * capacity, KEEP * KEEP)[places], lower_ends, upper_ends, KEEP
    )
    rowsum = jnp.sum(fitter, axis=1)
    fitted = (
        chebyshev_fit(energy_block, fitter)
        - pair_terms[:number][:, :, :, None] * rowsum[None, None, None, :]
        - pair_terms[number : 2 * number][:, :, None, :] * rowsum[None, None, :, None]
        - pair_terms[2 * number :][:, None, :, :] * rowsum[None, :, None, None]
    )
    ground_first = ground[slot_first]
    ground_second = ground[slot_second]
    ground_third = ground[slot_third]
    field_first = jnp.einsum(
        "bcde,bd,be->bc", fitted, ground_second, ground_third, precision=highest
    )
    field_second = jnp.einsum(
        "bcde,bc,be->bd", fitted, ground_first, ground_third, precision=highest
    )
    field_third = jnp.einsum(
        "bcde,bc,bd->be", fitted, ground_first, ground_second, precision=highest
    )
    triple_energy = jnp.sum(field_first * ground_first, axis=1)
    slot_ids = jnp.concatenate([slot_first, slot_second, slot_third])
    slot_range = jnp.arange(mode_rows * devices, dtype=jnp.int32)
    onehot = (slot_range[:, None] == slot_ids[None, :]).astype(jnp.float32)
    fields = jnp.concatenate([field_first, field_second, field_third], axis=0)
    partial_value = jnp.dot(onehot, fields, precision=highest)
    across = over_copies(partial_value, "grp")
    owned = sum_at_owner(across, "dev", 0)
    weighted = jnp.dot(owned, cosines, precision=highest)
    mean_field = jnp.einsum("mga,mg,mgb->mab", shaped, weighted, shaped, precision=highest).reshape(
        mode_rows, S * S
    )
    coefficients = fitted.reshape(number, KEEP * KEEP * KEEP).astype(jnp.bfloat16)
    return (coefficients, triple_energy, mean_field)


def solution(mesh):
    in_specs = (
        P(("grp", "dev"), None),
        P(("grp", "dev"), None),
        P("dev", None),
        P(),
        P("dev", None),
        P("dev", None),
        P(),
    )
    out_specs = (P(("grp", "dev"), None), P(("grp", "dev")), P("dev", None))
    return jax.shard_map(body, mesh=mesh, in_specs=in_specs, out_specs=out_specs, check_vma=False)
```

profile of v0, /device:TPU:1, one launch (start us, length us, event | category | flops | bytes accessed | tf_op | source)
XLA Modules:
  0.0 220.9 jit_solution(17617835407005504739)
XLA Ops:
  0.7 0.8 slice_bitcast_fusion
  1.5 4.4 %gather_fusion.6 = s32[384]{0:T(512)S(1)} fusion(s32[114,114]{1,0:T(8,128)} %param.10, s32[384]{0:T(512)S(1)} %fusion.78), kind=kCustom, calls=%fused_computation.6 | custom fusion | bytes 6144 | tf_op jit(solution)/shard_map/gather | solution.py:85
  5.9 0.9 reduce-window.6
  6.8 0.2 slice_reduce_fusion
  7.1 0.1 fusion.19
  7.2 2.9 %scatter_custom_fusion = s32[384]{0:T(512)S(1)} fusion(s32[384]{0:T(512)S(1)} %fusion.72, s32[384]{0:T(512)S(1)} %get-tuple-element.38, s32[]{:T(128)} %constant.29.clone.1), kind=kCustom, calls=%fused_computation.141 | custom fusion | bytes 1540 | tf_op jit(solution)/shard_map/scatter | solution.py:96
  10.1 0.7 all_to_all.17
  10.9 12.0 %all-to-all-start = ((s32[32,1,12]{2,1,0:T(1,128)}), s32[32,1,12]{2,1,0:T(1,128)S(1)}, u32[]{:S(2)}, u32[]{:S(2)}) async-start(s32[32,1,12]{2,1,0:T(1,128)} %bitcast.29), calls=%async_computation | async-start | bytes 32768 | tf_op jit(solution)/shard_map/all_to_all | solution.py:111
  22.9 0.8 reshape.470
  23.7 0.1 fusion.16
  23.8 0.2 fusion.35
  24.1 0.8 maximum_bitcast_fusion
  24.8 37.1 %all-gather = f32[32,4,48]{2,1,0:T(4,128)S(1)} all-gather(f32[1,4,48]{2,1,0:T(4,128)S(1)} %maximum_bitcast_fusion), channel_id=1, replica_groups=mesh['grp'=8,'dev'=32] {'dev'}, dimensions={0}, use_global_device_ids=true | all-gather | bytes 25344 | tf_op jit(solution)/shard_map/all_gather | solution.py:16
  61.9 0.1 slice.69
  62.0 1.2 gather_fusion.2
  63.3 1.2 gather_fusion.4
  64.5 0.6 gather_fusion.3
  65.2 0.6 gather_fusion.5
  65.8 0.6 gather_fusion.10
  66.5 0.6 gather_fusion.9
  67.1 1.2 gather_fusion
  68.4 0.6 gather_fusion.1
  69.0 0.6 gather_fusion.11
  69.8 0.2 copy.86
  70.0 0.1 copy.87
  70.0 0.1 sub.63
  70.1 0.2 copy.88
  70.3 15.9 %copy.135 = f32[16,8,32,1024]{3,2,1,0:T(8,128)} copy(bf16[16,8,32,1024]{3,1,2,0:T(8,128)(2,1)} %bitcast.127) | data formatting | bytes 25165824
  86.2 7.5 %fusion.1 = f32[128,32,1024]{2,1,0:T(8,128)S(1)} fusion(f32[16,8,32,1024]{3,2,1,0:T(8,128)} %copy.135, f32[128,1024]{1,0:T(8,128)S(1)} %copy.88, f32[128,1024]{1,0:T(8,128)S(1)} %copy.86, f32[128,32]{1,0:T(8,128)S(1)} %gather_fusion.1), kind=kLoop, calls=%fused_computation.15 | loop fusion | flops 12582912 | bytes 34619392 | tf_op jit(solution)/shard_map/sub | solution.py:106
  93.7 13.2 %convolution_bitcast_fusion = f32[128,16,1024]{2,1,0:T(8,128)} fusion(f32[128,32,1024]{2,1,0:T(8,128)S(1)} %fusion.1, f32[16]{0:T(128)S(1)} %get-tuple-element.43, f32[32]{0:T(128)S(1)} %iota_add_fusion, f32[16]{0:T(128)S(1)} %get-tuple-element.44), kind=kOutput, calls=%fused_computation.20 | convolution fusion | flops 805307904 | bytes 25166080 | tf_op jit(solution)/shard_map/cg,bgx->bcx/dot_general | solution.py:57
  106.9 1.5 multiply_bitcast_fusion.1
  108.4 8.7 %copy.89 = f32[128,16,1024]{0,2,1:T(8,128)} copy(f32[128,16,1024]{2,1,0:T(8,128)} %convolution_bitcast_fusion) | data formatting | bytes 16777216 | tf_op jit(solution)/shard_map/cg,bgx->bcx/transpose | solution.py:57
  117.1 1.6 copy.130
  118.7 1.1 copy.129
  119.8 0.5 copy.128
  120.3 0.1 reshape.537
  120.5 1.8 gather_fusion.7
  122.3 4.2 %reshape.473 = f32[32,12,32,32]{3,2,1,0:T(8,128)} reshape(f32[384,1024]{1,0:T(8,128)S(1)} %gather_fusion.7) | data formatting | bytes 3145728 | tf_op jit(solution)/shard_map/reshape | solution.py:112
  126.5 5.8 %fusion.28 = f32[32,12,32,16]{2,3,1,0:T(8,128)S(1)} fusion(f32[32,12,32,32]{3,2,1,0:T(8,128)} %reshape.473, f32[16]{0:T(128)S(1)} %get-tuple-element.43, f32[32]{0:T(128)S(1)} %iota_add_fusion, f32[16]{0:T(128)S(1)} %get-tuple-element.44), kind=kOutput, calls=%fused_computation.60 | convolution fusion | flops 75499008 | bytes 2359552 | tf_op jit(solution)/shard_map/cg,dh,xygh->xycd/dot_general | solution.py:113
  132.2 12.7 %fusion.6 = f32[32,12,16,16]{0,3,2,1:T(8,128)S(1)} fusion(f32[32,12,32,16]{2,3,1,0:T(8,128)S(1)} %fusion.28, f32[16]{0:T(128)S(1)} %get-tuple-element.43, f32[32]{0:T(128)S(1)} %iota_add_fusion, f32[16]{0:T(128)S(1)} %get-tuple-element.44), kind=kOutput, calls=%fused_computation.21 | convolution fusion | flops 37750272 | bytes 1179904 | tf_op jit(solution)/shard_map/cg,dh,xygh->xycd/dot_general | solution.py:113
  144.9 1.5 copy.95
  146.4 6.9 %all-to-all-start.1 = ((f32[32,12,256]{2,1,0:T(8,128)}), f32[32,12,256]{2,1,0:T(8,128)S(1)}, u32[]{:S(2)}, u32[]{:S(2)}) async-start(f32[32,12,256]{2,1,0:T(8,128)} %copy.95), calls=%async_computation.1 | async-start | bytes 1048576 | tf_op jit(solution)/shard_map/all_to_all | solution.py:114
  153.3 0.2 fusion.39
  153.6 13.7 %fusion.8 = f32[128,16,16,32]{0,2,3,1:T(8,128)} fusion(f32[128,16,32,32]{0,3,2,1:T(8,128)} %bitcast.126, f32[16]{0:T(128)S(1)} %get-tuple-element.43, f32[32]{0:T(128)S(1)} %iota_add_fusion, f32[16]{0:T(128)S(1)} %get-tuple-element.44), kind=kOutput, calls=%fused_computation.23 | convolution fusion | flops 402654720 | bytes 12583168 | tf_op jit(solution)/shard_map/dh,bchl->bcdl/dot_general | solution.py:61
  167.3 1.7 gather_fusion.8
  168.9 0.2 copy.96
  169.1 0.1 bitcast_select_fusion
  169.3 6.4 %multiply_reduce_fusion = (f32[128,16]{0,1:T(8,128)S(1)}, bf16[128,16,16,16]{0,3,2,1:T(8,128)(2,1)S(1)}, f32[128,16,16,16]{0,3,2,1:T(8,128)S(1)}) fusion(f32[128,16,16]{0,2,1:T(8,128)S(1)} %copy.130, f32[16]{0:T(128)S(1)} %fusion.39, f32[128,16,16]{0,2,1:T(8,128)S(1)} %get-tuple-element.24, f32[128,16,16]{0,2,1:T(8,128)S(1)} %get-tuple-element.25, ...), kind=kOutput, calls=%fused_computation.24 | convolution fusion | flops 206044672 | bytes 7872832 | tf_op jit(solution)/shard_map/el,bcdl->bcde/dot_general | solution.py:62
  175.7 0.2 multiply_reduce_fusion.1
  175.9 0.2 multiply_reduce_fusion.2
  176.0 0.2 fusion.13
  176.2 0.7 broadcast_in_dim.18
  176.9 18.3 %all-to-all-start.2 = ((f32[8,128,16]{1,2,0:T(8,128)}), f32[8,128,16]{1,2,0:T(8,128)S(1)}, u32[]{:S(2)}, u32[]{:S(2)}) async-start(f32[8,128,16]{1,2,0:T(8,128)} %broadcast_in_dim.18), calls=%async_computation.2 | async-start | bytes 131072 | tf_op jit(solution)/shard_map/all_to_all | solution.py:25
  195.2 0.1 copy.112
  195.3 4.8 %all-to-all-done.2 = f32[8,128,16]{1,2,0:T(8,128)S(1)} async-done(((f32[8,128,16]{1,2,0:T(8,128)}), f32[8,128,16]{1,2,0:T(8,128)S(1)}, u32[]{:S(2)}, u32[]{:S(2)}) %all-to-all-start.2) | async-done | bytes 65568 | tf_op jit(solution)/shard_map/all_to_all | solution.py:25
  200.0 0.7 copy.99
  200.7 9.6 %all-to-all-start.3 = ((f32[32,4,16]{2,1,0:T(4,128)}), f32[32,4,16]{2,1,0:T(4,128)S(1)}, u32[]{:S(2)}, u32[]{:S(2)}) async-start(f32[32,4,16]{2,1,0:T(4,128)} %bitcast.36), calls=%async_computation.3 | async-start | bytes 131072 | tf_op jit(solution)/shard_map/all_to_all | solution.py:43
  210.4 0.6 multiply_reduce_fusion.3
  211.0 1.3 copy.103
  212.3 6.9 %all-to-all-done.3 = f32[32,4,16]{2,1,0:T(4,128)S(1)} async-done(((f32[32,4,16]{2,1,0:T(4,128)}), f32[32,4,16]{2,1,0:T(4,128)S(1)}, u32[]{:S(2)}, u32[]{:S(2)}) %all-to-all-start.3) | async-done | bytes 8224 | tf_op jit(solution)/shard_map/all_to_all | solution.py:43
  219.3 0.2 fusion.33
  219.5 0.4 convolution_bitcast_fusion.1
  219.9 0.1 copy.102
  219.9 0.7 reshape.478
  (35 shorter events, 0.5 us)
Async XLA Ops:
  0.6 119.8 %copy-start = (f32[256,1024]{1,0:T(8,128)S(1)}, f32[256,1024]{1,0:T(8,128)}, u32[]{:S(2)}) copy-start(f32[256,1024]{1,0:T(8,128)} %param.9) | copy-start | bytes 3145732
  0.6 61.4 %copy-start.1 = (s32[114]{0:T(128)S(1)}, s32[114]{0:T(128)}, u32[]{:S(2)}) copy-start(s32[114]{0:T(128)} %param.13) | copy-start | bytes 1372
  10.9 109.5 %all-to-all-start = ((s32[32,1,12]{2,1,0:T(1,128)}), s32[32,1,12]{2,1,0:T(1,128)S(1)}, u32[]{:S(2)}, u32[]{:S(2)}) async-start(s32[32,1,12]{2,1,0:T(1,128)} %bitcast.29), calls=%async_computation | async-start | bytes 32768 | tf_op jit(solution)/shard_map/all_to_all | solution.py:111
  146.4 20.8 %all-to-all-start.1 = ((f32[32,12,256]{2,1,0:T(8,128)}), f32[32,12,256]{2,1,0:T(8,128)S(1)}, u32[]{:S(2)}, u32[]{:S(2)}) async-start(f32[32,12,256]{2,1,0:T(8,128)} %copy.95), calls=%async_computation.1 | async-start | bytes 1048576 | tf_op jit(solution)/shard_map/all_to_all | solution.py:114
  169.3 6.4 %copy-start.2 = (f32[128,16,16]{0,2,1:T(8,128)S(1)}, f32[128,16,16]{0,2,1:T(8,128)}, u32[]{:S(2)}) copy-start(f32[128,16,16]{0,2,1:T(8,128)} %copy.129) | copy-start | bytes 393220
  176.9 23.1 %all-to-all-start.2 = ((f32[8,128,16]{1,2,0:T(8,128)}), f32[8,128,16]{1,2,0:T(8,128)S(1)}, u32[]{:S(2)}, u32[]{:S(2)}) async-start(f32[8,128,16]{1,2,0:T(8,128)} %broadcast_in_dim.18), calls=%async_computation.2 | async-start | bytes 131072 | tf_op jit(solution)/shard_map/all_to_all | solution.py:25
  200.7 18.5 %all-to-all-start.3 = ((f32[32,4,16]{2,1,0:T(4,128)}), f32[32,4,16]{2,1,0:T(4,128)S(1)}, u32[]{:S(2)}, u32[]{:S(2)}) async-start(f32[32,4,16]{2,1,0:T(4,128)} %bitcast.36), calls=%async_computation.3 | async-start | bytes 131072 | tf_op jit(solution)/shard_map/all_to_all | solution.py:43
where the time goes:
time: 225 us; the launch traced here: 221 us
  local copies, waits for them, and re-layouts  58.1 us (26%)
  matrix products  52.7 us (23%)
  starting transfers between devices  46.8 us (21%)
  blocking collectives  37.1 us (16%)
  other arithmetic  13.2 us (6%)
  waiting for transfers between devices  11.7 us (5%)
    all_gather x1, blocking collectives, in_one_piece(): lax.all_gather(both, axis, axis=dim, tiled=True)  37.1 us
    unnamed x11, local copies, waits for them, and re-layouts  20.4 us
    dot_general x2, matrix products, body(): jnp.einsum('cg,dh,xygh->xycd', fitter, fitter, picked, precision=highest)  18.5 us
    all_to_all x1, starting transfers between devices, copy_for_each(): lax.all_to_all(jnp.broadcast_to(shard[None], (length, *shard.shape)), axi...  18.3 us
    dot_general x1, matrix products, chebyshev_fit(): jnp.einsum('dh,bchl->bcdl', fitter, section_one, precision=highest)  13.7 us
    dot_general x1, matrix products, chebyshev_fit(): jnp.einsum('cg,bgx->bcx', fitter, values.reshape(number, G, G * G), preci...  13.2 us
    all_to_all x1, starting transfers between devices, body(): lax.all_to_all(requests, 'dev', split_axis=0, concat_axis=0, tiled=True)  12 us
    all_to_all x1, starting transfers between devices, sum_at_owner(): tiles = lax.all_to_all(split_up(shard, dim, length), axis, 0, 0, tiled=True)  9.62 us
  transfers between devices with their start and end apart: 4, of which 2 were waited for; matrix products, arithmetic and copies ran while one was open for 34% of the time, Pallas kernels for 0%

commit v1 on v0

v1 whole, which is shorter than its diff:
```python
import numpy as np
import jax
import jax.numpy as jnp
from jax import lax
from jax.experimental import pallas as pl
from jax.experimental.pallas import tpu as pltpu
from jax.sharding import PartitionSpec as P

G = 32
KEEP = 16
S = 16
F32 = jnp.float32
BF16 = jnp.bfloat16
HIGHEST = lax.Precision.HIGHEST
VMEM_LIMIT = 56 * 2**20


def tables():
    orders = np.arange(KEEP, dtype=np.float64)
    points = np.arange(G, dtype=np.float64) + 0.5
    cosines = np.cos(np.pi * orders[:, None] * points[None, :] / G)
    weights = np.where(orders == 0, 1.0, 2.0) / G
    return cosines, weights[:, None] * cosines


COSINES, FITTER = tables()


def halves(a):
    hi = a.astype(BF16)
    return hi, (a - hi.astype(F32)).astype(BF16)


def halves_np(a):
    a = a.astype(np.float32)
    hi = a.astype(jnp.bfloat16)
    return hi, (a - hi.astype(np.float32)).astype(jnp.bfloat16)


def dot(a, b):
    return jnp.dot(a, b, preferred_element_type=F32)


def dot_exact(a, b):
    return jnp.dot(a, b, preferred_element_type=F32, precision=HIGHEST)


def iota(shape, dim):
    return lax.broadcasted_iota(jnp.int32, shape, dim)


def lane_sum(a):
    return jnp.sum(a, axis=1, keepdims=True)


def ask_kernel(tri_ref, pair_ref, slot_ref, modal_ref, single_ref, cos_ref, fit_ref, out_ref, meta_ref):
    modes = slot_ref.shape[1]
    tri = tri_ref[...]
    first, second, third = tri[:, 0:1], tri[:, 1:2], tri[:, 2:3]
    lower = jnp.concatenate([first, first, second], axis=0)
    upper = jnp.concatenate([second, third, third], axis=0)
    each = jnp.concatenate([first, second, third], axis=0)
    rows = lower.shape[0]
    lane = iota((rows, modes), 1)
    pair = pair_ref[...]
    high = (pair >> 8).astype(F32).astype(BF16)
    low = (pair & 255).astype(F32).astype(BF16)
    pick = (lane == lower).astype(F32).astype(BF16)
    at = lane == upper
    owner = lane_sum(jnp.where(at, dot(pick, high), 0.0))
    local = lane_sum(jnp.where(at, dot(pick, low), 0.0))
    slot = lane_sum(jnp.where(lane == each, slot_ref[...].astype(F32), 0.0))
    wide = iota((rows, 128), 1)
    wide_f = wide.astype(F32)
    hit = wide_f == owner
    hit_f = hit.astype(F32)
    hit_b = hit_f.astype(BF16)
    earlier = (iota((rows, rows), 1) < iota((rows, rows), 0)).astype(F32).astype(BF16)
    rank = lane_sum(jnp.where(hit, dot(earlier, hit_b), 0.0))
    ordered = lower < upper
    is_first = iota((rows, 1), 0) < rows // 3
    turned = jnp.where(is_first, ordered.astype(F32), 1.0 - ordered.astype(F32))
    said = jnp.where(wide_f == rank, local, 0.0) + jnp.where(wide_f == rank + 16.0, turned, 0.0)
    asked = lax.dot_general(hit_b, said.astype(BF16), (((0,), (0,)), ((), ())), preferred_element_type=F32)
    square = modal_ref[...] * modal_ref[...]
    mine = dot_exact(square, cos_ref[...]) + dot_exact(single_ref[...], fit_ref[...])
    four = mine.shape
    mine = jnp.sum(jnp.where((iota(four, 1) >> 5) == iota(four, 0), mine, 0.0), axis=0, keepdims=True)
    peers = out_ref.shape[0]
    out_ref[:, 0, :] = jnp.broadcast_to(mine, (peers, 128))
    out_ref[:, 1, :] = asked[:peers]
    meta_ref[...] = jnp.where(wide == 0, owner * 24.0 + rank, jnp.where(wide == 1, slot, 0.0))


def table_kernel(pair_ref, hi_ref, lo_ref, modal_ref, cosine_ref, table_ref, integral_ref):
    a_hi, a_lo = halves(pair_ref[...])
    k_hi, k_lo = hi_ref[...], lo_ref[...]
    terms = dot(a_hi, k_hi) + dot(a_hi, k_lo) + dot(a_lo, k_hi)
    square = (256, 256)
    i, j = iota(square, 0), iota(square, 1)
    turn = (((i & 15) == (j >> 4)) & ((i >> 4) == (j & 15))).astype(F32).astype(BF16)
    t_hi, t_lo = halves(terms)
    table_ref[:, :256] = terms
    table_ref[:, 256:] = dot(t_hi, turn) + dot(t_lo, turn)
    modal = modal_ref[...]
    own = modal.shape[0]
    row = iota((own * G, G * S), 0)
    lane = iota((own * G, G * S), 1)
    spread = jnp.zeros((own * G, G * S), F32)
    for m in range(own):
        spread = jnp.where((row >> 5) == m, modal[m : m + 1, :], spread)
    spread = jnp.where((lane >> 4) == (row & 31), spread, 0.0)
    k, n = iota((G * S, 256), 0), iota((G * S, 256), 1)
    left = dot_exact(spread, ((k & 15) == (n >> 4)).astype(F32))
    right = dot_exact(spread, ((k & 15) == (n & 15)).astype(F32))
    integral_ref[...] = dot_exact(cosine_ref[...], left * right)


def answer_kernel(came_ref, table_ref, out_ref):
    asked = came_ref[:, 1, :].astype(BF16)
    rows = out_ref.shape[0]
    peers = asked.shape[0]
    at = iota((rows, 1), 0).astype(F32)
    peer = jnp.floor((at + 0.5) * (1.0 / 24.0))
    rest = at - 24.0 * peer
    late = rest >= 12.0
    rank = rest - jnp.where(late, 12.0, 0.0)
    pick = (iota((rows, peers), 1).astype(F32) == peer).astype(F32).astype(BF16)
    wide = iota((rows, 128), 1).astype(F32)
    seen = dot(pick, asked)
    local = lane_sum(jnp.where(wide == rank, seen, 0.0))
    turned = lane_sum(jnp.where(wide == rank + 16.0, seen, 0.0))
    pick = (iota((rows, 256), 1).astype(F32) == local).astype(F32).astype(BF16)
    hi, lo = halves(table_ref[...])
    both = dot(pick, hi) + dot(pick, lo)
    terms = jnp.where(turned > 0.5, both[:, 256:], both[:, :256])
    out_ref[...] = jnp.where(late, terms[:, 128:], terms[:, :128])


def fit_kernel(fit_ref, front_ref, back_ref, hi_ref, lo_ref, out_ref):
    step = pl.program_id(0)
    number = front_ref.shape[0]
    cells = G * G
    per = front_ref.shape[1] // cells
    parts = []
    for j in range(per):
        parts.append(front_ref[:, j * cells : (j + 1) * cells])
    for j in range(per):
        parts.append(back_ref[:, (per - 1 - j) * cells : (per - j) * cells])
    stacked = jnp.concatenate(parts, axis=0)
    two = dot(stacked, hi_ref[...]) + dot(stacked, lo_ref[...])
    evens, odds = [], []
    for j in range(per):
        a = two[j * number : (j + 1) * number]
        b = two[(per + j) * number : (per + j + 1) * number]
        evens.append(a + b)
        odds.append(a - b)

    def add(fresh):
        for c in range(KEEP):
            chosen = odds if c % 2 else evens
            total = chosen[0] * fit_ref[c, step * per]
            for j in range(1, per):
                total = total + chosen[j] * fit_ref[c, step * per + j]
            where = slice(c * 256, (c + 1) * 256)
            if fresh:
                out_ref[:, where] = total
            else:
                out_ref[:, where] += total

    @pl.when(step == 0)
    def _():
        add(True)

    @pl.when(step > 0)
    def _():
        add(False)


def field_kernel(fit_ref, came_ref, ground_ref, meta_ref, coef_ref, energy_ref, part_ref):
    number = fit_ref.shape[0]
    rows = meta_ref.shape[0]
    peers = ground_ref.shape[0]
    place = meta_ref[:, 0:1]
    slot = meta_ref[:, 1:2]
    home = jnp.floor((slot + 0.5) * 0.25)
    sub = slot - 4.0 * home
    lane = iota((rows, 128), 1)
    pick = (iota((rows, peers), 1).astype(F32) == home).astype(F32)
    known = dot_exact(pick, ground_ref[:, 0, :])
    known = jnp.where((lane >> 5).astype(F32) == sub, known, 0.0)
    known = known + pltpu.roll(known, 64, 1)
    known = known + pltpu.roll(known, 32, 1)
    one, two, three = (known[p * number : (p + 1) * number] for p in range(3))
    hi, lo = halves(came_ref[...])
    slots = came_ref.shape[0]
    where = iota((rows, slots), 1).astype(F32)
    got = []
    for h in range(2):
        choose = (where == place + 12.0 * h).astype(F32).astype(BF16)
        got.append(dot(choose, hi) + dot(choose, lo))
    lane = iota((number, 128), 1)
    k, n = iota((128, 256), 0), iota((128, 256), 1)
    two_wide = dot_exact(two, (k == (n >> 4)).astype(F32))
    two_single = dot_exact(two, ((k == (n >> 4) + 16) & ((n & 15) == 0)).astype(F32))
    three_low = jnp.where((lane & 31) < 16, three, 0.0)
    three_wide = three_low + pltpu.roll(three_low, 16, 1)
    start = lane < 16
    first_pair = [g[:number] for g in got]
    first_pair[0] = first_pair[0] + jnp.where(start, pltpu.roll(one, 112, 1), 0.0)
    second_pair = [g[number : 2 * number] for g in got]
    third_pair = [g[2 * number :] for g in got]
    third_pair[0] = third_pair[0] + jnp.where(start, pltpu.roll(three, 112, 1), 0.0)
    third_pair = [t + two_single[:, h * 128 : (h + 1) * 128] for h, t in enumerate(third_pair)]
    twos = [two_wide[:, :128], two_wide[:, 128:]]
    both = [w * three_wide for w in twos]
    spaced = (lane & 15) == 0
    field_first = jnp.zeros((number, 128), F32)
    lead = [jnp.zeros((number, 128), F32), jnp.zeros((number, 128), F32)]
    for c in range(KEEP):
        at_c = one[:, c : c + 1]
        along = jnp.zeros((number, 128), F32)
        for h in range(2):
            cols = slice(c * 256 + h * 128, c * 256 + (h + 1) * 128)
            moved = pltpu.roll(first_pair[h], 128 - c, 1) if c else first_pair[h]
            value = fit_ref[:, cols] - jnp.where(spaced, moved, 0.0)
            if h == 0:
                shift = (c % 8) * 16
                moved = second_pair[c // 8]
                moved = pltpu.roll(moved, 128 - shift, 1) if shift else moved
                value = value - jnp.where(start, moved, 0.0)
            if c == 0:
                value = value - third_pair[h]
            coef_ref[:, cols] = value.astype(BF16)
            along = along + value * both[h]
            lead[h] = lead[h] + at_c * value
        field_first = field_first + jnp.where(lane == c, lane_sum(along), 0.0)
    field_second = jnp.zeros((number, 128), F32)
    field_third = jnp.zeros((number, 128), F32)
    k, n = iota((128, 128), 0), iota((128, 128), 1)
    for h in range(2):
        to_second = ((k >> 4) + 8 * h == n).astype(F32)
        to_third = ((k & 15) == n).astype(F32)
        field_second = field_second + dot_exact(lead[h] * three_wide, to_second)
        field_third = field_third + dot_exact(lead[h] * twos[h], to_third)
    ones = jnp.full((8, 128), 1.0, F32)
    energy = lax.dot_general(
        ones, field_first * one, (((1,), (1,)), ((), ())), preferred_element_type=F32, precision=HIGHEST
    )
    energy_ref[...] = energy[0:1]
    fields = jnp.concatenate([field_first, field_second, field_third], axis=0)
    fields = fields + pltpu.roll(fields, 16, 1)
    fields = fields + pltpu.roll(fields, 32, 1)
    fields = jnp.where((iota((rows, 128), 1) >> 4).astype(F32) == sub, fields, 0.0)
    part = lax.dot_general(
        pick, fields, (((0,), (0,)), ((), ())), preferred_element_type=F32, precision=HIGHEST
    )
    for g in range(part_ref.shape[0]):
        part_ref[g] = part


def integral_kernel(parts_ref, integral_ref, out_ref):
    total = jnp.sum(parts_ref[...], axis=0, keepdims=True)
    shape = (out_ref.shape[0], 128)
    total = jnp.where((iota(shape, 1) >> 4) == iota(shape, 0), total, 0.0)
    out_ref[...] = dot_exact(total, integral_ref[...])


def call(kernel, outs, *args, name, smem=(), flops=0):
    vm = pl.BlockSpec(memory_space=pltpu.VMEM)
    moved = sum(int(np.prod(a.shape)) * a.dtype.itemsize for a in args) + sum(
        int(np.prod(o.shape)) * o.dtype.itemsize for o in outs
    )
    return pl.pallas_call(
        kernel,
        out_shape=outs,
        in_specs=[vm] * len(args),
        out_specs=[vm] * len(outs),
        compiler_params=pltpu.CompilerParams(vmem_limit_bytes=VMEM_LIMIT),
        cost_estimate=pl.CostEstimate(flops=flops, bytes_accessed=moved, transcendentals=0),
        name=name,
    )(*args)


def shaped(shape, dtype=F32):
    return jax.ShapeDtypeStruct(shape, dtype)


def body(energies, triples, pair_surfaces, pair_slot, single_surfaces, modals, mode_slot):
    devices = lax.axis_size("dev")
    groups = lax.axis_size("grp")
    number = triples.shape[0]
    own = modals.shape[0]
    capacity = 3 * number // devices
    cos_wide = np.zeros((G * S, 128), np.float32)
    fit_wide = np.zeros((G, 128), np.float32)
    cos_block = np.zeros((128, own * G), np.float32)
    for m in range(own):
        cos_wide[::S, m * 32 : m * 32 + KEEP] = COSINES.T
        fit_wide[:, m * 32 + KEEP : m * 32 + 2 * KEEP] = FITTER.T
        cos_block[m * KEEP : (m + 1) * KEEP, m * G : (m + 1) * G] = COSINES
    kron = np.einsum("dh,el->hlde", FITTER, FITTER).reshape(G * G, KEEP * KEEP)
    hi, lo = (jnp.asarray(x) for x in halves_np(kron))
    send, meta = call(
        ask_kernel,
        [shaped((devices, 2, 128)), shaped((3 * number, 128))],
        triples,
        pair_slot,
        mode_slot.reshape(1, -1),
        modals,
        single_surfaces,
        jnp.asarray(cos_wide),
        jnp.asarray(fit_wide),
        name="ask",
    )
    came = lax.all_to_all(send, "dev", 0, 0, tiled=True)
    table, integral = call(
        table_kernel,
        [shaped((pair_surfaces.shape[0], 512)), shaped((128, S * S))],
        pair_surfaces,
        hi,
        lo,
        modals,
        jnp.asarray(cos_block),
        name="table",
        flops=10**9,
    )
    (answer,) = call(
        answer_kernel, [shaped((devices * 2 * capacity, 128))], came, table, name="answer"
    )
    terms = lax.all_to_all(
        answer.reshape(devices, 2 * capacity, 128), "dev", 0, 0, tiled=True
    ).reshape(devices * 2 * capacity, 128)
    per = 2
    steps = G // (2 * per)
    block = per * G * G
    fitted = pl.pallas_call(
        fit_kernel,
        grid=(steps,),
        out_shape=shaped((number, KEEP**3)),
        in_specs=[
            pl.BlockSpec(memory_space=pltpu.SMEM),
            pl.BlockSpec((number, block), lambda i: (0, i)),
            pl.BlockSpec((number, block), lambda i: (0, 2 * steps - 1 - i)),
            pl.BlockSpec((G * G, 256), lambda i: (0, 0)),
            pl.BlockSpec((G * G, 256), lambda i: (0, 0)),
        ],
        out_specs=pl.BlockSpec((number, KEEP**3), lambda i: (0, 0)),
        compiler_params=pltpu.CompilerParams(vmem_limit_bytes=VMEM_LIMIT),
        cost_estimate=pl.CostEstimate(flops=5 * 10**9, bytes_accessed=11 * 2**20, transcendentals=0),
        name="fit",
    )(jnp.asarray(FITTER.astype(np.float32)), energies, energies, hi, lo)
    coefficients, energy, part = call(
        field_kernel,
        [shaped((number, KEEP**3), BF16), shaped((1, number)), shaped((groups, devices, 128))],
        fitted,
        terms,
        came,
        meta,
        name="fields",
        flops=10**9,
    )
    parts = lax.all_to_all(
        part.reshape(groups * devices, 1, 128), ("grp", "dev"), 0, 0, tiled=True
    )
    (mean_field,) = call(
        integral_kernel,
        [shaped((own, S * S))],
        parts.reshape(groups * devices, 128),
        integral,
        name="integrals",
    )
    return coefficients, energy.reshape(number), mean_field


def solution(mesh):
    in_specs = (
        P(("grp", "dev"), None),
        P(("grp", "dev"), None),
        P("dev", None),
        P(),
        P("dev", None),
        P("dev", None),
        P(),
    )
    out_specs = (P(("grp", "dev"), None), P(("grp", "dev")), P("dev", None))
    return jax.shard_map(body, mesh=mesh, in_specs=in_specs, out_specs=out_specs, check_vma=False)
```

time: 225 us -> 81.8 us (0.36); the launches traced: 221 us -> 81.3 us
  local copies, waits for them, and re-layouts: 58.1 us -> 2.77 us
  matrix products: 52.7 us -> 0 us
  starting transfers between devices: 46.8 us -> 17 us
  Pallas kernels: 0 us -> 29 us
  other arithmetic: 13.2 us -> 0 us
  blocking collectives: 37.1 us -> 27.6 us
  waiting for transfers between devices: 11.7 us -> 4.26 us
    dot_general x9 -> x0, matrix products: 52.7 us -> none  [the longest x2 18.5 us: body(): jnp.einsum('cg,dh,xygh->xycd', fitter, fitter, picked, precision=highest)]
    all_gather x1 -> x0, blocking collectives: 37.1 us -> none  [in_one_piece(): lax.all_gather(both, axis, axis=dim, tiled=True)]
    all_to_all x4 -> x2, starting transfers between devices: 46.8 us -> 17 us  [the longest x1 12 us: body(): came = lax.all_to_all(send, 'dev', 0, 0, tiled=True)]
    pallas_call x0 -> x6, Pallas kernels: none -> 29 us  [the longest x5 17.2 us: call(): pl.pallas_call(kernel, out_shape=outs, in_specs=[vm] * len(args), out_spe...]
    all_to_all x0 -> x1, blocking collectives: none -> 27.6 us  [body(): lax.all_to_all(part.reshape(groups * devices, 1, 128), ('grp', 'dev'), 0,...]
    unnamed x11 -> x5, local copies, waits for them, and re-layouts: 20.4 us -> 2.77 us
    gather x15 -> x0, local copies, waits for them, and re-layouts: 15.7 us -> none  [the longest x1 4.4 us: body(): pair_ids = pair_slot[lower_ends, upper_ends]]
    transpose x1 -> x0, local copies, waits for them, and re-layouts: 8.74 us -> none  [chebyshev_fit(): jnp.einsum('cg,bgx->bcx', fitter, values.reshape(number, G, G * G), preci...]
  transfers between devices with their start and end apart: 4 -> 2, of which waited for: 2 -> 1; matrix products, arithmetic and copies ran while one was open for 34% -> 0% of each run, Pallas kernels for 0% -> 20%
where the time goes in v1:
time: 81.8 us; the launch traced here: 81.3 us
  Pallas kernels  29 us (35%)
  blocking collectives  27.6 us (34%)
  starting transfers between devices  17 us (21%)
  waiting for transfers between devices  4.26 us (5%)
  local copies, waits for them, and re-layouts  2.77 us (3%)
    all_to_all x1, blocking collectives, body(): lax.all_to_all(part.reshape(groups * devices, 1, 128), ('grp', 'dev'), 0,...  27.6 us
    pallas_call x5, Pallas kernels, call(): pl.pallas_call(kernel, out_shape=outs, in_specs=[vm] * len(args), out_spe...  17.2 us
    all_to_all x1, starting transfers between devices, body(): came = lax.all_to_all(send, 'dev', 0, 0, tiled=True)  12 us
    pallas_call x1, Pallas kernels, body(): pl.pallas_call(fit_kernel, grid=(steps,), out_shape=shaped((number, KEEP...  11.7 us
    all_to_all x1, starting transfers between devices, body(): lax.all_to_all(answer.reshape(devices, 2 * capacity, 128), 'dev', 0, 0, t...  4.96 us
    all_to_all x1, waiting for transfers between devices, body(): came = lax.all_to_all(send, 'dev', 0, 0, tiled=True)  4.26 us
    unnamed x5, local copies, waits for them, and re-layouts  2.77 us
  transfers between devices with their start and end apart: 2, of which 1 were waited for; matrix products, arithmetic and copies ran while one was open for 0% of the time, Pallas kernels for 20%

profile of v1, /device:TPU:1, one launch (start us, length us, event | category | flops | bytes accessed | tf_op | source)
XLA Modules:
  0.0 81.3 jit_solution(2029866796950465752)
XLA Ops:
  0.6 1.4 %copy.17.tri_ref = s32[128,3]{1,0:T(8,128)} copy(s32[128,3]{0,1:T(4,128)} %param.14) | data formatting | bytes 3072 | tf_op args[1]
  2.0 2.7 %ask.1 = (f32[32,2,128]{2,1,0:T(2,128)}, f32[384,128]{1,0:T(8,128)}) custom-call(s32[128,3]{1,0:T(8,128)} %copy.17.tri_ref, s32[114,114]{1,0:T(8,128)} %pair_ref.2, s32[1,114]{1,0:T(1,128)} %bitcast.12, f32[4,512]{1,0:T(4,128)} %modal_ref.3, f32[4,32]{1,0:T(4,128)} %single_ref.1, f32[512,128]{1,0:T(8,128)} %constant.14.clone.cos_ref, ...), custom_call_target="tpu_custom_call" | custom-call | bytes 570584 | tf_op jit(solution)/shard_map/ask/pallas_call | solution.py:274
  4.7 12.0 %all-to-all-start = ((f32[32,2,128]{2,1,0:T(2,128)}), f32[32,2,128]{2,1,0:T(2,128)S(1)}, u32[]{:S(2)}, u32[]{:S(2)}) async-start(f32[32,2,128]{2,1,0:T(2,128)} %get-tuple-element.10), calls=%async_computation | async-start | bytes 65536 | tf_op jit(solution)/shard_map/all_to_all | solution.py:316
  16.8 4.5 %table.1 = (f32[256,512]{1,0:T(8,128)}, f32[128,256]{1,0:T(8,128)}) custom-call(f32[256,1024]{1,0:T(8,128)} %pair_ref.3, bf16[1024,256]{1,0:T(8,128)(2,1)} %constant.12.clone.hi_ref, bf16[1024,256]{1,0:T(8,128)(2,1)} %constant.13.clone.lo_ref, f32[4,512]{1,0:T(4,128)} %modal_ref.3, f32[128,128]{1,0:T(8,128)} %constant.16.clone.cosine_ref), custom_call_target="tpu_custom_call" | custom-call | flops 1000000000 | bytes 2826240 | tf_op jit(solution)/shard_map/table/pallas_call | solution.py:274
  21.3 4.3 %all-to-all-done.came_ref.ground_ref = f32[32,2,128]{2,1,0:T(2,128)S(1)} async-done(((f32[32,2,128]{2,1,0:T(2,128)}), f32[32,2,128]{2,1,0:T(2,128)S(1)}, u32[]{:S(2)}, u32[]{:S(2)}) %all-to-all-start) | async-done | bytes 32800 | tf_op jit(solution)/shard_map/all_to_all | solution.py:316
  25.5 0.0 copy-start.1
  25.5 0.6 copy-done.1
  26.2 2.6 %answer.1 = f32[768,128]{1,0:T(8,128)} custom-call(f32[32,2,128]{2,1,0:T(2,128)} %copy-done.1, f32[256,512]{1,0:T(8,128)} %get-tuple-element.11.table_ref), custom_call_target="tpu_custom_call" | custom-call | bytes 950272 | tf_op jit(solution)/shard_map/answer/pallas_call | solution.py:274
  28.8 5.0 %all-to-all-start.1 = ((f32[32,24,128]{2,1,0:T(8,128)}), f32[32,24,128]{2,1,0:T(8,128)S(1)}, u32[]{:S(2)}, u32[]{:S(2)}) async-start(f32[32,24,128]{2,1,0:T(8,128)} %bitcast.8), calls=%async_computation.1 | async-start | bytes 786432 | tf_op jit(solution)/shard_map/all_to_all | solution.py:331
  33.7 11.7 %fit.1.fit_ref = f32[128,4096]{1,0:T(8,128)} custom-call(f32[16,32]{1,0:T(8,128)} %constant.17.clone.fit_ref, bf16[128,32768]{1,0:T(8,128)(2,1)} %back_ref.1, bf16[128,32768]{1,0:T(8,128)(2,1)} %back_ref.1, bf16[1024,256]{1,0:T(8,128)(2,1)} %constant.12.clone.hi_ref, bf16[1024,256]{1,0:T(8,128)(2,1)} %constant.13.clone.lo_ref), custom_call_target="tpu_custom_call" | custom-call | flops 5000000000 | bytes 11534336 | tf_op jit(solution)/shard_map/fit/pallas_call | solution.py:337
  45.5 0.0 all-to-all-done.1
  45.5 0.0 copy-start
  45.5 0.8 copy-done
  46.2 5.7 %fields.1 = (bf16[128,4096]{1,0:T(8,128)(2,1)}, f32[1,128]{1,0:T(1,128)}, f32[8,32,128]{2,1,0:T(8,128)}) custom-call(f32[128,4096]{1,0:T(8,128)} %fit.1.fit_ref, f32[768,128]{1,0:T(8,128)} %bitcast.10, f32[32,2,128]{2,1,0:T(2,128)} %copy-done.1, f32[384,128]{1,0:T(8,128)} %get-tuple-element.12.meta_ref), custom_call_target="tpu_custom_call" | custom-call | flops 1000000000 | bytes 3899904 | tf_op jit(solution)/shard_map/fields/pallas_call | solution.py:274
  51.9 27.6 %all_to_all.15 = f32[256,1,128]{2,1,0:T(1,128)} all-to-all(f32[256,1,128]{2,1,0:T(1,128)} %bitcast.11), channel_id=1, replica_groups=mesh['grp'=8,'dev'=32] {'grp','dev'}, dimensions={0} | all-to-all | bytes 262144 | tf_op jit(solution)/shard_map/all_to_all | solution.py:363
  79.5 1.8 %integrals.1 = f32[4,256]{1,0:T(4,128)} custom-call(f32[256,128]{1,0:T(8,128)} %bitcast.9, f32[128,256]{1,0:T(8,128)} %get-tuple-element.16.integral_ref), custom_call_target="tpu_custom_call" | custom-call | bytes 266240 | tf_op jit(solution)/shard_map/integrals/pallas_call | solution.py:274
Async XLA Ops:
  4.7 20.8 %all-to-all-start = ((f32[32,2,128]{2,1,0:T(2,128)}), f32[32,2,128]{2,1,0:T(2,128)S(1)}, u32[]{:S(2)}, u32[]{:S(2)}) async-start(f32[32,2,128]{2,1,0:T(2,128)} %get-tuple-element.10), calls=%async_computation | async-start | bytes 65536 | tf_op jit(solution)/shard_map/all_to_all | solution.py:316
  25.5 0.6 copy-start.1
  28.8 16.7 %all-to-all-start.1 = ((f32[32,24,128]{2,1,0:T(8,128)}), f32[32,24,128]{2,1,0:T(8,128)S(1)}, u32[]{:S(2)}, u32[]{:S(2)}) async-start(f32[32,24,128]{2,1,0:T(8,128)} %bitcast.8), calls=%async_computation.1 | async-start | bytes 786432 | tf_op jit(solution)/shard_map/all_to_all | solution.py:331
  45.5 0.8 copy-start

commit v2 on v1

v2 whole, which is shorter than its diff:
```python
import numpy as np
import jax
import jax.numpy as jnp
from jax import lax
from jax.experimental import pallas as pl
from jax.experimental.pallas import tpu as pltpu
from jax.sharding import PartitionSpec as P

G = 32
KEEP = 16
S = 16
F32 = jnp.float32
BF16 = jnp.bfloat16
HIGHEST = lax.Precision.HIGHEST
VMEM_LIMIT = 56 * 2**20


def tables():
    orders = np.arange(KEEP, dtype=np.float64)
    points = np.arange(G, dtype=np.float64) + 0.5
    cosines = np.cos(np.pi * orders[:, None] * points[None, :] / G)
    weights = np.where(orders == 0, 1.0, 2.0) / G
    return cosines, weights[:, None] * cosines


COSINES, FITTER = tables()


def halves(a):
    hi = a.astype(BF16)
    return hi, (a - hi.astype(F32)).astype(BF16)


def halves_np(a):
    a = a.astype(np.float32)
    hi = a.astype(jnp.bfloat16)
    return hi, (a - hi.astype(np.float32)).astype(jnp.bfloat16)


def dot(a, b):
    return jnp.dot(a, b, preferred_element_type=F32)


def dot_exact(a, b):
    return jnp.dot(a, b, preferred_element_type=F32, precision=HIGHEST)


def iota(shape, dim):
    return lax.broadcasted_iota(jnp.int32, shape, dim)


def lane_sum(a):
    return jnp.sum(a, axis=1, keepdims=True)


def column(row):
    n = row.shape[1]
    return lane_sum(jnp.where(iota((n, n), 0) == iota((n, n), 1), row, 0.0))


def one_hot(column_f, width):
    return (iota((column_f.shape[0], width), 1).astype(F32) == column_f).astype(F32).astype(BF16)


def dot_two(a, b):
    hi, lo = halves(a)
    return dot(hi, b) + dot(lo, b)


def pick_two(pick, hi, lo):
    return dot(pick, hi) + dot(pick, lo)


def place_of(slot):
    home = jnp.floor((slot + 0.5) * 0.25)
    return home, slot - 4.0 * home


def ask_kernel(tri_ref, pair_ref, slot_ref, modal_ref, single_ref, cos_ref, fit_ref, out_ref, meta_ref):
    modes = slot_ref.shape[1]
    tri = tri_ref[...].astype(F32)
    first, second, third = (column(tri[p : p + 1]) for p in range(3))
    lower = jnp.concatenate([first, first, second], axis=0)
    upper = jnp.concatenate([second, third, third], axis=0)
    each = jnp.concatenate([first, second, third], axis=0)
    rows = lower.shape[0]
    number = rows // 3
    lane = iota((rows, modes), 1).astype(F32)
    pair = pair_ref[...]
    high = (pair >> 8).astype(F32).astype(BF16)
    low = (pair & 255).astype(F32).astype(BF16)
    pick = (lane == lower).astype(F32).astype(BF16)
    at = lane == upper
    owner = lane_sum(jnp.where(at, dot(pick, high), 0.0))
    local = lane_sum(jnp.where(at, dot(pick, low), 0.0))
    slot = lane_sum(jnp.where(lane == each, slot_ref[...].astype(F32), 0.0))
    wide = iota((rows, 128), 1)
    wide_f = wide.astype(F32)
    hit = wide_f == owner
    hit_b = hit.astype(F32).astype(BF16)
    earlier = (iota((rows, rows), 1) < iota((rows, rows), 0)).astype(F32).astype(BF16)
    rank = lane_sum(jnp.where(hit, dot(earlier, hit_b), 0.0))
    ordered = lower < upper
    is_first = iota((rows, 1), 0) < number
    turned = jnp.where(is_first, ordered.astype(F32), 1.0 - ordered.astype(F32))
    s1, s2, s3 = (slot[p * number : (p + 1) * number] for p in range(3))
    left = jnp.concatenate([s1, s1, s2], axis=0)
    right = jnp.concatenate([s2, s3, s3], axis=0)
    other = jnp.concatenate([s3, s2, s1], axis=0)
    small = jnp.where(ordered, left, right)
    large = jnp.where(ordered, right, left)
    off = wide_f - rank
    said = jnp.where(off == 0.0, local, 0.0)
    for k, value in enumerate((turned, small, large, other)):
        said = said + jnp.where(off == 16.0 * (k + 1), value, 0.0)
    asked = lax.dot_general(hit_b, said.astype(BF16), (((0,), (0,)), ((), ())), preferred_element_type=F32)
    square = modal_ref[...] * modal_ref[...]
    mine = dot_exact(square, cos_ref[...]) + dot_exact(single_ref[...], fit_ref[...])
    four = mine.shape
    mine = jnp.sum(jnp.where((iota(four, 1) >> 5) == iota(four, 0), mine, 0.0), axis=0, keepdims=True)
    peers = out_ref.shape[0]
    out_ref[:, 0, :] = jnp.broadcast_to(mine, (peers, 128))
    out_ref[:, 1, :] = asked[:peers]
    meta_ref[...] = jnp.where(wide == 0, owner * 25.0 + rank, jnp.where(wide == 1, slot, 0.0))


def table_kernel(pair_ref, hi_ref, lo_ref, table_hi_ref, table_lo_ref):
    a_hi, a_lo = halves(pair_ref[...])
    k_hi, k_lo = hi_ref[...], lo_ref[...]
    terms = dot(a_hi, k_hi) + dot(a_hi, k_lo) + dot(a_lo, k_hi)
    square = (256, 256)
    i, j = iota(square, 0), iota(square, 1)
    turn = (((i & 15) == (j >> 4)) & ((i >> 4) == (j & 15))).astype(F32).astype(BF16)
    t_hi, t_lo = halves(terms)
    table_hi_ref[:, :256] = t_hi
    table_lo_ref[:, :256] = t_lo
    table_hi_ref[:, 256:] = dot(t_hi, turn).astype(BF16)
    table_lo_ref[:, 256:] = dot(t_lo, turn).astype(BF16)


def unit_kernel(modal_ref, cosine_ref, integral_ref):
    modal = modal_ref[...]
    own = modal.shape[0]
    row = iota((own * G, G * S), 0)
    lane = iota((own * G, G * S), 1)
    spread = jnp.zeros((own * G, G * S), F32)
    for m in range(own):
        spread = jnp.where((row >> 5) == m, modal[m : m + 1, :], spread)
    spread = jnp.where((lane >> 4) == (row & 31), spread, 0.0)
    k, n = iota((G * S, 256), 0), iota((G * S, 256), 1)
    hi, lo = halves(spread)
    to_left = ((k & 15) == (n >> 4)).astype(F32).astype(BF16)
    to_right = ((k & 15) == (n & 15)).astype(F32).astype(BF16)
    left = dot(hi, to_left) + dot(lo, to_left)
    right = dot(hi, to_right) + dot(lo, to_right)
    integral_ref[...] = dot_exact(cosine_ref[...], left * right)


def fit_kernel(fit_ref, front_ref, back_ref, hi_ref, lo_ref, out_ref, two_ref):
    step = pl.program_id(0)
    number = front_ref.shape[0]
    cells = G * G
    per = front_ref.shape[1] // cells
    parts = [front_ref[:, j * cells : (j + 1) * cells] for j in range(per)]
    parts += [back_ref[:, (per - 1 - j) * cells : (per - j) * cells] for j in range(per)]
    stacked = jnp.concatenate(parts, axis=0)
    two = dot(stacked, hi_ref[...]) + dot(stacked, lo_ref[...])
    for j in range(per):
        a = two[j * number : (j + 1) * number]
        b = two[(per + j) * number : (per + j + 1) * number]
        two_ref[0, j] = a + b
        two_ref[1, j] = a - b

    @pl.when(step == 0)
    def _():
        out_ref[...] = jnp.zeros_like(out_ref)

    def add(q, carry):
        for parity in range(2):
            c = 2 * q + parity
            total = two_ref[parity, 0] * fit_ref[c, step * per]
            for j in range(1, per):
                total = total + two_ref[parity, j] * fit_ref[c, step * per + j]
            out_ref[c] += total
        return carry

    lax.fori_loop(0, KEEP // 2, add, 0)


def share_kernel(came_ref, hi_ref, lo_ref, fit_ref, meta_ref, out_ref, known_ref):
    peers = came_ref.shape[0]
    number = fit_ref.shape[1]
    rows = 3 * number
    asked = came_ref[:, 1, :].astype(BF16)
    per = float(rows // peers)
    at = iota((rows, 1), 0).astype(F32)
    peer = jnp.floor((at + 0.5) * (1.0 / per))
    rank = at - per * peer
    seen = dot(one_hot(peer, peers), asked)
    off = iota((rows, 128), 1).astype(F32) - rank
    local, small, large, other = (
        lane_sum(jnp.where(off == 16.0 * k, seen, 0.0)) for k in (0, 2, 3, 4)
    )
    slot = jnp.concatenate([meta_ref[:, 1:2], small, large, other], axis=0)
    home, sub = place_of(slot)
    pick = one_hot(home, peers)
    g_hi, g_lo = halves(came_ref[:, 0, :])
    lane = iota((4 * rows, 128), 1)
    known = pick_two(pick, g_hi, g_lo)
    known = jnp.where((lane >> 5).astype(F32) == sub, known, 0.0)
    known = known + pltpu.roll(known, 64, 1)
    known = known + pltpu.roll(known, 32, 1)
    known_ref[...] = known[:rows]
    k, n = iota((128, 256), 0), iota((128, 256), 1)
    widen = (k == (n >> 4)).astype(F32).astype(BF16)
    widen_single = ((k == (n >> 4) + 16) & ((n & 15) == 0)).astype(F32).astype(BF16)
    k, n = iota((256, 128), 0), iota((256, 128), 1)
    to_high = ((k >> 4) == n).astype(F32).astype(BF16)
    to_low = ((k & 15) == n).astype(F32).astype(BF16)

    def repeated(a):
        part = jnp.where((iota(a.shape, 1) & 31) < 16, a, 0.0)
        return part + pltpu.roll(part, 16, 1)

    def twice(a):
        return jnp.concatenate([a, a], axis=1)

    terms = pick_two(one_hot(local, 256), hi_ref[:, :256], lo_ref[:, :256])
    g_small, g_large, g_other = (known[p * rows : (p + 1) * rows] for p in (1, 2, 3))
    of_small = dot_two(terms * twice(repeated(g_large)), to_high)
    of_large = dot_two(terms * dot_two(g_small, widen), to_low)
    norm = g_other[:, 0:1]
    of_other = lane_sum(of_small * g_small)
    lane = iota((rows, 128), 1)
    shares = [-norm * of_small, -norm * of_large, jnp.where(lane == 0, -of_other, 0.0)]
    one, two, three = (known[p * number : (p + 1) * number] for p in range(3))
    two_wide = dot_two(two, widen)
    three_wide = twice(repeated(three))
    both = two_wide * three_wide
    lane = iota((number, 256), 1)
    single = dot_two(two, widen_single) + jnp.where(
        lane < 16, twice(pltpu.roll(three, 112, 1)), 0.0
    )
    thin = iota((number, 128), 1)
    field_first = jnp.zeros((number, 128), F32)
    lead = jnp.zeros((number, 256), F32)
    for c in range(KEEP):
        value = fit_ref[c] - jnp.where(lane == 0, one[:, 16 + c : 17 + c], 0.0)
        if c == 0:
            value = value - single
        along = value * both
        field_first = field_first + jnp.where(thin == c, lane_sum(along[:, :128] + along[:, 128:]), 0.0)
        lead = lead + one[:, c : c + 1] * value
    field_second = dot_two(lead * three_wide, to_high)
    field_third = dot_two(lead * two_wide, to_low)
    fields = jnp.concatenate([field_first, field_second, field_third] + shares, axis=0)
    fields = fields + pltpu.roll(fields, 16, 1)
    fields = fields + pltpu.roll(fields, 32, 1)
    fields = jnp.where((iota(fields.shape, 1) >> 4).astype(F32) == sub, fields, 0.0)
    f_hi, f_lo = halves(fields)
    dims = (((0,), (0,)), ((), ()))
    part = lax.dot_general(pick, f_hi, dims, preferred_element_type=F32) + lax.dot_general(
        pick, f_lo, dims, preferred_element_type=F32
    )
    slots = out_ref.shape[0]
    each = float(slots // peers)
    at = iota((slots, 1), 0).astype(F32)
    peer = jnp.floor((at + 0.5) * (1.0 / each))
    rest = at - each * peer
    late = rest >= per
    rank = rest - jnp.where(late, per, 0.0)
    from_peer = one_hot(peer, peers)
    seen = dot(from_peer, asked)
    off = iota((slots, 128), 1).astype(F32) - rank
    local = lane_sum(jnp.where(off == 0.0, seen, 0.0))
    turned = lane_sum(jnp.where(off == 16.0, seen, 0.0))
    terms = pick_two(one_hot(local, 256), hi_ref[...], lo_ref[...])
    terms = jnp.where(turned > 0.5, terms[:, 256:], terms[:, :256])
    terms = jnp.where(late, terms[:, 128:], terms[:, :128])
    p_hi, p_lo = halves(part)
    out_ref[...] = jnp.where(rest == 2.0 * per, pick_two(from_peer, p_hi, p_lo), terms)


def own_kernel(came_ref, out_ref):
    peers = came_ref.shape[0] // 25
    each = 25
    rows = came_ref[pl.ds(each - 1, peers, stride=each), :]
    total = jnp.sum(rows, axis=0, keepdims=True)
    out_ref[...] = jnp.broadcast_to(total, out_ref.shape)


def face_kernel(fit_ref, came_ref, known_ref, meta_ref, coef_ref, energy_ref):
    number = fit_ref.shape[1]
    place = meta_ref[:, 0:1]
    known = known_ref[...]
    one, two, three = (known[p * number : (p + 1) * number] for p in range(3))
    hi, lo = halves(came_ref[...])
    slots = came_ref.shape[0]
    got = [pick_two(one_hot(place + 12.0 * h, slots), hi, lo) for h in range(2)]
    lane = iota((number, 128), 1)
    k, n = iota((128, 256), 0), iota((128, 256), 1)
    two_wide = dot_two(two, (k == (n >> 4)).astype(F32).astype(BF16))
    two_single = dot_two(two, ((k == (n >> 4) + 16) & ((n & 15) == 0)).astype(F32).astype(BF16))
    three_low = jnp.where((lane & 31) < 16, three, 0.0)
    three_wide = three_low + pltpu.roll(three_low, 16, 1)
    start = lane < 16
    first_pair = [g[:number] for g in got]
    first_pair[0] = first_pair[0] + jnp.where(start, pltpu.roll(one, 112, 1), 0.0)
    second_pair = [g[number : 2 * number] for g in got]
    third_pair = [g[2 * number :] for g in got]
    third_pair[0] = third_pair[0] + jnp.where(start, pltpu.roll(three, 112, 1), 0.0)
    third_pair = [t + two_single[:, h * 128 : (h + 1) * 128] for h, t in enumerate(third_pair)]
    both = [two_wide[:, h * 128 : (h + 1) * 128] * three_wide for h in range(2)]
    spaced = (lane & 15) == 0
    energy = jnp.zeros((number, 128), F32)
    for c in range(KEEP):
        along = jnp.zeros((number, 128), F32)
        for h in range(2):
            moved = pltpu.roll(first_pair[h], 128 - c, 1) if c else first_pair[h]
            value = fit_ref[c, :, h * 128 : (h + 1) * 128] - jnp.where(spaced, moved, 0.0)
            if h == 0:
                shift = (c % 8) * 16
                moved = second_pair[c // 8]
                moved = pltpu.roll(moved, 128 - shift, 1) if shift else moved
                value = value - jnp.where(start, moved, 0.0)
            if c == 0:
                value = value - third_pair[h]
            coef_ref[:, c * 256 + h * 128 : c * 256 + (h + 1) * 128] = value.astype(BF16)
            along = along + value * both[h]
        energy = energy + one[:, c : c + 1] * along
    energy_ref[...] = lax.dot_general(
        jnp.full((8, 128), 1.0, F32), energy, (((1,), (1,)), ((), ())), preferred_element_type=F32, precision=HIGHEST
    )[0:1]


def integral_kernel(parts_ref, integral_ref, out_ref):
    total = jnp.sum(parts_ref[...], axis=0, keepdims=True)
    shape = (out_ref.shape[0], 128)
    total = jnp.where((iota(shape, 1) >> 4) == iota(shape, 0), total, 0.0)
    out_ref[...] = dot_exact(total, integral_ref[...])


def call(kernel, outs, *args, name, smem=(), flops=0):
    vm = pl.BlockSpec(memory_space=pltpu.VMEM)
    moved = sum(int(np.prod(a.shape)) * a.dtype.itemsize for a in args) + sum(
        int(np.prod(o.shape)) * o.dtype.itemsize for o in outs
    )
    return pl.pallas_call(
        kernel,
        out_shape=outs,
        in_specs=[vm] * len(args),
        out_specs=[vm] * len(outs),
        compiler_params=pltpu.CompilerParams(vmem_limit_bytes=VMEM_LIMIT),
        cost_estimate=pl.CostEstimate(flops=flops, bytes_accessed=moved, transcendentals=0),
        name=name,
    )(*args)


def shaped(shape, dtype=F32):
    return jax.ShapeDtypeStruct(shape, dtype)


def body(energies, triples, pair_surfaces, pair_slot, single_surfaces, modals, mode_slot):
    devices = lax.axis_size("dev")
    groups = lax.axis_size("grp")
    number = triples.shape[0]
    own = modals.shape[0]
    capacity = 3 * number // devices
    cos_wide = np.zeros((G * S, 128), np.float32)
    fit_wide = np.zeros((G, 128), np.float32)
    cos_block = np.zeros((128, own * G), np.float32)
    for m in range(own):
        cos_wide[::S, m * 32 : m * 32 + KEEP] = COSINES.T
        fit_wide[:, m * 32 + KEEP : m * 32 + 2 * KEEP] = FITTER.T
        cos_block[m * KEEP : (m + 1) * KEEP, m * G : (m + 1) * G] = COSINES
    kron = np.einsum("dh,el->hlde", FITTER, FITTER).reshape(G * G, KEEP * KEEP)
    hi, lo = (jnp.asarray(x) for x in halves_np(kron))
    send, meta = call(
        ask_kernel,
        [shaped((devices, 2, 128)), shaped((3 * number, 128))],
        triples.T,
        pair_slot,
        mode_slot.reshape(1, -1),
        modals,
        single_surfaces,
        jnp.asarray(cos_wide),
        jnp.asarray(fit_wide),
        name="ask",
    )
    came = lax.all_to_all(send, "dev", 0, 0, tiled=True)
    table = shaped((pair_surfaces.shape[0], 512), BF16)
    table_hi, table_lo = call(
        table_kernel, [table, table], pair_surfaces, hi, lo, name="table", flops=5 * 10**8
    )
    per = 4
    steps = G // (2 * per)
    block = per * G * G
    fitted = pl.pallas_call(
        fit_kernel,
        grid=(steps,),
        out_shape=shaped((KEEP, number, KEEP**2)),
        in_specs=[
            pl.BlockSpec(memory_space=pltpu.SMEM),
            pl.BlockSpec((number, block), lambda i: (0, i)),
            pl.BlockSpec((number, block), lambda i: (0, 2 * steps - 1 - i)),
            pl.BlockSpec((G * G, 256), lambda i: (0, 0)),
            pl.BlockSpec((G * G, 256), lambda i: (0, 0)),
        ],
        out_specs=pl.BlockSpec((KEEP, number, KEEP**2), lambda i: (0, 0, 0)),
        scratch_shapes=[pltpu.VMEM((2, per, number, 256), F32)],
        compiler_params=pltpu.CompilerParams(vmem_limit_bytes=VMEM_LIMIT),
        cost_estimate=pl.CostEstimate(flops=5 * 10**9, bytes_accessed=11 * 2**20, transcendentals=0),
        name="fit",
    )(jnp.asarray(FITTER.astype(np.float32)), energies, energies, hi, lo)
    each = 2 * capacity + 1
    answer, known = call(
        share_kernel,
        [shaped((devices * each, 128)), shaped((3 * number, 128))],
        came,
        table_hi,
        table_lo,
        fitted,
        meta,
        name="share",
        flops=10**9,
    )
    terms = lax.all_to_all(
        answer.reshape(devices, each, 1, 128), "dev", 0, 0, tiled=True
    ).reshape(devices * each, 128)
    (integral,) = call(
        unit_kernel, [shaped((128, S * S))], modals, jnp.asarray(cos_block), name="unit", flops=10**9
    )
    (mine,) = call(own_kernel, [shaped((groups, 128))], terms, name="own")
    parts = lax.all_to_all(mine.reshape(groups, 1, 128), "grp", 0, 0, tiled=True)
    coefficients, energy = call(
        face_kernel,
        [shaped((number, KEEP**3), BF16), shaped((1, number))],
        fitted,
        terms,
        known,
        meta,
        name="faces",
        flops=10**9,
    )
    (mean_field,) = call(
        integral_kernel,
        [shaped((own, S * S))],
        parts.reshape(groups, 128),
        integral,
        name="integrals",
    )
    return coefficients, energy.reshape(number), mean_field


def solution(mesh):
    in_specs = (
        P(("grp", "dev"), None),
        P(("grp", "dev"), None),
        P("dev", None),
        P(),
        P("dev", None),
        P("dev", None),
        P(),
    )
    out_specs = (P(("grp", "dev"), None), P(("grp", "dev")), P("dev", None))
    return jax.shard_map(body, mesh=mesh, in_specs=in_specs, out_specs=out_specs, check_vma=False)
```

time: 81.8 us -> 76.9 us (0.940)
  blocking collectives: 27.6 us -> 0 us
  starting transfers between devices: 17 us -> 30.3 us
  Pallas kernels: 29 us -> 34.7 us
  waiting for transfers between devices: 4.26 us -> 8.75 us
    all_to_all x1 -> x0, blocking collectives: 27.6 us -> none  [body(): lax.all_to_all(part.reshape(groups * devices, 1, 128), ('grp', 'dev'), 0,...]
    all_to_all x1 -> x2, starting transfers between devices: 4.96 us -> 18.3 us  [the longest x1 9.22 us: body(): lax.all_to_all(answer.reshape(devices, each, 1, 128), 'dev', 0, 0, tiled=...]
    all_to_all x1 -> x2, waiting for transfers between devices: 0.01 us -> 8.74 us  [the longest x1 8.58 us: body(): lax.all_to_all(answer.reshape(devices, each, 1, 128), 'dev', 0, 0, tiled=...]
    pallas_call x5 -> x7, Pallas kernels: 17.2 us -> 23.7 us  [call(): pl.pallas_call(kernel, out_shape=outs, in_specs=[vm] * len(args), out_spe...]
    all_to_all x1, waiting for transfers between devices: 4.26 us -> 0.01 us  [body(): came = lax.all_to_all(send, 'dev', 0, 0, tiled=True)]
    unnamed x5 -> x6, local copies, waits for them, and re-layouts: 2.77 us -> 1.96 us
  transfers between devices with their start and end apart: 2 -> 3, of which waited for: 1 -> 2; matrix products, arithmetic and copies ran while one was open for 0% -> 0% of each run, Pallas kernels for 20% -> 27%
where the time goes in v2:
time: 76.9 us; the launch traced here: 76.4 us
  Pallas kernels  34.7 us (45%)
  starting transfers between devices  30.3 us (39%)
  waiting for transfers between devices  8.75 us (11%)
  local copies, waits for them, and re-layouts  1.96 us (3%)
    pallas_call x7, Pallas kernels, call(): pl.pallas_call(kernel, out_shape=outs, in_specs=[vm] * len(args), out_spe...  23.7 us
    all_to_all x1, starting transfers between devices, body(): came = lax.all_to_all(send, 'dev', 0, 0, tiled=True)  12 us
    pallas_call x1, Pallas kernels, body(): pl.pallas_call(fit_kernel, grid=(steps,), out_shape=shaped((KEEP, number,...  11 us
    all_to_all x1, starting transfers between devices, body(): lax.all_to_all(answer.reshape(devices, each, 1, 128), 'dev', 0, 0, tiled=...  9.22 us
    all_to_all x1, starting transfers between devices, body(): lax.all_to_all(mine.reshape(groups, 1, 128), 'grp', 0, 0, tiled=True)  9.05 us
    all_to_all x1, waiting for transfers between devices, body(): lax.all_to_all(answer.reshape(devices, each, 1, 128), 'dev', 0, 0, tiled=...  8.58 us
    unnamed x6, local copies, waits for them, and re-layouts  1.96 us
  transfers between devices with their start and end apart: 3, of which 2 were waited for; matrix products, arithmetic and copies ran while one was open for 0% of the time, Pallas kernels for 27%

profile of v2, /device:TPU:1, one launch (start us, length us, event | category | flops | bytes accessed | tf_op | source)
XLA Modules:
  0.0 76.4 jit_solution(3678991670227347251)
XLA Ops:
  0.6 2.9 %ask.1 = (f32[32,2,128]{2,1,0:T(2,128)}, f32[384,128]{1,0:T(8,128)}) custom-call(s32[3,128]{1,0:T(4,128)} %bitcast.14, s32[114,114]{1,0:T(8,128)} %pair_ref.2, s32[1,114]{1,0:T(1,128)} %bitcast.15, f32[4,512]{1,0:T(4,128)} %modal_ref.3, f32[4,32]{1,0:T(4,128)} %single_ref.1, f32[512,128]{1,0:T(8,128)} %constant.14.clone.cos_ref, ...), custom_call_target="tpu_custom_call" | custom-call | bytes 570584 | tf_op jit(solution)/shard_map/ask/pallas_call | solution.py:348
  3.5 12.0 %all-to-all-start = ((f32[32,2,128]{2,1,0:T(2,128)}), f32[32,2,128]{2,1,0:T(2,128)S(1)}, u32[]{:S(2)}, u32[]{:S(2)}) async-start(f32[32,2,128]{2,1,0:T(2,128)} %get-tuple-element.11), calls=%async_computation | async-start | bytes 65536 | tf_op jit(solution)/shard_map/all_to_all | solution.py:390
  15.5 11.0 %fit.1.fit_ref = f32[16,128,256]{2,1,0:T(8,128)} custom-call(f32[16,32]{1,0:T(8,128)} %constant.16.clone.fit_ref, bf16[128,32768]{1,0:T(8,128)(2,1)} %back_ref.1, bf16[128,32768]{1,0:T(8,128)(2,1)} %back_ref.1, bf16[1024,256]{1,0:T(8,128)(2,1)} %constant.12.clone.hi_ref, bf16[1024,256]{1,0:T(8,128)(2,1)} %constant.13.clone.lo_ref), custom_call_target="tpu_custom_call" | custom-call | flops 5000000000 | bytes 11534336 | tf_op jit(solution)/shard_map/fit/pallas_call | solution.py:398
  26.5 3.1 %table.1 = (bf16[256,512]{1,0:T(8,128)(2,1)}, bf16[256,512]{1,0:T(8,128)(2,1)}) custom-call(f32[256,1024]{1,0:T(8,128)} %pair_ref.3, bf16[1024,256]{1,0:T(8,128)(2,1)} %constant.12.clone.hi_ref, bf16[1024,256]{1,0:T(8,128)(2,1)} %constant.13.clone.lo_ref), custom_call_target="tpu_custom_call" | custom-call | flops 500000000 | bytes 2621440 | tf_op jit(solution)/shard_map/table/pallas_call | solution.py:348
  29.6 0.0 all-to-all-done.came_ref
  29.6 0.0 copy-start.1
  29.6 0.6 copy-done.1
  30.2 7.9 %share.1 = (f32[800,128]{1,0:T(8,128)}, f32[384,128]{1,0:T(8,128)}) custom-call(f32[32,2,128]{2,1,0:T(2,128)} %copy-done.1, bf16[256,512]{1,0:T(8,128)(2,1)} %get-tuple-element.12.hi_ref, bf16[256,512]{1,0:T(8,128)(2,1)} %get-tuple-element.13.lo_ref, f32[16,128,256]{2,1,0:T(8,128)} %fit.1.fit_ref, f32[384,128]{1,0:T(8,128)} %get-tuple-element.14.meta_ref), custom_call_target="tpu_custom_call" | custom-call | flops 1000000000 | bytes 3457024 | tf_op jit(solution)/shard_map/share/pallas_call | solution.py:348
  38.1 9.2 %all-to-all-start.1 = ((f32[32,25,1,128]{3,2,1,0:T(1,128)}), f32[32,25,1,128]{3,2,1,0:T(1,128)S(1)}, u32[]{:S(2)}, u32[]{:S(2)}) async-start(f32[32,25,1,128]{3,2,1,0:T(1,128)} %bitcast.11), calls=%async_computation.1 | async-start | bytes 819200 | tf_op jit(solution)/shard_map/all_to_all | solution.py:427
  47.3 2.3 %unit.1.integral_ref = f32[128,256]{1,0:T(8,128)} custom-call(f32[4,512]{1,0:T(4,128)} %modal_ref.3, f32[128,128]{1,0:T(8,128)} %constant.17.clone.cosine_ref), custom_call_target="tpu_custom_call" | custom-call | flops 1000000000 | bytes 204800 | tf_op jit(solution)/shard_map/unit/pallas_call | solution.py:348
  49.6 8.6 %all-to-all-done.1 = f32[32,25,1,128]{3,2,1,0:T(1,128)S(1)} async-done(((f32[32,25,1,128]{3,2,1,0:T(1,128)}), f32[32,25,1,128]{3,2,1,0:T(1,128)S(1)}, u32[]{:S(2)}, u32[]{:S(2)}) %all-to-all-start.1) | async-done | bytes 409632 | tf_op jit(solution)/shard_map/all_to_all | solution.py:427
  58.2 0.0 copy-start
  58.2 0.8 %copy-done = f32[32,25,1,128]{3,2,1,0:T(1,128)} copy-done((f32[32,25,1,128]{3,2,1,0:T(1,128)}, f32[32,25,1,128]{3,2,1,0:T(1,128)S(1)}, u32[]{:S(2)}) %copy-start) | copy-done | bytes 409624
  58.9 1.6 %own.1 = f32[8,128]{1,0:T(8,128)} custom-call(f32[800,128]{1,0:T(8,128)} %bitcast.9), custom_call_target="tpu_custom_call" | custom-call | bytes 413696 | tf_op jit(solution)/shard_map/own/pallas_call | solution.py:348
  60.5 9.1 %all-to-all-start.2 = ((f32[8,1,128]{2,1,0:T(1,128)}), f32[8,1,128]{2,1,0:T(1,128)S(1)}, u32[]{:S(2)}, u32[]{:S(2)}) async-start(f32[8,1,128]{2,1,0:T(1,128)} %bitcast.12), calls=%async_computation.2 | async-start | bytes 8192 | tf_op jit(solution)/shard_map/all_to_all | solution.py:434
  69.6 4.3 %faces.1 = (bf16[128,4096]{1,0:T(8,128)(2,1)}, f32[1,128]{1,0:T(1,128)}) custom-call(f32[16,128,256]{2,1,0:T(8,128)} %fit.1.fit_ref, f32[800,128]{1,0:T(8,128)} %bitcast.10, f32[384,128]{1,0:T(8,128)} %get-tuple-element.16.known_ref, f32[384,128]{1,0:T(8,128)} %get-tuple-element.14.meta_ref), custom_call_target="tpu_custom_call" | custom-call | flops 1000000000 | bytes 3949056 | tf_op jit(solution)/shard_map/faces/pallas_call | solution.py:348
  73.9 0.2 all-to-all-done.2
  74.1 0.0 copy-start.2
  74.1 0.6 copy-done.2
  74.7 1.7 %integrals.1 = f32[4,256]{1,0:T(4,128)} custom-call(f32[8,128]{1,0:T(8,128)} %bitcast.13, f32[128,256]{1,0:T(8,128)} %unit.1.integral_ref), custom_call_target="tpu_custom_call" | custom-call | bytes 139264 | tf_op jit(solution)/shard_map/integrals/pallas_call | solution.py:348
Async XLA Ops:
  3.5 26.1 %all-to-all-start = ((f32[32,2,128]{2,1,0:T(2,128)}), f32[32,2,128]{2,1,0:T(2,128)S(1)}, u32[]{:S(2)}, u32[]{:S(2)}) async-start(f32[32,2,128]{2,1,0:T(2,128)} %get-tuple-element.11), calls=%async_computation | async-start | bytes 65536 | tf_op jit(solution)/shard_map/all_to_all | solution.py:390
  29.6 0.6 copy-start.1
  38.1 20.1 %all-to-all-start.1 = ((f32[32,25,1,128]{3,2,1,0:T(1,128)}), f32[32,25,1,128]{3,2,1,0:T(1,128)S(1)}, u32[]{:S(2)}, u32[]{:S(2)}) async-start(f32[32,25,1,128]{3,2,1,0:T(1,128)} %bitcast.11), calls=%async_computation.1 | async-start | bytes 819200 | tf_op jit(solution)/shard_map/all_to_all | solution.py:427
  58.2 0.8 %copy-start = (f32[32,25,1,128]{3,2,1,0:T(1,128)}, f32[32,25,1,128]{3,2,1,0:T(1,128)S(1)}, u32[]{:S(2)}) copy-start(f32[32,25,1,128]{3,2,1,0:T(1,128)S(1)} %all-to-all-done.1) | copy-start | bytes 1228804
  60.5 13.6 %all-to-all-start.2 = ((f32[8,1,128]{2,1,0:T(1,128)}), f32[8,1,128]{2,1,0:T(1,128)S(1)}, u32[]{:S(2)}, u32[]{:S(2)}) async-start(f32[8,1,128]{2,1,0:T(1,128)} %bitcast.12), calls=%async_computation.2 | async-start | bytes 8192 | tf_op jit(solution)/shard_map/all_to_all | solution.py:434
  74.1 0.6 copy-start.2

commit v3 on v2

--- a/solution.py
+++ b/solution.py
@@ -12,7 +12,8 @@
 F32 = jnp.float32
 BF16 = jnp.bfloat16
 HIGHEST = lax.Precision.HIGHEST
-VMEM_LIMIT = 56 * 2**20
+VMEM_LIMIT = 24 * 2**20
+LARGE_LIMIT = 52 * 2**20
 
 
 def tables():
@@ -156,40 +157,80 @@
     integral_ref[...] = dot_exact(cosine_ref[...], left * right)
 
 
-def fit_kernel(fit_ref, front_ref, back_ref, hi_ref, lo_ref, out_ref, two_ref):
-    step = pl.program_id(0)
-    number = front_ref.shape[0]
+def fit_kernel(fit_ref, source_ref, hi_ref, lo_ref, out_ref, two_ref, energy_ref, sems):
+    number = energy_ref.shape[0]
     cells = G * G
-    per = front_ref.shape[1] // cells
-    parts = [front_ref[:, j * cells : (j + 1) * cells] for j in range(per)]
-    parts += [back_ref[:, (per - 1 - j) * cells : (per - j) * cells] for j in range(per)]
-    stacked = jnp.concatenate(parts, axis=0)
-    two = dot(stacked, hi_ref[...]) + dot(stacked, lo_ref[...])
-    for j in range(per):
-        a = two[j * number : (j + 1) * number]
-        b = two[(per + j) * number : (per + j + 1) * number]
-        two_ref[0, j] = a + b
-        two_ref[1, j] = a - b
-
-    @pl.when(step == 0)
-    def _():
-        out_ref[...] = jnp.zeros_like(out_ref)
-
-    def add(q, carry):
-        for parity in range(2):
-            c = 2 * q + parity
-            total = two_ref[parity, 0] * fit_ref[c, step * per]
-            for j in range(1, per):
-                total = total + two_ref[parity, j] * fit_ref[c, step * per + j]
-            out_ref[c] += total
-        return carry
-
-    lax.fori_loop(0, KEEP // 2, add, 0)
-
-
-def share_kernel(came_ref, hi_ref, lo_ref, fit_ref, meta_ref, out_ref, known_ref):
+    per = two_ref.shape[1]
+    steps = G // (2 * per)
+
+    def copies(step):
+        for end, block in enumerate((step, 2 * steps - 1 - step)):
+            cols = pl.ds(pl.multiple_of(block * per * cells, cells), per * cells)
+            yield pltpu.make_async_copy(source_ref.at[:, cols], energy_ref.at[:, cols], sems.at[step, end])
+
+    for step in range(steps):
+        for copy in copies(step):
+            copy.start()
+    out_ref[...] = jnp.zeros_like(out_ref)
+
+    def step_of(step, carry):
+        for copy in copies(step):
+            copy.wait()
+        front = pl.multiple_of(step * per * cells, cells)
+        back = pl.multiple_of((2 * steps - 1 - step) * per * cells, cells)
+        front = energy_ref[:, pl.ds(front, per * cells)]
+        back = energy_ref[:, pl.ds(back, per * cells)]
+        parts = [front[:, j * cells : (j + 1) * cells] for j in range(per)]
+        parts += [back[:, (per - 1 - j) * cells : (per - j) * cells] for j in range(per)]
+        stacked = jnp.concatenate(parts, axis=0)
+        two = dot(stacked, hi_ref[...]) + dot(stacked, lo_ref[...])
+        for j in range(per):
+            a = two[j * number : (j + 1) * number]
+            b = two[(per + j) * number : (per + j + 1) * number]
+            two_ref[0, j] = a + b
+            two_ref[1, j] = a - b
+
+        def add(q, carry):
+            for parity in range(2):
+                c = 2 * q + parity
+                total = two_ref[parity, 0] * fit_ref[c, step * per]
+                for j in range(1, per):
+                    total = total + two_ref[parity, j] * fit_ref[c, step * per + j]
+                out_ref[c] += total
+            return carry
+
+        return lax.fori_loop(0, KEEP // 2, add, carry)
+
+    lax.fori_loop(0, steps, step_of, 0)
+
+
+def share_kernel(
+    came_ref,
+    hi_ref,
+    lo_ref,
+    source_ref,
+    meta_ref,
+    fit_ref,
+    wide_ref,
+    out_ref,
+    known_ref,
+    w1_ref,
+    w23_ref,
+    lead_ref,
+    v_ref,
+    energy_ref,
+    sems,
+):
+    tile = 16
+
+    def copy(r):
+        rows_r = pl.ds(pl.multiple_of(r * tile, tile), tile)
+        return pltpu.make_async_copy(source_ref.at[rows_r], energy_ref.at[rows_r], sems.at[r])
+
+    for r in range(energy_ref.shape[0] // tile):
+        copy(r).start()
     peers = came_ref.shape[0]
-    number = fit_ref.shape[1]
+    number = energy_ref.shape[0]
     rows = 3 * number
     asked = came_ref[:, 1, :].astype(BF16)
     per = float(rows // peers)
@@ -213,7 +254,6 @@
     known_ref[...] = known[:rows]
     k, n = iota((128, 256), 0), iota((128, 256), 1)
     widen = (k == (n >> 4)).astype(F32).astype(BF16)
-    widen_single = ((k == (n >> 4) + 16) & ((n & 15) == 0)).astype(F32).astype(BF16)
     k, n = iota((256, 128), 0), iota((256, 128), 1)
     to_high = ((k >> 4) == n).astype(F32).astype(BF16)
     to_low = ((k & 15) == n).astype(F32).astype(BF16)
@@ -234,26 +274,69 @@
     lane = iota((rows, 128), 1)
     shares = [-norm * of_small, -norm * of_large, jnp.where(lane == 0, -of_other, 0.0)]
     one, two, three = (known[p * number : (p + 1) * number] for p in range(3))
-    two_wide = dot_two(two, widen)
-    three_wide = twice(repeated(three))
-    both = two_wide * three_wide
-    lane = iota((number, 256), 1)
-    single = dot_two(two, widen_single) + jnp.where(
-        lane < 16, twice(pltpu.roll(three, 112, 1)), 0.0
-    )
-    thin = iota((number, 128), 1)
-    field_first = jnp.zeros((number, 128), F32)
-    lead = jnp.zeros((number, 256), F32)
-    for c in range(KEEP):
-        value = fit_ref[c] - jnp.where(lane == 0, one[:, 16 + c : 17 + c], 0.0)
-        if c == 0:
-            value = value - single
-        along = value * both
-        field_first = field_first + jnp.where(thin == c, lane_sum(along[:, :128] + along[:, 128:]), 0.0)
-        lead = lead + one[:, c : c + 1] * value
-    field_second = dot_two(lead * three_wide, to_high)
-    field_third = dot_two(lead * two_wide, to_low)
-    fields = jnp.concatenate([field_first, field_second, field_third] + shares, axis=0)
+    cells = G * G
+    w1_ref[...] = jnp.broadcast_to(lane_sum(fit_ref[...] * one[0:1]), w1_ref.shape)
+    ways = [wide_ref[p] for p in range(4)]
+
+    def weights(a, hi, lo):
+        a_hi, a_lo = halves(a[:, :32])
+        return dot(a_hi, hi) + dot(a_hi, lo) + dot(a_lo, hi)
+
+    w2 = weights(two, ways[0], ways[1])
+    w3 = weights(three, ways[2], ways[3])
+    w23_ref[...] = w2 * w3
+    lanes = cells // 128
+
+    def over_rows(r, carry):
+        copy(r).wait()
+        rows_r = pl.ds(pl.multiple_of(r * tile, tile), tile)
+        w23 = [w23_ref[rows_r, k * 128 : (k + 1) * 128] for k in range(lanes)]
+        thin = iota((tile, 128), 1)
+
+        def over_points(g, state):
+            v, lead = state
+            x = energy_ref[rows_r, pl.ds(pl.multiple_of(g * cells, cells), cells)].astype(F32)
+            w1 = w1_ref[pl.ds(g, 1), :]
+            fresh, along = [], None
+            for k in range(lanes):
+                part = x[:, k * 128 : (k + 1) * 128]
+                fresh.append(lead[k] + w1 * part)
+                term = part * w23[k]
+                along = term if along is None else along + term
+            return v + jnp.where(thin == g, lane_sum(along), 0.0), tuple(fresh)
+
+        none = jnp.zeros((tile, 128), F32)
+        v, lead = lax.fori_loop(0, G, over_points, (none, (none,) * lanes), unroll=2)
+        v_ref[rows_r, :] = v
+        for k in range(lanes):
+            lead_ref[rows_r, k * 128 : (k + 1) * 128] = lead[k]
+        return carry
+
+    lax.fori_loop(0, number // tile, over_rows, 0)
+
+    def back(a, hi, lo):
+        a_hi, a_lo = halves(a)
+        dims = (((1,), (1,)), ((), ()))
+        total = lax.dot_general(a_hi, hi, dims, preferred_element_type=F32)
+        total = total + lax.dot_general(a_hi, lo, dims, preferred_element_type=F32)
+        total = total + lax.dot_general(a_lo, hi, dims, preferred_element_type=F32)
+        return jnp.concatenate([total, jnp.zeros((number, 96), F32)], axis=1)
+
+    field_first = dot_exact(v_ref[:, :G], fit_ref[...])
+    field_second = back(lead_ref[...] * w3, ways[0], ways[1])
+    field_third = back(lead_ref[...] * w2, ways[2], ways[3])
+    own = known[:rows]
+    lane = iota((rows, 128), 1)
+    single = jnp.where(lane < 16, pltpu.roll(own, 112, 1), 0.0)
+    along = lane_sum(single * own)
+    norms = own[:, 0:1]
+    n1, n2, n3 = (norms[p * number : (p + 1) * number] for p in range(3))
+    q1, q2, q3 = (along[p * number : (p + 1) * number] for p in range(3))
+    scale = jnp.concatenate([n2 * n3, n1 * n3, n1 * n2], axis=0)
+    shift = jnp.concatenate([n3 * q2 + n2 * q3, n3 * q1 + n1 * q3, n2 * q1 + n1 * q2], axis=0)
+    from_grid = jnp.concatenate([field_first, field_second, field_third], axis=0)
+    from_grid = from_grid - scale * single - jnp.where(lane == 0, shift, 0.0)
+    fields = jnp.concatenate([from_grid] + shares, axis=0)
     fields = fields + pltpu.roll(fields, 16, 1)
     fields = fields + pltpu.roll(fields, 32, 1)
     fields = jnp.where((iota(fields.shape, 1) >> 4).astype(F32) == sub, fields, 0.0)
@@ -340,7 +423,7 @@
     out_ref[...] = dot_exact(total, integral_ref[...])
 
 
-def call(kernel, outs, *args, name, smem=(), flops=0):
+def call(kernel, outs, *args, name, smem=(), apart=(), flops=0, scratch=(), room=VMEM_LIMIT):
     vm = pl.BlockSpec(memory_space=pltpu.VMEM)
     moved = sum(int(np.prod(a.shape)) * a.dtype.itemsize for a in args) + sum(
         int(np.prod(o.shape)) * o.dtype.itemsize for o in outs
@@ -348,9 +431,13 @@
     return pl.pallas_call(
         kernel,
         out_shape=outs,
-        in_specs=[vm] * len(args),
+        in_specs=[
+            pl.BlockSpec(memory_space=pltpu.SMEM if i in smem else pltpu.HBM if i in apart else pltpu.VMEM)
+            for i in range(len(args))
+        ],
         out_specs=[vm] * len(outs),
-        compiler_params=pltpu.CompilerParams(vmem_limit_bytes=VMEM_LIMIT),
+        scratch_shapes=list(scratch),
+        compiler_params=pltpu.CompilerParams(vmem_limit_bytes=room),
         cost_estimate=pl.CostEstimate(flops=flops, bytes_accessed=moved, transcendentals=0),
         name=name,
     )(*args)
@@ -375,6 +462,12 @@
         cos_block[m * KEEP : (m + 1) * KEEP, m * G : (m + 1) * G] = COSINES
     kron = np.einsum("dh,el->hlde", FITTER, FITTER).reshape(G * G, KEEP * KEEP)
     hi, lo = (jnp.asarray(x) for x in halves_np(kron))
+    fit_rows = np.zeros((G, 128), np.float32)
+    fit_rows[:, :KEEP] = FITTER.T
+    wide = np.zeros((2, 32, G, G))
+    wide[0, :KEEP] = FITTER[:, :, None]
+    wide[1, :KEEP] = FITTER[:, None, :]
+    wide = jnp.asarray(np.stack([h[p] for p in range(2) for h in halves_np(wide.reshape(2, 32, G * G))]))
     send, meta = call(
         ask_kernel,
         [shaped((devices, 2, 128)), shaped((3 * number, 128))],
@@ -392,26 +485,6 @@
     table_hi, table_lo = call(
         table_kernel, [table, table], pair_surfaces, hi, lo, name="table", flops=5 * 10**8
     )
-    per = 4
-    steps = G // (2 * per)
-    block = per * G * G
-    fitted = pl.pallas_call(
-        fit_kernel,
-        grid=(steps,),
-        out_shape=shaped((KEEP, number, KEEP**2)),
-        in_specs=[
-            pl.BlockSpec(memory_space=pltpu.SMEM),
-            pl.BlockSpec((number, block), lambda i: (0, i)),
-            pl.BlockSpec((number, block), lambda i: (0, 2 * steps - 1 - i)),
-            pl.BlockSpec((G * G, 256), lambda i: (0, 0)),
-            pl.BlockSpec((G * G, 256), lambda i: (0, 0)),
-        ],
-        out_specs=pl.BlockSpec((KEEP, number, KEEP**2), lambda i: (0, 0, 0)),
-        scratch_shapes=[pltpu.VMEM((2, per, number, 256), F32)],
-        compiler_params=pltpu.CompilerParams(vmem_limit_bytes=VMEM_LIMIT),
-        cost_estimate=pl.CostEstimate(flops=5 * 10**9, bytes_accessed=11 * 2**20, transcendentals=0),
-        name="fit",
-    )(jnp.asarray(FITTER.astype(np.float32)), energies, energies, hi, lo)
     each = 2 * capacity + 1
     answer, known = call(
         share_kernel,
@@ -419,14 +492,45 @@
         came,
         table_hi,
         table_lo,
-        fitted,
+        energies,
         meta,
+        jnp.asarray(fit_rows),
+        wide,
+        apart=(3,),
+        room=LARGE_LIMIT,
         name="share",
         flops=10**9,
+        scratch=[
+            pltpu.VMEM((G, 128), F32),
+            pltpu.VMEM((number, G * G), F32),
+            pltpu.VMEM((number, G * G), F32),
+            pltpu.VMEM((number, 128), F32),
+            pltpu.VMEM(energies.shape, BF16),
+            pltpu.SemaphoreType.DMA((number // 16,)),
+        ],
     )
     terms = lax.all_to_all(
         answer.reshape(devices, each, 1, 128), "dev", 0, 0, tiled=True
     ).reshape(devices * each, 128)
+    per = 4
+    (fitted,) = call(
+        fit_kernel,
+        [shaped((KEEP, number, KEEP**2))],
+        jnp.asarray(FITTER.astype(np.float32)),
+        energies,
+        hi,
+        lo,
+        name="fit",
+        flops=5 * 10**9,
+        smem=(0,),
+        apart=(1,),
+        room=LARGE_LIMIT,
+        scratch=[
+            pltpu.VMEM((2, per, number, 256), F32),
+            pltpu.VMEM(energies.shape, BF16),
+            pltpu.SemaphoreType.DMA((G // (2 * per), 2)),
+        ],
+    )
     (integral,) = call(
         unit_kernel, [shaped((128, S * S))], modals, jnp.asarray(cos_block), name="unit", flops=10**9
     )

time: 76.9 us -> 79.9 us (1.039)
  local copies, waits for them, and re-layouts: 1.96 us -> 11.8 us
  starting transfers between devices: 30.3 us -> 24.6 us
  waiting for transfers between devices: 8.75 us -> 4.91 us
  Pallas kernels: 34.7 us -> 37.1 us
    unnamed x6 -> x36, local copies, waits for them, and re-layouts: 1.96 us -> 11.8 us
    all_to_all x1, waiting for transfers between devices: 8.58 us -> 0.01 us  [body(): lax.all_to_all(answer.reshape(devices, each, 1, 128), 'dev', 0, 0, tiled=...]
    all_to_all x1, waiting for transfers between devices: 0.01 us -> 4.61 us  [body(): came = lax.all_to_all(send, 'dev', 0, 0, tiled=True)]
    all_to_all x1, starting transfers between devices: 9.22 us -> 4.65 us  [body(): lax.all_to_all(answer.reshape(devices, each, 1, 128), 'dev', 0, 0, tiled=...]
    pallas_call x8, Pallas kernels: 34.7 us -> 37.1 us  [call(): pl.pallas_call(kernel, out_shape=outs, in_specs=[pl.BlockSpec(memory_spac...]
    all_to_all x1, starting transfers between devices: 9.05 us -> 7.92 us  [body(): lax.all_to_all(mine.reshape(groups, 1, 128), 'grp', 0, 0, tiled=True)]
  transfers between devices with their start and end apart: 3 -> 3, of which waited for: 2 -> 2; matrix products, arithmetic and copies ran while one was open for 0% -> 0% of each run, Pallas kernels for 27% -> 19%
where the time goes in v3:
time: 79.9 us; the launch traced here: 79.1 us
  Pallas kernels  37.1 us (46%)
  starting transfers between devices  24.6 us (31%)
  local copies, waits for them, and re-layouts  11.8 us (15%)
  waiting for transfers between devices  4.91 us (6%)
    pallas_call x8, Pallas kernels, call(): pl.pallas_call(kernel, out_shape=outs, in_specs=[pl.BlockSpec(memory_spac...  37.1 us
    all_to_all x1, starting transfers between devices, body(): came = lax.all_to_all(send, 'dev', 0, 0, tiled=True)  12 us
    unnamed x36, local copies, waits for them, and re-layouts  11.8 us
    all_to_all x1, starting transfers between devices, body(): lax.all_to_all(mine.reshape(groups, 1, 128), 'grp', 0, 0, tiled=True)  7.92 us
    all_to_all x1, starting transfers between devices, body(): lax.all_to_all(answer.reshape(devices, each, 1, 128), 'dev', 0, 0, tiled=...  4.65 us
    all_to_all x1, waiting for transfers between devices, body(): came = lax.all_to_all(send, 'dev', 0, 0, tiled=True)  4.61 us
  transfers between devices with their start and end apart: 3, of which 2 were waited for; matrix products, arithmetic and copies ran while one was open for 0% of the time, Pallas kernels for 19%

profile of v3, /device:TPU:1, one launch (start us, length us, event | category | flops | bytes accessed | tf_op | source)
XLA Modules:
  0.0 79.1 jit_solution(9874264934921565106)
XLA Ops:
  0.6 0.0 copy-start.6
  0.6 0.9 %copy-done.6 = f32[512,128]{1,0:T(8,128)S(1)} copy-done((f32[512,128]{1,0:T(8,128)S(1)}, f32[512,128]{1,0:T(8,128)}, u32[]{:S(2)}) %copy-start.6) | copy-done | bytes 262168
  1.6 0.0 copy-start.7
  1.6 0.8 %copy-done.7 = s32[114,114]{1,0:T(8,128)S(1)} copy-done((s32[114,114]{1,0:T(8,128)S(1)}, s32[114,114]{1,0:T(8,128)}, u32[]{:S(2)}) %copy-start.7) | copy-done | bytes 52008
  2.4 0.0 copy-start.9
  2.4 0.7 copy-done.9
  3.1 0.0 copy-start.10
  3.1 0.7 copy-done.10
  3.8 0.0 copy-start.12
  3.8 0.7 copy-done.12
  4.5 0.0 copy-start.13
  4.5 0.7 copy-done.13
  5.2 0.0 copy-start.14
  5.2 0.7 copy-done.14
  5.9 0.0 copy-start.11
  5.9 0.0 copy-start.15
  5.9 0.0 copy-start.16
  5.9 1.9 %ask.1 = (f32[32,2,128]{2,1,0:T(2,128)}, f32[384,128]{1,0:T(8,128)S(1)}) custom-call(s32[3,128]{1,0:T(4,128)S(1)} %bitcast.12, s32[114,114]{1,0:T(8,128)S(1)} %copy-done.7, s32[1,114]{1,0:T(1,128)S(1)} %bitcast.13, f32[4,512]{1,0:T(4,128)S(1)} %copy-done.10, f32[4,32]{1,0:T(4,128)S(1)} %copy-done.13, f32[512,128]{1,0:T(8,128)S(1)} %copy-done.6, ...), custom_call_target="tpu_custom_call" | custom-call | bytes 570584 | tf_op jit(solution)/shard_map/ask/pallas_call | solution.py:431
  7.8 12.0 %all-to-all-start = ((f32[32,2,128]{2,1,0:T(2,128)}), f32[32,2,128]{2,1,0:T(2,128)S(1)}, u32[]{:S(2)}, u32[]{:S(2)}) async-start(f32[32,2,128]{2,1,0:T(2,128)} %get-tuple-element.11), calls=%async_computation | async-start | bytes 65536 | tf_op jit(solution)/shard_map/all_to_all | solution.py:483
  19.8 0.0 copy-start
  19.8 1.2 %copy-done = f32[256,1024]{1,0:T(8,128)S(1)} copy-done((f32[256,1024]{1,0:T(8,128)S(1)}, f32[256,1024]{1,0:T(8,128)}, u32[]{:S(2)}) %copy-start) | copy-done | bytes 1048600
  21.0 0.0 copy-start.1
  21.0 1.0 %copy-done.1 = bf16[1024,256]{1,0:T(8,128)(2,1)S(1)} copy-done((bf16[1024,256]{1,0:T(8,128)(2,1)S(1)}, bf16[1024,256]{1,0:T(8,128)(2,1)}, u32[]{:S(2)}) %copy-start.1) | copy-done | bytes 524312
  22.1 0.0 copy-start.3
  22.1 1.0 %copy-done.3 = bf16[1024,256]{1,0:T(8,128)(2,1)S(1)} copy-done((bf16[1024,256]{1,0:T(8,128)(2,1)S(1)}, bf16[1024,256]{1,0:T(8,128)(2,1)}, u32[]{:S(2)}) %copy-start.3) | copy-done | bytes 524312
  23.1 0.0 copy-start.2
  23.1 0.0 copy-start.4
  23.1 0.8 %table.1 = (bf16[256,512]{1,0:T(8,128)(2,1)S(1)}, bf16[256,512]{1,0:T(8,128)(2,1)S(1)}) custom-call(f32[256,1024]{1,0:T(8,128)S(1)} %copy-done, bf16[1024,256]{1,0:T(8,128)(2,1)S(1)} %copy-done.1, bf16[1024,256]{1,0:T(8,128)(2,1)S(1)} %copy-done.3), custom_call_target="tpu_custom_call" | custom-call | flops 500000000 | bytes 2621440 | tf_op jit(solution)/shard_map/table/pallas_call | solution.py:431
  24.0 4.6 %all-to-all-done.came_ref = f32[32,2,128]{2,1,0:T(2,128)S(1)} async-done(((f32[32,2,128]{2,1,0:T(2,128)}), f32[32,2,128]{2,1,0:T(2,128)S(1)}, u32[]{:S(2)}, u32[]{:S(2)}) %all-to-all-start) | async-done | bytes 32800 | tf_op jit(solution)/shard_map/all_to_all | solution.py:483
  28.6 0.0 copy-start.5
  28.6 0.9 %copy-done.5 = bf16[4,32,1024]{2,1,0:T(8,128)(2,1)S(1)} copy-done((bf16[4,32,1024]{2,1,0:T(8,128)(2,1)S(1)}, bf16[4,32,1024]{2,1,0:T(8,128)(2,1)}, u32[]{:S(2)}) %copy-start.5) | copy-done | bytes 262168
  29.5 0.0 copy-start.8
  29.5 0.7 copy-done.8
  30.2 18.4 %share.1 = (f32[800,128]{1,0:T(8,128)}, f32[384,128]{1,0:T(8,128)S(1)}) custom-call(f32[32,2,128]{2,1,0:T(2,128)S(1)} %all-to-all-done.came_ref, bf16[256,512]{1,0:T(8,128)(2,1)S(1)} %get-tuple-element.12.hi_ref, bf16[256,512]{1,0:T(8,128)(2,1)S(1)} %get-tuple-element.13.lo_ref, bf16[128,32768]{1,0:T(8,128)(2,1)} %source_ref.3, ...), custom_call_target="tpu_custom_call" | custom-call | flops 1000000000 | bytes 10027008 | tf_op jit(solution)/shard_map/share/pallas_call | solution.py:431
  48.7 4.6 %all-to-all-start.1 = ((f32[32,25,1,128]{3,2,1,0:T(1,128)}), f32[32,25,1,128]{3,2,1,0:T(1,128)S(1)}, u32[]{:S(2)}, u32[]{:S(2)}) async-start(f32[32,25,1,128]{3,2,1,0:T(1,128)} %bitcast.2), calls=%async_computation.1 | async-start | bytes 819200 | tf_op jit(solution)/shard_map/all_to_all | solution.py:512
  53.3 0.0 copy-done.11
  53.3 0.0 copy-done.15
  53.3 0.8 unit.1.integral_ref
  54.1 0.0 copy-done.16
  54.1 0.0 copy-done.2
  54.1 0.0 copy-done.4
  54.1 11.2 %fit.1.fit_ref = f32[16,128,256]{2,1,0:T(8,128)} custom-call(f32[16,32]{1,0:T(8,128)S(1)} %copy-done.16, bf16[128,32768]{1,0:T(8,128)(2,1)} %source_ref.3, bf16[1024,256]{1,0:T(8,128)(2,1)S(1)} %copy-done.2, bf16[1024,256]{1,0:T(8,128)(2,1)S(1)} %copy-done.4), custom_call_target="tpu_custom_call" | custom-call | flops 5000000000 | bytes 11536384 | tf_op jit(solution)/shard_map/fit/pallas_call | solution.py:431
  65.3 0.0 all-to-all-done.1
  65.3 0.6 own.1
  65.9 7.9 %all-to-all-start.2 = ((f32[8,1,128]{2,1,0:T(1,128)}), f32[8,1,128]{2,1,0:T(1,128)S(1)}, u32[]{:S(2)}, u32[]{:S(2)}) async-start(f32[8,1,128]{2,1,0:T(1,128)} %bitcast.6), calls=%async_computation.2 | async-start | bytes 8192 | tf_op jit(solution)/shard_map/all_to_all | solution.py:538
  73.8 0.0 copy-start.17
  73.8 1.6 %copy-done.17 = f32[16,128,256]{2,1,0:T(8,128)S(1)} copy-done((f32[16,128,256]{2,1,0:T(8,128)S(1)}, f32[16,128,256]{2,1,0:T(8,128)}, u32[]{:S(2)}) %copy-start.17) | copy-done | bytes 2097176
  75.4 2.6 %faces.1 = (bf16[128,4096]{1,0:T(8,128)(2,1)}, f32[1,128]{1,0:T(1,128)}) custom-call(f32[16,128,256]{2,1,0:T(8,128)S(1)} %copy-done.17, f32[800,128]{1,0:T(8,128)S(1)} %bitcast.10, f32[384,128]{1,0:T(8,128)S(1)} %get-tuple-element.16.known_ref, f32[384,128]{1,0:T(8,128)S(1)} %get-tuple-element.14.meta_ref), custom_call_target="tpu_custom_call" | custom-call | flops 1000000000 | bytes 3949056 | tf_op jit(solution)/shard_map/faces/pallas_call | solution.py:431
  78.0 0.3 all-to-all-done.2
  78.3 0.8 integrals.1
Async XLA Ops:
  0.6 1.0 %copy-start.6 = (f32[512,128]{1,0:T(8,128)S(1)}, f32[512,128]{1,0:T(8,128)}, u32[]{:S(2)}) copy-start(f32[512,128]{1,0:T(8,128)} %constant.19.clone.cos_ref) | copy-start | bytes 786436
  1.6 0.8 %copy-start.7 = (s32[114,114]{1,0:T(8,128)S(1)}, s32[114,114]{1,0:T(8,128)}, u32[]{:S(2)}) copy-start(s32[114,114]{1,0:T(8,128)} %pair_ref.2) | copy-start | bytes 155956
  2.4 0.7 copy-start.9
  3.1 0.7 copy-start.10
  3.8 0.7 copy-start.12
  4.5 0.7 copy-start.13
  5.2 0.7 copy-start.14
  5.9 47.5 %copy-start.11 = (f32[4,512]{1,0:T(4,128)S(1)}, f32[4,512]{1,0:T(4,128)}, u32[]{:S(2)}) copy-start(f32[4,512]{1,0:T(4,128)} %modal_ref.3) | copy-start | bytes 24580
  5.9 47.5 %copy-start.15 = (f32[128,128]{1,0:T(8,128)S(1)}, f32[128,128]{1,0:T(8,128)}, u32[]{:S(2)}) copy-start(f32[128,128]{1,0:T(8,128)} %constant.23.clone.cosine_ref) | copy-start | bytes 196612
  5.9 48.3 %copy-start.16 = (f32[16,32]{1,0:T(8,128)S(1)}, f32[16,32]{1,0:T(8,128)}, u32[]{:S(2)}) copy-start(f32[16,32]{1,0:T(8,128)} %constant.22.clone.fit_ref) | copy-start | bytes 6148
  7.8 20.8 %all-to-all-start = ((f32[32,2,128]{2,1,0:T(2,128)}), f32[32,2,128]{2,1,0:T(2,128)S(1)}, u32[]{:S(2)}, u32[]{:S(2)}) async-start(f32[32,2,128]{2,1,0:T(2,128)} %get-tuple-element.11), calls=%async_computation | async-start | bytes 65536 | tf_op jit(solution)/shard_map/all_to_all | solution.py:483
  19.8 1.2 %copy-start = (f32[256,1024]{1,0:T(8,128)S(1)}, f32[256,1024]{1,0:T(8,128)}, u32[]{:S(2)}) copy-start(f32[256,1024]{1,0:T(8,128)} %pair_ref.3) | copy-start | bytes 3145732
  21.0 1.0 %copy-start.1 = (bf16[1024,256]{1,0:T(8,128)(2,1)S(1)}, bf16[1024,256]{1,0:T(8,128)(2,1)}, u32[]{:S(2)}) copy-start(bf16[1024,256]{1,0:T(8,128)(2,1)} %constant.16.clone.hi_ref) | copy-start | bytes 1572868
  22.1 1.0 %copy-start.3 = (bf16[1024,256]{1,0:T(8,128)(2,1)S(1)}, bf16[1024,256]{1,0:T(8,128)(2,1)}, u32[]{:S(2)}) copy-start(bf16[1024,256]{1,0:T(8,128)(2,1)} %constant.17.clone.lo_ref) | copy-start | bytes 1572868
  23.1 31.0 %copy-start.2 = (bf16[1024,256]{1,0:T(8,128)(2,1)S(1)}, bf16[1024,256]{1,0:T(8,128)(2,1)}, u32[]{:S(2)}) copy-start(bf16[1024,256]{1,0:T(8,128)(2,1)} %constant.16.clone.hi_ref) | copy-start | bytes 1572868
  23.1 31.0 %copy-start.4 = (bf16[1024,256]{1,0:T(8,128)(2,1)S(1)}, bf16[1024,256]{1,0:T(8,128)(2,1)}, u32[]{:S(2)}) copy-start(bf16[1024,256]{1,0:T(8,128)(2,1)} %constant.17.clone.lo_ref) | copy-start | bytes 1572868
  28.6 1.0 %copy-start.5 = (bf16[4,32,1024]{2,1,0:T(8,128)(2,1)S(1)}, bf16[4,32,1024]{2,1,0:T(8,128)(2,1)}, u32[]{:S(2)}) copy-start(bf16[4,32,1024]{2,1,0:T(8,128)(2,1)} %constant.18.clone.wide_ref) | copy-start | bytes 786436
  29.5 0.7 copy-start.8
  48.7 16.7 %all-to-all-start.1 = ((f32[32,25,1,128]{3,2,1,0:T(1,128)}), f32[32,25,1,128]{3,2,1,0:T(1,128)S(1)}, u32[]{:S(2)}, u32[]{:S(2)}) async-start(f32[32,25,1,128]{3,2,1,0:T(1,128)} %bitcast.2), calls=%async_computation.1 | async-start | bytes 819200 | tf_op jit(solution)/shard_map/all_to_all | solution.py:512
  65.9 12.4 %all-to-all-start.2 = ((f32[8,1,128]{2,1,0:T(1,128)}), f32[8,1,128]{2,1,0:T(1,128)S(1)}, u32[]{:S(2)}, u32[]{:S(2)}) async-start(f32[8,1,128]{2,1,0:T(1,128)} %bitcast.6), calls=%async_computation.2 | async-start | bytes 8192 | tf_op jit(solution)/shard_map/all_to_all | solution.py:538
  73.8 1.6 %copy-start.17 = (f32[16,128,256]{2,1,0:T(8,128)S(1)}, f32[16,128,256]{2,1,0:T(8,128)}, u32[]{:S(2)}) copy-start(f32[16,128,256]{2,1,0:T(8,128)} %fit.1.fit_ref) | copy-start | bytes 6291460

commit v4 on v3

--- a/solution.py
+++ b/solution.py
@@ -13,7 +13,6 @@
 BF16 = jnp.bfloat16
 HIGHEST = lax.Precision.HIGHEST
 VMEM_LIMIT = 24 * 2**20
-LARGE_LIMIT = 52 * 2**20
 
 
 def tables():
@@ -157,51 +156,45 @@
     integral_ref[...] = dot_exact(cosine_ref[...], left * right)
 
 
-def fit_kernel(fit_ref, source_ref, hi_ref, lo_ref, out_ref, two_ref, energy_ref, sems):
+def fit_kernel(
+    source_ref, hi_ref, lo_ref, first_hi_ref, first_lo_ref, far_ref, energy_ref, out_ref, sems, out_sems
+):
     number = energy_ref.shape[0]
     cells = G * G
-    per = two_ref.shape[1]
-    steps = G // (2 * per)
-
-    def copies(step):
-        for end, block in enumerate((step, 2 * steps - 1 - step)):
-            cols = pl.ds(pl.multiple_of(block * per * cells, cells), per * cells)
-            yield pltpu.make_async_copy(source_ref.at[:, cols], energy_ref.at[:, cols], sems.at[step, end])
-
-    for step in range(steps):
-        for copy in copies(step):
-            copy.start()
-    out_ref[...] = jnp.zeros_like(out_ref)
-
-    def step_of(step, carry):
-        for copy in copies(step):
-            copy.wait()
-        front = pl.multiple_of(step * per * cells, cells)
-        back = pl.multiple_of((2 * steps - 1 - step) * per * cells, cells)
-        front = energy_ref[:, pl.ds(front, per * cells)]
-        back = energy_ref[:, pl.ds(back, per * cells)]
-        parts = [front[:, j * cells : (j + 1) * cells] for j in range(per)]
-        parts += [back[:, (per - 1 - j) * cells : (per - j) * cells] for j in range(per)]
-        stacked = jnp.concatenate(parts, axis=0)
+    tile, few = 32, 8
+    tiles = number // tile
+
+    def copy(r):
+        rows = pl.ds(pl.multiple_of(r * tile, tile), tile)
+        return pltpu.make_async_copy(source_ref.at[rows], energy_ref.at[rows], sems.at[r])
+
+    def copy_out(r):
+        rows = pl.ds(pl.multiple_of(r * tile, tile), tile)
+        return pltpu.make_async_copy(out_ref.at[:, rows], far_ref.at[:, rows], out_sems.at[r])
+
+    for r in range(tiles):
+        copy(r).start()
+
+    def over_rows(r, carry):
+        copy(r).wait()
+        rows = pl.ds(pl.multiple_of(r * tile, tile), tile)
+        stacked = jnp.concatenate([energy_ref[rows, g * cells : (g + 1) * cells] for g in range(G)], axis=0)
         two = dot(stacked, hi_ref[...]) + dot(stacked, lo_ref[...])
-        for j in range(per):
-            a = two[j * number : (j + 1) * number]
-            b = two[(per + j) * number : (per + j + 1) * number]
-            two_ref[0, j] = a + b
-            two_ref[1, j] = a - b
-
-        def add(q, carry):
-            for parity in range(2):
-                c = 2 * q + parity
-                total = two_ref[parity, 0] * fit_ref[c, step * per]
-                for j in range(1, per):
-                    total = total + two_ref[parity, j] * fit_ref[c, step * per + j]
-                out_ref[c] += total
-            return carry
-
-        return lax.fori_loop(0, KEEP // 2, add, carry)
-
-    lax.fori_loop(0, steps, step_of, 0)
+        for h in range(tile // few):
+            part = jnp.concatenate(
+                [two[g * tile + h * few : g * tile + (h + 1) * few] for g in range(G)], axis=0
+            )
+            p_hi, p_lo = halves(part)
+            all_three = dot(first_hi_ref[...], p_hi) + dot(first_hi_ref[...], p_lo) + dot(first_lo_ref[...], p_hi)
+            at = pl.ds(pl.multiple_of(r * tile + h * few, few), few)
+            for c in range(KEEP):
+                out_ref[c, at, :] = all_three[c * few : (c + 1) * few]
+        copy_out(r).start()
+        return carry
+
+    lax.fori_loop(0, tiles, over_rows, 0)
+    for r in range(tiles):
+        copy_out(r).wait()
 
 
 def share_kernel(
@@ -210,18 +203,27 @@
     lo_ref,
     source_ref,
     meta_ref,
-    fit_ref,
-    wide_ref,
+    fit_in,
+    wide_in,
     out_ref,
     known_ref,
     w1_ref,
     w23_ref,
     lead_ref,
-    v_ref,
+    along_ref,
     energy_ref,
+    fit_ref,
+    wide_ref,
     sems,
+    more_sems,
 ):
     tile = 16
+    tables_in = [
+        pltpu.make_async_copy(fit_in, fit_ref, more_sems.at[0]),
+        pltpu.make_async_copy(wide_in, wide_ref, more_sems.at[1]),
+    ]
+    for part in tables_in:
+        part.start()
 
     def copy(r):
         rows_r = pl.ds(pl.multiple_of(r * tile, tile), tile)
@@ -275,6 +277,8 @@
     shares = [-norm * of_small, -norm * of_large, jnp.where(lane == 0, -of_other, 0.0)]
     one, two, three = (known[p * number : (p + 1) * number] for p in range(3))
     cells = G * G
+    for part in tables_in:
+        part.wait()
     w1_ref[...] = jnp.broadcast_to(lane_sum(fit_ref[...] * one[0:1]), w1_ref.shape)
     ways = [wide_ref[p] for p in range(4)]
 
@@ -291,10 +295,8 @@
         copy(r).wait()
         rows_r = pl.ds(pl.multiple_of(r * tile, tile), tile)
         w23 = [w23_ref[rows_r, k * 128 : (k + 1) * 128] for k in range(lanes)]
-        thin = iota((tile, 128), 1)
-
-        def over_points(g, state):
-            v, lead = state
+
+        def over_points(g, lead):
             x = energy_ref[rows_r, pl.ds(pl.multiple_of(g * cells, cells), cells)].astype(F32)
             w1 = w1_ref[pl.ds(g, 1), :]
             fresh, along = [], None
@@ -303,11 +305,11 @@
                 fresh.append(lead[k] + w1 * part)
                 term = part * w23[k]
                 along = term if along is None else along + term
-            return v + jnp.where(thin == g, lane_sum(along), 0.0), tuple(fresh)
+            along_ref[g, rows_r, :] = along
+            return tuple(fresh)
 
         none = jnp.zeros((tile, 128), F32)
-        v, lead = lax.fori_loop(0, G, over_points, (none, (none,) * lanes), unroll=2)
-        v_ref[rows_r, :] = v
+        lead = lax.fori_loop(0, G, over_points, (none,) * lanes, unroll=8)
         for k in range(lanes):
             lead_ref[rows_r, k * 128 : (k + 1) * 128] = lead[k]
         return carry
@@ -322,7 +324,11 @@
         total = total + lax.dot_general(a_lo, hi, dims, preferred_element_type=F32)
         return jnp.concatenate([total, jnp.zeros((number, 96), F32)], axis=1)
 
-    field_first = dot_exact(v_ref[:, :G], fit_ref[...])
+    thin = iota((number, 128), 1)
+    v = jnp.zeros((number, 128), F32)
+    for g in range(G):
+        v = v + jnp.where(thin == g, lane_sum(along_ref[g]), 0.0)
+    field_first = dot_exact(v[:, :G], fit_ref[...])
     field_second = back(lead_ref[...] * w3, ways[0], ways[1])
     field_third = back(lead_ref[...] * w2, ways[2], ways[3])
     own = known[:rows]
@@ -372,8 +378,15 @@
     out_ref[...] = jnp.broadcast_to(total, out_ref.shape)
 
 
-def face_kernel(fit_ref, came_ref, known_ref, meta_ref, coef_ref, energy_ref):
+def face_kernel(far_ref, came_ref, known_ref, meta_ref, coef_ref, energy_ref, fit_ref, sems):
     number = fit_ref.shape[1]
+    some = 4
+    copies = [
+        pltpu.make_async_copy(far_ref.at[c : c + some], fit_ref.at[c : c + some], sems.at[c // some])
+        for c in range(0, KEEP, some)
+    ]
+    for copy in copies:
+        copy.start()
     place = meta_ref[:, 0:1]
     known = known_ref[...]
     one, two, three = (known[p * number : (p + 1) * number] for p in range(3))
@@ -397,6 +410,8 @@
     spaced = (lane & 15) == 0
     energy = jnp.zeros((number, 128), F32)
     for c in range(KEEP):
+        if c % some == 0:
+            copies[c // some].wait()
         along = jnp.zeros((number, 128), F32)
         for h in range(2):
             moved = pltpu.roll(first_pair[h], 128 - c, 1) if c else first_pair[h]
@@ -423,24 +438,47 @@
     out_ref[...] = dot_exact(total, integral_ref[...])
 
 
-def call(kernel, outs, *args, name, smem=(), apart=(), flops=0, scratch=(), room=VMEM_LIMIT):
-    vm = pl.BlockSpec(memory_space=pltpu.VMEM)
+def call(kernel, outs, *args, name, apart=(), fetched=(), outs_apart=False, flops=0, scratch=()):
     moved = sum(int(np.prod(a.shape)) * a.dtype.itemsize for a in args) + sum(
         int(np.prod(o.shape)) * o.dtype.itemsize for o in outs
     )
+    count = len(args) + len(outs) + len(scratch)
+
+    def fetching(*refs):
+        refs, held, sems = list(refs[:count]), refs[count:-1], refs[-1]
+        copies = [
+            pltpu.make_async_copy(refs[i], buffer, sems.at[k])
+            for k, (i, buffer) in enumerate(zip(fetched, held, strict=True))
+        ]
+        for copy in copies:
+            copy.start()
+        for copy in copies:
+            copy.wait()
+        for i, buffer in zip(fetched, held, strict=True):
+            refs[i] = buffer
+        kernel(*refs)
+
+    extra = []
+    if fetched:
+        extra = [pltpu.VMEM(args[i].shape, args[i].dtype) for i in fetched]
+        extra.append(pltpu.SemaphoreType.DMA((len(fetched),)))
+    outside = set(apart) | set(fetched)
     return pl.pallas_call(
-        kernel,
+        fetching if fetched else kernel,
         out_shape=outs,
         in_specs=[
-            pl.BlockSpec(memory_space=pltpu.SMEM if i in smem else pltpu.HBM if i in apart else pltpu.VMEM)
-            for i in range(len(args))
+            pl.BlockSpec(memory_space=pltpu.HBM if i in outside else pltpu.VMEM) for i in range(len(args))
         ],
-        out_specs=[vm] * len(outs),
-        scratch_shapes=list(scratch),
-        compiler_params=pltpu.CompilerParams(vmem_limit_bytes=room),
+        out_specs=[pl.BlockSpec(memory_space=pltpu.HBM if outs_apart else pltpu.VMEM)] * len(outs),
+        scratch_shapes=list(scratch) + extra,
+        compiler_params=pltpu.CompilerParams(vmem_limit_bytes=VMEM_LIMIT),
         cost_estimate=pl.CostEstimate(flops=flops, bytes_accessed=moved, transcendentals=0),
         name=name,
-    )(*args)
+    )(*(far(a) if i in outside else a for i, a in enumerate(args)))
+
+
+def far(a):
+    return pltpu.with_memory_space_constraint(a, pltpu.HBM)
 
 
 def shaped(shape, dtype=F32):
@@ -478,12 +516,20 @@
         single_surfaces,
         jnp.asarray(cos_wide),
         jnp.asarray(fit_wide),
+        fetched=tuple(range(7)),
         name="ask",
     )
     came = lax.all_to_all(send, "dev", 0, 0, tiled=True)
     table = shaped((pair_surfaces.shape[0], 512), BF16)
     table_hi, table_lo = call(
-        table_kernel, [table, table], pair_surfaces, hi, lo, name="table", flops=5 * 10**8
+        table_kernel,
+        [table, table],
+        pair_surfaces,
+        hi,
+        lo,
+        fetched=(0, 1, 2),
+        name="table",
+        flops=5 * 10**8,
     )
     each = 2 * capacity + 1
     answer, known = call(
@@ -496,40 +542,43 @@
         meta,
         jnp.asarray(fit_rows),
         wide,
-        apart=(3,),
-        room=LARGE_LIMIT,
+        apart=(3, 5, 6),
         name="share",
         flops=10**9,
         scratch=[
             pltpu.VMEM((G, 128), F32),
             pltpu.VMEM((number, G * G), F32),
             pltpu.VMEM((number, G * G), F32),
-            pltpu.VMEM((number, 128), F32),
+            pltpu.VMEM((G, number, 128), F32),
             pltpu.VMEM(energies.shape, BF16),
+            pltpu.VMEM(fit_rows.shape, F32),
+            pltpu.VMEM(wide.shape, BF16),
             pltpu.SemaphoreType.DMA((number // 16,)),
+            pltpu.SemaphoreType.DMA((2,)),
         ],
     )
     terms = lax.all_to_all(
         answer.reshape(devices, each, 1, 128), "dev", 0, 0, tiled=True
     ).reshape(devices * each, 128)
-    per = 4
+    first_hi, first_lo = (jnp.asarray(x) for x in halves_np(np.kron(FITTER, np.eye(8))))
     (fitted,) = call(
         fit_kernel,
-        [shaped((KEEP, number, KEEP**2))],
-        jnp.asarray(FITTER.astype(np.float32)),
+        [pltpu.HBM((KEEP, number, KEEP**2), F32)],
         energies,
         hi,
         lo,
+        first_hi,
+        first_lo,
+        apart=(0,),
+        outs_apart=True,
+        scratch=[
+            pltpu.VMEM(energies.shape, BF16),
+            pltpu.VMEM((KEEP, number, KEEP**2), F32),
+            pltpu.SemaphoreType.DMA((number // 32,)),
+            pltpu.SemaphoreType.DMA((number // 32,)),
+        ],
         name="fit",
         flops=5 * 10**9,
-        smem=(0,),
-        apart=(1,),
-        room=LARGE_LIMIT,
-        scratch=[
-            pltpu.VMEM((2, per, number, 256), F32),
-            pltpu.VMEM(energies.shape, BF16),
-            pltpu.SemaphoreType.DMA((G // (2 * per), 2)),
-        ],
     )
     (integral,) = call(
         unit_kernel, [shaped((128, S * S))], modals, jnp.asarray(cos_block), name="unit", flops=10**9
@@ -543,6 +592,8 @@
         terms,
         known,
         meta,
+        apart=(0,),
+        scratch=[pltpu.VMEM(fitted.shape, F32), pltpu.SemaphoreType.DMA((4,))],
         name="faces",
         flops=10**9,
     )

time: 79.9 us -> 64.1 us (0.80)
  local copies, waits for them, and re-layouts: 11.8 us -> 0.04 us
  Pallas kernels: 37.1 us -> 31.7 us
  waiting for transfers between devices: 4.91 us -> 6.64 us
    unnamed x36 -> x12, local copies, waits for them, and re-layouts: 11.8 us -> 0.04 us
    pallas_call x8, Pallas kernels: 37.1 us -> 31.7 us  [call(): pl.pallas_call(fetching if fetched else kernel, out_shape=outs, in_specs=...]
    all_to_all x1, waiting for transfers between devices: 4.61 us -> 6.38 us  [body(): came = lax.all_to_all(send, 'dev', 0, 0, tiled=True)]
  transfers between devices with their start and end apart: 3 -> 3, of which waited for: 2 -> 2; matrix products, arithmetic and copies ran while one was open for 0% -> 0% of each run, Pallas kernels for 19% -> 28%
where the time goes in v4:
time: 64.1 us; the launch traced here: 63.7 us
  Pallas kernels  31.7 us (49%)
  starting transfers between devices  24.6 us (38%)
  waiting for transfers between devices  6.64 us (10%)
  between operations  0.8 us (1%)
    pallas_call x8, Pallas kernels, call(): pl.pallas_call(fetching if fetched else kernel, out_shape=outs, in_specs=...  31.7 us
    all_to_all x1, starting transfers between devices, body(): came = lax.all_to_all(send, 'dev', 0, 0, tiled=True)  12 us
    all_to_all x1, starting transfers between devices, body(): lax.all_to_all(mine.reshape(groups, 1, 128), 'grp', 0, 0, tiled=True)  8.63 us
    all_to_all x1, waiting for transfers between devices, body(): came = lax.all_to_all(send, 'dev', 0, 0, tiled=True)  6.38 us
    all_to_all x1, starting transfers between devices, body(): lax.all_to_all(answer.reshape(devices, each, 1, 128), 'dev', 0, 0, tiled=...  3.9 us
  transfers between devices with their start and end apart: 3, of which 2 were waited for; matrix products, arithmetic and copies ran while one was open for 0% of the time, Pallas kernels for 28%

profile of v4, /device:TPU:1, one launch (start us, length us, event | category | flops | bytes accessed | tf_op | source)
XLA Modules:
  0.0 63.7 jit_solution(17623883157471336532)
XLA Ops:
  0.6 0.0 copy-start
  0.6 0.0 copy-start.1
  0.7 0.0 copy-start.5
  0.7 0.0 copy-start.3
  0.7 0.0 copy-start.4
  0.7 0.0 copy-start.2
  0.7 3.0 %ask.1 = (f32[32,2,128]{2,1,0:T(2,128)}, f32[384,128]{1,0:T(8,128)S(1)}) custom-call(s32[3,128]{1,0:T(4,128)} %bitcast.12, s32[114,114]{1,0:T(8,128)} %refs_1_.2, s32[1,114]{1,0:T(1,128)} %bitcast.13, f32[4,512]{1,0:T(4,128)} %modal_ref.1, f32[4,32]{1,0:T(4,128)} %refs_4_.1, f32[512,128]{1,0:T(8,128)} %constant.21.clone.refs_5_, ...), custom_call_target="tpu_custom_call" | custom-call | bytes 570584 | tf_op jit(solution)/shard_map/ask/pallas_call | solution.py:466
  3.7 12.0 %all-to-all-start = ((f32[32,2,128]{2,1,0:T(2,128)}), f32[32,2,128]{2,1,0:T(2,128)S(1)}, u32[]{:S(2)}, u32[]{:S(2)}) async-start(f32[32,2,128]{2,1,0:T(2,128)} %get-tuple-element.11), calls=%async_computation | async-start | bytes 65536 | tf_op jit(solution)/shard_map/all_to_all | solution.py:522
  15.8 2.4 %table.1 = (bf16[256,512]{1,0:T(8,128)(2,1)S(1)}, bf16[256,512]{1,0:T(8,128)(2,1)S(1)}) custom-call(f32[256,1024]{1,0:T(8,128)} %refs_0_.1, bf16[1024,256]{1,0:T(8,128)(2,1)} %constant.18.clone.hi_ref.refs_1_, bf16[1024,256]{1,0:T(8,128)(2,1)} %constant.19.clone.lo_ref.refs_2_), custom_call_target="tpu_custom_call" | custom-call | flops 500000000 | bytes 2621440 | tf_op jit(solution)/shard_map/table/pallas_call | solution.py:466
  18.2 6.4 %all-to-all-done.came_ref = f32[32,2,128]{2,1,0:T(2,128)S(1)} async-done(((f32[32,2,128]{2,1,0:T(2,128)}), f32[32,2,128]{2,1,0:T(2,128)S(1)}, u32[]{:S(2)}, u32[]{:S(2)}) %all-to-all-start) | async-done | bytes 32800 | tf_op jit(solution)/shard_map/all_to_all | solution.py:522
  24.5 9.5 %share.1 = (f32[800,128]{1,0:T(8,128)}, f32[384,128]{1,0:T(8,128)S(1)}) custom-call(f32[32,2,128]{2,1,0:T(2,128)S(1)} %all-to-all-done.came_ref, bf16[256,512]{1,0:T(8,128)(2,1)S(1)} %get-tuple-element.12.hi_ref, bf16[256,512]{1,0:T(8,128)(2,1)S(1)} %get-tuple-element.13.lo_ref, bf16[128,32768]{1,0:T(8,128)(2,1)} %source_ref.3, ...), custom_call_target="tpu_custom_call" | custom-call | flops 1000000000 | bytes 10027008 | tf_op jit(solution)/shard_map/share/pallas_call | solution.py:466
  34.0 3.9 %all-to-all-start.1 = ((f32[32,25,1,128]{3,2,1,0:T(1,128)}), f32[32,25,1,128]{3,2,1,0:T(1,128)S(1)}, u32[]{:S(2)}, u32[]{:S(2)}) async-start(f32[32,25,1,128]{3,2,1,0:T(1,128)} %bitcast.2), calls=%async_computation.1 | async-start | bytes 819200 | tf_op jit(solution)/shard_map/all_to_all | solution.py:560
  37.9 0.0 copy-done.5
  37.9 0.0 copy-done.2
  37.9 0.8 %unit.1.integral_ref = f32[128,256]{1,0:T(8,128)S(1)} custom-call(f32[4,512]{1,0:T(4,128)S(1)} %copy-done.2, f32[128,128]{1,0:T(8,128)S(1)} %copy-done.5), custom_call_target="tpu_custom_call" | custom-call | flops 1000000000 | bytes 204800 | tf_op jit(solution)/shard_map/unit/pallas_call | solution.py:466
  38.7 0.0 copy-done
  38.7 0.0 copy-done.1
  38.7 0.0 copy-done.3
  38.7 0.0 copy-done.4
  38.8 10.4 %fit.1.far_ref = f32[16,128,256]{2,1,0:T(8,128)} custom-call(bf16[128,32768]{1,0:T(8,128)(2,1)} %source_ref.3, bf16[1024,256]{1,0:T(8,128)(2,1)S(1)} %copy-done, bf16[1024,256]{1,0:T(8,128)(2,1)S(1)} %copy-done.1, bf16[128,256]{1,0:T(8,128)(2,1)S(1)} %copy-done.3, bf16[128,256]{1,0:T(8,128)(2,1)S(1)} %copy-done.4), custom_call_target="tpu_custom_call" | custom-call | flops 5000000000 | bytes 11665408 | tf_op jit(solution)/shard_map/fit/pallas_call | solution.py:466
  49.2 0.0 all-to-all-done.1
  49.2 0.6 own.1
  49.8 8.6 %all-to-all-start.2 = ((f32[8,1,128]{2,1,0:T(1,128)}), f32[8,1,128]{2,1,0:T(1,128)S(1)}, u32[]{:S(2)}, u32[]{:S(2)}) async-start(f32[8,1,128]{2,1,0:T(1,128)} %bitcast.6), calls=%async_computation.2 | async-start | bytes 8192 | tf_op jit(solution)/shard_map/all_to_all | solution.py:587
  58.4 4.2 %faces.1 = (bf16[128,4096]{1,0:T(8,128)(2,1)}, f32[1,128]{1,0:T(1,128)}) custom-call(f32[16,128,256]{2,1,0:T(8,128)} %fit.1.far_ref, f32[800,128]{1,0:T(8,128)S(1)} %bitcast.10, f32[384,128]{1,0:T(8,128)S(1)} %get-tuple-element.16.known_ref, f32[384,128]{1,0:T(8,128)S(1)} %get-tuple-element.14.meta_ref), custom_call_target="tpu_custom_call" | custom-call | flops 1000000000 | bytes 3949056 | tf_op jit(solution)/shard_map/faces/pallas_call | solution.py:466
  62.7 0.3 all-to-all-done.2
  62.9 0.8 %integrals.1 = f32[4,256]{1,0:T(4,128)} custom-call(f32[8,128]{1,0:T(8,128)S(1)} %bitcast.11, f32[128,256]{1,0:T(8,128)S(1)} %unit.1.integral_ref), custom_call_target="tpu_custom_call" | custom-call | bytes 139264 | tf_op jit(solution)/shard_map/integrals/pallas_call | solution.py:466
Async XLA Ops:
  0.6 38.1 %copy-start = (bf16[1024,256]{1,0:T(8,128)(2,1)S(1)}, bf16[1024,256]{1,0:T(8,128)(2,1)}, u32[]{:S(2)}) copy-start(bf16[1024,256]{1,0:T(8,128)(2,1)} %constant.18.clone.hi_ref.refs_1_) | copy-start | bytes 1572868
  0.6 38.1 %copy-start.1 = (bf16[1024,256]{1,0:T(8,128)(2,1)S(1)}, bf16[1024,256]{1,0:T(8,128)(2,1)}, u32[]{:S(2)}) copy-start(bf16[1024,256]{1,0:T(8,128)(2,1)} %constant.19.clone.lo_ref.refs_2_) | copy-start | bytes 1572868
  0.7 37.3 %copy-start.5 = (f32[128,128]{1,0:T(8,128)S(1)}, f32[128,128]{1,0:T(8,128)}, u32[]{:S(2)}) copy-start(f32[128,128]{1,0:T(8,128)} %constant.26.clone.cosine_ref) | copy-start | bytes 196612
  0.7 38.1 %copy-start.3 = (bf16[128,256]{1,0:T(8,128)(2,1)S(1)}, bf16[128,256]{1,0:T(8,128)(2,1)}, u32[]{:S(2)}) copy-start(bf16[128,256]{1,0:T(8,128)(2,1)} %constant.24.clone.first_hi_ref) | copy-start | bytes 196612
  0.7 38.1 %copy-start.4 = (bf16[128,256]{1,0:T(8,128)(2,1)S(1)}, bf16[128,256]{1,0:T(8,128)(2,1)}, u32[]{:S(2)}) copy-start(bf16[128,256]{1,0:T(8,128)(2,1)} %constant.25.clone.first_lo_ref) | copy-start | bytes 196612
  0.7 37.2 %copy-start.2 = (f32[4,512]{1,0:T(4,128)S(1)}, f32[4,512]{1,0:T(4,128)}, u32[]{:S(2)}) copy-start(f32[4,512]{1,0:T(4,128)} %modal_ref.1) | copy-start | bytes 24580
  3.7 20.8 %all-to-all-start = ((f32[32,2,128]{2,1,0:T(2,128)}), f32[32,2,128]{2,1,0:T(2,128)S(1)}, u32[]{:S(2)}, u32[]{:S(2)}) async-start(f32[32,2,128]{2,1,0:T(2,128)} %get-tuple-element.11), calls=%async_computation | async-start | bytes 65536 | tf_op jit(solution)/shard_map/all_to_all | solution.py:522
  34.0 15.2 %all-to-all-start.1 = ((f32[32,25,1,128]{3,2,1,0:T(1,128)}), f32[32,25,1,128]{3,2,1,0:T(1,128)S(1)}, u32[]{:S(2)}, u32[]{:S(2)}) async-start(f32[32,25,1,128]{3,2,1,0:T(1,128)} %bitcast.2), calls=%async_computation.1 | async-start | bytes 819200 | tf_op jit(solution)/shard_map/all_to_all | solution.py:560
  49.8 13.1 %all-to-all-start.2 = ((f32[8,1,128]{2,1,0:T(1,128)}), f32[8,1,128]{2,1,0:T(1,128)S(1)}, u32[]{:S(2)}, u32[]{:S(2)}) async-start(f32[8,1,128]{2,1,0:T(1,128)} %bitcast.6), calls=%async_computation.2 | async-start | bytes 8192 | tf_op jit(solution)/shard_map/all_to_all | solution.py:587

commit v5 on v4

--- a/solution.py
+++ b/solution.py
@@ -69,11 +69,6 @@
 
 def pick_two(pick, hi, lo):
     return dot(pick, hi) + dot(pick, lo)
-
-
-def place_of(slot):
-    home = jnp.floor((slot + 0.5) * 0.25)
-    return home, slot - 4.0 * home
 
 
 def ask_kernel(tri_ref, pair_ref, slot_ref, modal_ref, single_ref, cos_ref, fit_ref, out_ref, meta_ref):
@@ -93,7 +88,9 @@
     at = lane == upper
     owner = lane_sum(jnp.where(at, dot(pick, high), 0.0))
     local = lane_sum(jnp.where(at, dot(pick, low), 0.0))
-    slot = lane_sum(jnp.where(lane == each, slot_ref[...].astype(F32), 0.0))
+    slots = slot_ref[...]
+    slots = ((slots & 3) * 32 + (slots >> 2)).astype(F32)
+    slot = lane_sum(jnp.where(lane == each, slots, 0.0))
     wide = iota((rows, 128), 1)
     wide_f = wide.astype(F32)
     hit = wide_f == owner
@@ -124,7 +121,7 @@
     meta_ref[...] = jnp.where(wide == 0, owner * 25.0 + rank, jnp.where(wide == 1, slot, 0.0))
 
 
-def table_kernel(pair_ref, hi_ref, lo_ref, table_hi_ref, table_lo_ref):
+def table_kernel(pair_ref, hi_ref, lo_ref, modal_ref, cosine_ref, table_hi_ref, table_lo_ref, integral_ref):
     a_hi, a_lo = halves(pair_ref[...])
     k_hi, k_lo = hi_ref[...], lo_ref[...]
     terms = dot(a_hi, k_hi) + dot(a_hi, k_lo) + dot(a_lo, k_hi)
@@ -136,9 +133,6 @@
     table_lo_ref[:, :256] = t_lo
     table_hi_ref[:, 256:] = dot(t_hi, turn).astype(BF16)
     table_lo_ref[:, 256:] = dot(t_lo, turn).astype(BF16)
-
-
-def unit_kernel(modal_ref, cosine_ref, integral_ref):
     modal = modal_ref[...]
     own = modal.shape[0]
     row = iota((own * G, G * S), 0)
@@ -172,11 +166,16 @@
         rows = pl.ds(pl.multiple_of(r * tile, tile), tile)
         return pltpu.make_async_copy(out_ref.at[:, rows], far_ref.at[:, rows], out_sems.at[r])
 
-    for r in range(tiles):
+    for r in range(2):
         copy(r).start()
 
     def over_rows(r, carry):
         copy(r).wait()
+
+        @pl.when(r + 2 < tiles)
+        def _():
+            copy(r + 2).start()
+
         rows = pl.ds(pl.multiple_of(r * tile, tile), tile)
         stacked = jnp.concatenate([energy_ref[rows, g * cells : (g + 1) * cells] for g in range(G)], axis=0)
         two = dot(stacked, hi_ref[...]) + dot(stacked, lo_ref[...])
@@ -229,7 +228,8 @@
         rows_r = pl.ds(pl.multiple_of(r * tile, tile), tile)
         return pltpu.make_async_copy(source_ref.at[rows_r], energy_ref.at[rows_r], sems.at[r])
 
-    for r in range(energy_ref.shape[0] // tile):
+    tiles, ahead = energy_ref.shape[0] // tile, 4
+    for r in range(ahead):
         copy(r).start()
     peers = came_ref.shape[0]
     number = energy_ref.shape[0]
@@ -245,14 +245,14 @@
         lane_sum(jnp.where(off == 16.0 * k, seen, 0.0)) for k in (0, 2, 3, 4)
     )
     slot = jnp.concatenate([meta_ref[:, 1:2], small, large, other], axis=0)
-    home, sub = place_of(slot)
-    pick = one_hot(home, peers)
-    g_hi, g_lo = halves(came_ref[:, 0, :])
-    lane = iota((4 * rows, 128), 1)
-    known = pick_two(pick, g_hi, g_lo)
-    known = jnp.where((lane >> 5).astype(F32) == sub, known, 0.0)
-    known = known + pltpu.roll(known, 64, 1)
-    known = known + pltpu.roll(known, 32, 1)
+    pick = one_hot(slot, 128)
+    ground = came_ref[:, 0, :]
+    spots = 128 // peers
+    ground = jnp.concatenate([pltpu.roll(ground, 128 - 32 * j, 1) if j else ground for j in range(spots)], axis=0)
+    ground = jnp.where(iota((128, 128), 1) < 32, ground, 0.0)
+    ground = ground + pltpu.roll(ground, 32, 1)
+    ground = ground + pltpu.roll(ground, 64, 1)
+    known = pick_two(pick, *halves(ground))
     known_ref[...] = known[:rows]
     k, n = iota((128, 256), 0), iota((128, 256), 1)
     widen = (k == (n >> 4)).astype(F32).astype(BF16)
@@ -293,6 +293,11 @@
 
     def over_rows(r, carry):
         copy(r).wait()
+
+        @pl.when(r + ahead < tiles)
+        def _():
+            copy(r + ahead).start()
+
         rows_r = pl.ds(pl.multiple_of(r * tile, tile), tile)
         w23 = [w23_ref[rows_r, k * 128 : (k + 1) * 128] for k in range(lanes)]
 
@@ -314,7 +319,7 @@
             lead_ref[rows_r, k * 128 : (k + 1) * 128] = lead[k]
         return carry
 
-    lax.fori_loop(0, number // tile, over_rows, 0)
+    lax.fori_loop(0, tiles, over_rows, 0)
 
     def back(a, hi, lo):
         a_hi, a_lo = halves(a)
@@ -343,13 +348,13 @@
     from_grid = jnp.concatenate([field_first, field_second, field_third], axis=0)
     from_grid = from_grid - scale * single - jnp.where(lane == 0, shift, 0.0)
     fields = jnp.concatenate([from_grid] + shares, axis=0)
-    fields = fields + pltpu.roll(fields, 16, 1)
-    fields = fields + pltpu.roll(fields, 32, 1)
-    fields = jnp.where((iota(fields.shape, 1) >> 4).astype(F32) == sub, fields, 0.0)
     f_hi, f_lo = halves(fields)
     dims = (((0,), (0,)), ((), ()))
     part = lax.dot_general(pick, f_hi, dims, preferred_element_type=F32) + lax.dot_general(
         pick, f_lo, dims, preferred_element_type=F32
+    )
+    part = part[:peers] + sum(
+        pltpu.roll(part[j * peers : (j + 1) * peers], 16 * j, 1) for j in range(1, spots)
     )
     slots = out_ref.shape[0]
     each = float(slots // peers)
@@ -521,13 +526,15 @@
     )
     came = lax.all_to_all(send, "dev", 0, 0, tiled=True)
     table = shaped((pair_surfaces.shape[0], 512), BF16)
-    table_hi, table_lo = call(
+    table_hi, table_lo, integral = call(
         table_kernel,
-        [table, table],
+        [table, table, shaped((128, S * S))],
         pair_surfaces,
         hi,
         lo,
-        fetched=(0, 1, 2),
+        modals,
+        jnp.asarray(cos_block),
+        fetched=(0, 1, 2, 3, 4),
         name="table",
         flops=5 * 10**8,
     )
@@ -580,9 +587,6 @@
         name="fit",
         flops=5 * 10**9,
     )
-    (integral,) = call(
-        unit_kernel, [shaped((128, S * S))], modals, jnp.asarray(cos_block), name="unit", flops=10**9
-    )
     (mine,) = call(own_kernel, [shaped((groups, 128))], terms, name="own")
     parts = lax.all_to_all(mine.reshape(groups, 1, 128), "grp", 0, 0, tiled=True)
     coefficients, energy = call(

time: 64.1 us -> 63.1 us (0.984)
  Pallas kernels: 31.7 us -> 30.7 us
  starting transfers between devices: 24.6 us -> 25.3 us
  waiting for transfers between devices: 6.64 us -> 5.94 us
    pallas_call x8 -> x7, Pallas kernels: 31.7 us -> 30.7 us  [call(): pl.pallas_call(fetching if fetched else kernel, out_shape=outs, in_specs=...]
    all_to_all x1, waiting for transfers between devices: 6.38 us -> 5.5 us  [body(): came = lax.all_to_all(send, 'dev', 0, 0, tiled=True)]
    all_to_all x1, starting transfers between devices: 8.63 us -> 9.33 us  [body(): lax.all_to_all(mine.reshape(groups, 1, 128), 'grp', 0, 0, tiled=True)]
  transfers between devices with their start and end apart: 3 -> 3, of which waited for: 2 -> 3; matrix products, arithmetic and copies ran while one was open for 0% -> 0% of each run, Pallas kernels for 28% -> 29%
where the time goes in v5:
time: 63.1 us; the launch traced here: 62.7 us
  Pallas kernels  30.7 us (49%)
  starting transfers between devices  25.3 us (40%)
  waiting for transfers between devices  5.94 us (9%)
  between operations  0.75 us (1%)
    pallas_call x7, Pallas kernels, call(): pl.pallas_call(fetching if fetched else kernel, out_shape=outs, in_specs=...  30.7 us
    all_to_all x1, starting transfers between devices, body(): came = lax.all_to_all(send, 'dev', 0, 0, tiled=True)  12 us
    all_to_all x1, starting transfers between devices, body(): lax.all_to_all(mine.reshape(groups, 1, 128), 'grp', 0, 0, tiled=True)  9.33 us
    all_to_all x1, waiting for transfers between devices, body(): came = lax.all_to_all(send, 'dev', 0, 0, tiled=True)  5.5 us
    all_to_all x1, starting transfers between devices, body(): lax.all_to_all(answer.reshape(devices, each, 1, 128), 'dev', 0, 0, tiled=...  3.89 us
  transfers between devices with their start and end apart: 3, of which 3 were waited for; matrix products, arithmetic and copies ran while one was open for 0% of the time, Pallas kernels for 29%

profile of v5, /device:TPU:1, one launch (start us, length us, event | category | flops | bytes accessed | tf_op | source)
XLA Modules:
  0.0 62.7 jit_solution(7747732820664941407)
XLA Ops:
  0.6 0.0 copy-start
  0.6 0.0 copy-start.1
  0.7 0.0 copy-start.2
  0.7 0.0 copy-start.3
  0.7 3.0 %ask.1 = (f32[32,2,128]{2,1,0:T(2,128)}, f32[384,128]{1,0:T(8,128)S(1)}) custom-call(s32[3,128]{1,0:T(4,128)} %bitcast.12, s32[114,114]{1,0:T(8,128)} %refs_1_.2, s32[1,114]{1,0:T(1,128)} %bitcast.13, f32[4,512]{1,0:T(4,128)} %refs_3_.3, f32[4,32]{1,0:T(4,128)} %refs_4_.2, f32[512,128]{1,0:T(8,128)} %constant.21.clone.refs_5_, f32[32,128]{1,0:T(8,128)} %constant.22.clone.refs_6_), custom_call_target="tpu_custom_call" | custom-call | bytes 570584 | tf_op jit(solution)/shard_map/ask/pallas_call | solution.py:471
  3.7 12.0 %all-to-all-start = ((f32[32,2,128]{2,1,0:T(2,128)}), f32[32,2,128]{2,1,0:T(2,128)S(1)}, u32[]{:S(2)}, u32[]{:S(2)}) async-start(f32[32,2,128]{2,1,0:T(2,128)} %get-tuple-element.12), calls=%async_computation | async-start | bytes 65536 | tf_op jit(solution)/shard_map/all_to_all | solution.py:527
  15.8 3.3 %table.1 = (bf16[256,512]{1,0:T(8,128)(2,1)S(1)}, bf16[256,512]{1,0:T(8,128)(2,1)S(1)}, f32[128,256]{1,0:T(8,128)S(1)}) custom-call(f32[256,1024]{1,0:T(8,128)} %refs_0_.1, bf16[1024,256]{1,0:T(8,128)(2,1)} %constant.18.clone.hi_ref.refs_1_, bf16[1024,256]{1,0:T(8,128)(2,1)} %constant.19.clone.lo_ref.refs_2_, f32[4,512]{1,0:T(4,128)} %refs_3_.3, ...), custom_call_target="tpu_custom_call" | custom-call | flops 500000000 | bytes 2826240 | tf_op jit(solution)/shard_map/table/pallas_call | solution.py:471
  19.0 5.5 %all-to-all-done.came_ref = f32[32,2,128]{2,1,0:T(2,128)S(1)} async-done(((f32[32,2,128]{2,1,0:T(2,128)}), f32[32,2,128]{2,1,0:T(2,128)S(1)}, u32[]{:S(2)}, u32[]{:S(2)}) %all-to-all-start) | async-done | bytes 32800 | tf_op jit(solution)/shard_map/all_to_all | solution.py:527
  24.5 8.5 %share.1 = (f32[800,128]{1,0:T(8,128)}, f32[384,128]{1,0:T(8,128)S(1)}) custom-call(f32[32,2,128]{2,1,0:T(2,128)S(1)} %all-to-all-done.came_ref, bf16[256,512]{1,0:T(8,128)(2,1)S(1)} %get-tuple-element.13.hi_ref, bf16[256,512]{1,0:T(8,128)(2,1)S(1)} %get-tuple-element.14.lo_ref, bf16[128,32768]{1,0:T(8,128)(2,1)} %source_ref.3, ...), custom_call_target="tpu_custom_call" | custom-call | flops 1000000000 | bytes 10027008 | tf_op jit(solution)/shard_map/share/pallas_call | solution.py:471
  33.0 3.9 %all-to-all-start.1 = ((f32[32,25,1,128]{3,2,1,0:T(1,128)}), f32[32,25,1,128]{3,2,1,0:T(1,128)S(1)}, u32[]{:S(2)}, u32[]{:S(2)}) async-start(f32[32,25,1,128]{3,2,1,0:T(1,128)} %bitcast.2), calls=%async_computation.1 | async-start | bytes 819200 | tf_op jit(solution)/shard_map/all_to_all | solution.py:567
  36.9 0.0 copy-done
  36.9 0.0 copy-done.1
  36.9 0.0 copy-done.2
  36.9 0.0 copy-done.3
  37.0 10.4 %fit.1.far_ref = f32[16,128,256]{2,1,0:T(8,128)} custom-call(bf16[128,32768]{1,0:T(8,128)(2,1)} %source_ref.3, bf16[1024,256]{1,0:T(8,128)(2,1)S(1)} %copy-done.1, bf16[1024,256]{1,0:T(8,128)(2,1)S(1)} %copy-done, bf16[128,256]{1,0:T(8,128)(2,1)S(1)} %copy-done.3, bf16[128,256]{1,0:T(8,128)(2,1)S(1)} %copy-done.2), custom_call_target="tpu_custom_call" | custom-call | flops 5000000000 | bytes 11665408 | tf_op jit(solution)/shard_map/fit/pallas_call | solution.py:471
  47.3 0.2 all-to-all-done.1
  47.5 0.6 own.1
  48.1 9.3 %all-to-all-start.2 = ((f32[8,1,128]{2,1,0:T(1,128)}), f32[8,1,128]{2,1,0:T(1,128)S(1)}, u32[]{:S(2)}, u32[]{:S(2)}) async-start(f32[8,1,128]{2,1,0:T(1,128)} %bitcast.6), calls=%async_computation.2 | async-start | bytes 8192 | tf_op jit(solution)/shard_map/all_to_all | solution.py:591
  57.5 4.2 %faces.1 = (bf16[128,4096]{1,0:T(8,128)(2,1)}, f32[1,128]{1,0:T(1,128)}) custom-call(f32[16,128,256]{2,1,0:T(8,128)} %fit.1.far_ref, f32[800,128]{1,0:T(8,128)S(1)} %bitcast.10, f32[384,128]{1,0:T(8,128)S(1)} %get-tuple-element.17.known_ref, f32[384,128]{1,0:T(8,128)S(1)} %get-tuple-element.15.meta_ref), custom_call_target="tpu_custom_call" | custom-call | flops 1000000000 | bytes 3949056 | tf_op jit(solution)/shard_map/faces/pallas_call | solution.py:471
  61.7 0.3 all-to-all-done.2
  62.0 0.8 %integrals.1 = f32[4,256]{1,0:T(4,128)} custom-call(f32[8,128]{1,0:T(8,128)S(1)} %bitcast.11, f32[128,256]{1,0:T(8,128)S(1)} %get-tuple-element.20.integral_ref), custom_call_target="tpu_custom_call" | custom-call | bytes 139264 | tf_op jit(solution)/shard_map/integrals/pallas_call | solution.py:471
Async XLA Ops:
  0.6 36.3 %copy-start = (bf16[1024,256]{1,0:T(8,128)(2,1)S(1)}, bf16[1024,256]{1,0:T(8,128)(2,1)}, u32[]{:S(2)}) copy-start(bf16[1024,256]{1,0:T(8,128)(2,1)} %constant.19.clone.lo_ref.refs_2_) | copy-start | bytes 1572868
  0.6 36.3 %copy-start.1 = (bf16[1024,256]{1,0:T(8,128)(2,1)S(1)}, bf16[1024,256]{1,0:T(8,128)(2,1)}, u32[]{:S(2)}) copy-start(bf16[1024,256]{1,0:T(8,128)(2,1)} %constant.18.clone.hi_ref.refs_1_) | copy-start | bytes 1572868
  0.7 36.3 %copy-start.2 = (bf16[128,256]{1,0:T(8,128)(2,1)S(1)}, bf16[128,256]{1,0:T(8,128)(2,1)}, u32[]{:S(2)}) copy-start(bf16[128,256]{1,0:T(8,128)(2,1)} %constant.26.clone.first_lo_ref) | copy-start | bytes 196612
  0.7 36.3 %copy-start.3 = (bf16[128,256]{1,0:T(8,128)(2,1)S(1)}, bf16[128,256]{1,0:T(8,128)(2,1)}, u32[]{:S(2)}) copy-start(bf16[128,256]{1,0:T(8,128)(2,1)} %constant.25.clone.first_hi_ref) | copy-start | bytes 196612
  3.7 20.8 %all-to-all-start = ((f32[32,2,128]{2,1,0:T(2,128)}), f32[32,2,128]{2,1,0:T(2,128)S(1)}, u32[]{:S(2)}, u32[]{:S(2)}) async-start(f32[32,2,128]{2,1,0:T(2,128)} %get-tuple-element.12), calls=%async_computation | async-start | bytes 65536 | tf_op jit(solution)/shard_map/all_to_all | solution.py:527
  33.0 14.5 %all-to-all-start.1 = ((f32[32,25,1,128]{3,2,1,0:T(1,128)}), f32[32,25,1,128]{3,2,1,0:T(1,128)S(1)}, u32[]{:S(2)}, u32[]{:S(2)}) async-start(f32[32,25,1,128]{3,2,1,0:T(1,128)} %bitcast.2), calls=%async_computation.1 | async-start | bytes 819200 | tf_op jit(solution)/shard_map/all_to_all | solution.py:567
  48.1 13.8 %all-to-all-start.2 = ((f32[8,1,128]{2,1,0:T(1,128)}), f32[8,1,128]{2,1,0:T(1,128)S(1)}, u32[]{:S(2)}, u32[]{:S(2)}) async-start(f32[8,1,128]{2,1,0:T(1,128)} %bitcast.6), calls=%async_computation.2 | async-start | bytes 8192 | tf_op jit(solution)/shard_map/all_to_all | solution.py:591

commit v6 on v5

--- a/solution.py
+++ b/solution.py
@@ -121,7 +121,47 @@
     meta_ref[...] = jnp.where(wide == 0, owner * 25.0 + rank, jnp.where(wide == 1, slot, 0.0))
 
 
-def table_kernel(pair_ref, hi_ref, lo_ref, modal_ref, cosine_ref, table_hi_ref, table_lo_ref, integral_ref):
+FIT_TILE = 32
+
+
+def fit_some(energy_ref, hi_ref, lo_ref, first_ref, out_ref, start):
+    cells = G * G
+    few = 8
+    rows = pl.ds(pl.multiple_of(start, FIT_TILE), FIT_TILE)
+    stacked = jnp.concatenate([energy_ref[rows, g * cells : (g + 1) * cells] for g in range(G)], axis=0)
+    two = dot(stacked, hi_ref[...]) + dot(stacked, lo_ref[...])
+    half = first_ref.shape[0] // 2
+    for h in range(FIT_TILE // few):
+        at = h * few
+        part = jnp.concatenate(
+            [two[g * FIT_TILE + at : g * FIT_TILE + at + few] for g in range(G)], axis=0
+        )
+        p_hi, p_lo = halves(part)
+        large = dot(first_ref[...], p_hi)
+        all_three = large[:half] + large[half:] + dot(first_ref[:half], p_lo)
+        some = pl.ds(pl.multiple_of(start + at, few), few)
+        for c in range(KEEP):
+            out_ref[c, some, :] = all_three[c * few : (c + 1) * few]
+
+
+def table_kernel(
+    pair_ref,
+    hi_ref,
+    lo_ref,
+    modal_ref,
+    cosine_ref,
+    first_ref,
+    source_ref,
+    table_hi_ref,
+    table_lo_ref,
+    integral_ref,
+    far_ref,
+    energy_ref,
+    fit_ref,
+    sem,
+):
+    copy_in = pltpu.make_async_copy(source_ref.at[:FIT_TILE], energy_ref, sem)
+    copy_in.start()
     a_hi, a_lo = halves(pair_ref[...])
     k_hi, k_lo = hi_ref[...], lo_ref[...]
     terms = dot(a_hi, k_hi) + dot(a_hi, k_lo) + dot(a_lo, k_hi)
@@ -133,6 +173,10 @@
     table_lo_ref[:, :256] = t_lo
     table_hi_ref[:, 256:] = dot(t_hi, turn).astype(BF16)
     table_lo_ref[:, 256:] = dot(t_lo, turn).astype(BF16)
+    copy_in.wait()
+    fit_some(energy_ref, hi_ref, lo_ref, first_ref, fit_ref, 0)
+    copy_out = pltpu.make_async_copy(fit_ref, far_ref, sem)
+    copy_out.start()
     modal = modal_ref[...]
     own = modal.shape[0]
     row = iota((own * G, G * S), 0)
@@ -148,22 +192,20 @@
     left = dot(hi, to_left) + dot(lo, to_left)
     right = dot(hi, to_right) + dot(lo, to_right)
     integral_ref[...] = dot_exact(cosine_ref[...], left * right)
-
-
-def fit_kernel(
-    source_ref, hi_ref, lo_ref, first_hi_ref, first_lo_ref, far_ref, energy_ref, out_ref, sems, out_sems
-):
-    number = energy_ref.shape[0]
-    cells = G * G
-    tile, few = 32, 8
-    tiles = number // tile
+    copy_out.wait()
+
+
+def fit_kernel(source_ref, hi_ref, lo_ref, first_ref, far_ref, energy_ref, out_ref, sems, out_sems):
+    skipped = source_ref.shape[0] - energy_ref.shape[0]
+    tiles = energy_ref.shape[0] // FIT_TILE
 
     def copy(r):
-        rows = pl.ds(pl.multiple_of(r * tile, tile), tile)
-        return pltpu.make_async_copy(source_ref.at[rows], energy_ref.at[rows], sems.at[r])
+        rows = pl.ds(pl.multiple_of(r * FIT_TILE, FIT_TILE), FIT_TILE)
+        there = pl.ds(pl.multiple_of(skipped + r * FIT_TILE, FIT_TILE), FIT_TILE)
+        return pltpu.make_async_copy(source_ref.at[there], energy_ref.at[rows], sems.at[r])
 
     def copy_out(r):
-        rows = pl.ds(pl.multiple_of(r * tile, tile), tile)
+        rows = pl.ds(pl.multiple_of(r * FIT_TILE, FIT_TILE), FIT_TILE)
         return pltpu.make_async_copy(out_ref.at[:, rows], far_ref.at[:, rows], out_sems.at[r])
 
     for r in range(2):
@@ -176,18 +218,7 @@
         def _():
             copy(r + 2).start()
 
-        rows = pl.ds(pl.multiple_of(r * tile, tile), tile)
-        stacked = jnp.concatenate([energy_ref[rows, g * cells : (g + 1) * cells] for g in range(G)], axis=0)
-        two = dot(stacked, hi_ref[...]) + dot(stacked, lo_ref[...])
-        for h in range(tile // few):
-            part = jnp.concatenate(
-                [two[g * tile + h * few : g * tile + (h + 1) * few] for g in range(G)], axis=0
-            )
-            p_hi, p_lo = halves(part)
-            all_three = dot(first_hi_ref[...], p_hi) + dot(first_hi_ref[...], p_lo) + dot(first_lo_ref[...], p_hi)
-            at = pl.ds(pl.multiple_of(r * tile + h * few, few), few)
-            for c in range(KEEP):
-                out_ref[c, at, :] = all_three[c * few : (c + 1) * few]
+        fit_some(energy_ref, hi_ref, lo_ref, first_ref, out_ref, r * FIT_TILE)
         copy_out(r).start()
         return carry
 
@@ -310,7 +341,7 @@
                 fresh.append(lead[k] + w1 * part)
                 term = part * w23[k]
                 along = term if along is None else along + term
-            along_ref[g, rows_r, :] = along
+            along_ref[g] += along
             return tuple(fresh)
 
         none = jnp.zeros((tile, 128), F32)
@@ -319,6 +350,7 @@
             lead_ref[rows_r, k * 128 : (k + 1) * 128] = lead[k]
         return carry
 
+    along_ref[...] = jnp.zeros_like(along_ref)
     lax.fori_loop(0, tiles, over_rows, 0)
 
     def back(a, hi, lo):
@@ -329,11 +361,9 @@
         total = total + lax.dot_general(a_lo, hi, dims, preferred_element_type=F32)
         return jnp.concatenate([total, jnp.zeros((number, 96), F32)], axis=1)
 
-    thin = iota((number, 128), 1)
-    v = jnp.zeros((number, 128), F32)
-    for g in range(G):
-        v = v + jnp.where(thin == g, lane_sum(along_ref[g]), 0.0)
-    field_first = dot_exact(v[:, :G], fit_ref[...])
+    sums = lane_sum(jnp.sum(along_ref[...], axis=1))
+    field_first = jnp.sum(sums * fit_ref[...], axis=0, keepdims=True)
+    field_first = jnp.where(iota((number, 128), 0) == 0, field_first, 0.0)
     field_second = back(lead_ref[...] * w3, ways[0], ways[1])
     field_third = back(lead_ref[...] * w2, ways[2], ways[3])
     own = known[:rows]
@@ -383,15 +413,22 @@
     out_ref[...] = jnp.broadcast_to(total, out_ref.shape)
 
 
-def face_kernel(far_ref, came_ref, known_ref, meta_ref, coef_ref, energy_ref, fit_ref, sems):
+def face_kernel(near_in, far_in, came_ref, known_ref, meta_ref, coef_ref, energy_ref, fit_ref, sems):
     number = fit_ref.shape[1]
     some = 4
-    copies = [
-        pltpu.make_async_copy(far_ref.at[c : c + some], fit_ref.at[c : c + some], sems.at[c // some])
-        for c in range(0, KEEP, some)
-    ]
-    for copy in copies:
-        copy.start()
+    split = near_in.shape[1]
+    copies = []
+    for k in range(KEEP // some):
+        these = slice(k * some, (k + 1) * some)
+        copies.append(
+            (
+                pltpu.make_async_copy(near_in.at[these], fit_ref.at[these, :split], sems.at[k, 0]),
+                pltpu.make_async_copy(far_in.at[these], fit_ref.at[these, split:], sems.at[k, 1]),
+            )
+        )
+    for pair in copies:
+        for copy in pair:
+            copy.start()
     place = meta_ref[:, 0:1]
     known = known_ref[...]
     one, two, three = (known[p * number : (p + 1) * number] for p in range(3))
@@ -416,7 +453,8 @@
     energy = jnp.zeros((number, 128), F32)
     for c in range(KEEP):
         if c % some == 0:
-            copies[c // some].wait()
+            for copy in copies[c // some]:
+                copy.wait()
         along = jnp.zeros((number, 128), F32)
         for h in range(2):
             moved = pltpu.roll(first_pair[h], 128 - c, 1) if c else first_pair[h]
@@ -443,7 +481,7 @@
     out_ref[...] = dot_exact(total, integral_ref[...])
 
 
-def call(kernel, outs, *args, name, apart=(), fetched=(), outs_apart=False, flops=0, scratch=()):
+def call(kernel, outs, *args, name, apart=(), fetched=(), outs_apart=(), flops=0, scratch=()):
     moved = sum(int(np.prod(a.shape)) * a.dtype.itemsize for a in args) + sum(
         int(np.prod(o.shape)) * o.dtype.itemsize for o in outs
     )
@@ -474,7 +512,9 @@
         in_specs=[
             pl.BlockSpec(memory_space=pltpu.HBM if i in outside else pltpu.VMEM) for i in range(len(args))
         ],
-        out_specs=[pl.BlockSpec(memory_space=pltpu.HBM if outs_apart else pltpu.VMEM)] * len(outs),
+        out_specs=[
+            pl.BlockSpec(memory_space=pltpu.HBM if i in outs_apart else pltpu.VMEM) for i in range(len(outs))
+        ],
         scratch_shapes=list(scratch) + extra,
         compiler_params=pltpu.CompilerParams(vmem_limit_bytes=VMEM_LIMIT),
         cost_estimate=pl.CostEstimate(flops=flops, bytes_accessed=moved, transcendentals=0),
@@ -526,15 +566,26 @@
     )
     came = lax.all_to_all(send, "dev", 0, 0, tiled=True)
     table = shaped((pair_surfaces.shape[0], 512), BF16)
-    table_hi, table_lo, integral = call(
+    first_hi, first_lo = halves_np(np.kron(FITTER, np.eye(8)))
+    first = jnp.asarray(np.concatenate([first_hi, first_lo], axis=0))
+    table_hi, table_lo, integral, fitted_first = call(
         table_kernel,
-        [table, table, shaped((128, S * S))],
+        [table, table, shaped((128, S * S)), pltpu.HBM((KEEP, FIT_TILE, KEEP**2), F32)],
         pair_surfaces,
         hi,
         lo,
         modals,
         jnp.asarray(cos_block),
-        fetched=(0, 1, 2, 3, 4),
+        first,
+        energies,
+        fetched=(0, 1, 2, 3, 4, 5),
+        apart=(6,),
+        outs_apart=(3,),
+        scratch=[
+            pltpu.VMEM((FIT_TILE, G**3), BF16),
+            pltpu.VMEM((KEEP, FIT_TILE, KEEP**2), F32),
+            pltpu.SemaphoreType.DMA,
+        ],
         name="table",
         flops=5 * 10**8,
     )
@@ -556,7 +607,7 @@
             pltpu.VMEM((G, 128), F32),
             pltpu.VMEM((number, G * G), F32),
             pltpu.VMEM((number, G * G), F32),
-            pltpu.VMEM((G, number, 128), F32),
+            pltpu.VMEM((G, 16, 128), F32),
             pltpu.VMEM(energies.shape, BF16),
             pltpu.VMEM(fit_rows.shape, F32),
             pltpu.VMEM(wide.shape, BF16),
@@ -567,22 +618,21 @@
     terms = lax.all_to_all(
         answer.reshape(devices, each, 1, 128), "dev", 0, 0, tiled=True
     ).reshape(devices * each, 128)
-    first_hi, first_lo = (jnp.asarray(x) for x in halves_np(np.kron(FITTER, np.eye(8))))
-    (fitted,) = call(
+    others = number - FIT_TILE
+    (fitted_others,) = call(
         fit_kernel,
-        [pltpu.HBM((KEEP, number, KEEP**2), F32)],
+        [pltpu.HBM((KEEP, others, KEEP**2), F32)],
         energies,
         hi,
         lo,
-        first_hi,
-        first_lo,
+        first,
         apart=(0,),
-        outs_apart=True,
+        outs_apart=(0,),
         scratch=[
-            pltpu.VMEM(energies.shape, BF16),
-            pltpu.VMEM((KEEP, number, KEEP**2), F32),
-            pltpu.SemaphoreType.DMA((number // 32,)),
-            pltpu.SemaphoreType.DMA((number // 32,)),
+            pltpu.VMEM((others, G**3), BF16),
+            pltpu.VMEM((KEEP, others, KEEP**2), F32),
+            pltpu.SemaphoreType.DMA((others // FIT_TILE,)),
+            pltpu.SemaphoreType.DMA((others // FIT_TILE,)),
         ],
         name="fit",
         flops=5 * 10**9,
@@ -592,12 +642,13 @@
     coefficients, energy = call(
         face_kernel,
         [shaped((number, KEEP**3), BF16), shaped((1, number))],
-        fitted,
+        fitted_first,
+        fitted_others,
         terms,
         known,
         meta,
-        apart=(0,),
-        scratch=[pltpu.VMEM(fitted.shape, F32), pltpu.SemaphoreType.DMA((4,))],
+        apart=(0, 1),
+        scratch=[pltpu.VMEM((KEEP, number, KEEP**2), F32), pltpu.SemaphoreType.DMA((4, 2))],
         name="faces",
         flops=10**9,
     )

time: 63.1 us -> 65.7 us (1.041)
  starting transfers between devices: 25.3 us -> 28.4 us
  waiting for transfers between devices: 5.94 us -> 4.64 us
  Pallas kernels: 30.7 us -> 31.5 us
    all_to_all x1, waiting for transfers between devices: 5.5 us -> 1.99 us  [body(): came = lax.all_to_all(send, 'dev', 0, 0, tiled=True)]
    all_to_all x1, starting transfers between devices: 3.89 us -> 7.27 us  [body(): lax.all_to_all(answer.reshape(devices, each, 1, 128), 'dev', 0, 0, tiled=...]
    all_to_all x1, waiting for transfers between devices: 0.18 us -> 2.47 us  [body(): lax.all_to_all(answer.reshape(devices, each, 1, 128), 'dev', 0, 0, tiled=...]
    pallas_call x7, Pallas kernels: 30.7 us -> 31.5 us  [call(): pl.pallas_call(fetching if fetched else kernel, out_shape=outs, in_specs=...]
  transfers between devices with their start and end apart: 3 -> 3, of which waited for: 3 -> 3; matrix products, arithmetic and copies ran while one was open for 0% -> 0% of each run, Pallas kernels for 29% -> 30%
where the time goes in v6:
time: 65.7 us; the launch traced here: 65.3 us
  Pallas kernels  31.5 us (48%)
  starting transfers between devices  28.4 us (43%)
  waiting for transfers between devices  4.64 us (7%)
  between operations  0.74 us (1%)
    pallas_call x7, Pallas kernels, call(): pl.pallas_call(fetching if fetched else kernel, out_shape=outs, in_specs=...  31.5 us
    all_to_all x1, starting transfers between devices, body(): came = lax.all_to_all(send, 'dev', 0, 0, tiled=True)  12 us
    all_to_all x1, starting transfers between devices, body(): lax.all_to_all(mine.reshape(groups, 1, 128), 'grp', 0, 0, tiled=True)  9.06 us
    all_to_all x1, starting transfers between devices, body(): lax.all_to_all(answer.reshape(devices, each, 1, 128), 'dev', 0, 0, tiled=...  7.27 us
    all_to_all x1, waiting for transfers between devices, body(): lax.all_to_all(answer.reshape(devices, each, 1, 128), 'dev', 0, 0, tiled=...  2.47 us
    all_to_all x1, waiting for transfers between devices, body(): came = lax.all_to_all(send, 'dev', 0, 0, tiled=True)  1.99 us
  transfers between devices with their start and end apart: 3, of which 3 were waited for; matrix products, arithmetic and copies ran while one was open for 0% of the time, Pallas kernels for 30%

profile of v6, /device:TPU:1, one launch (start us, length us, event | category | flops | bytes accessed | tf_op | source)
XLA Modules:
  0.0 65.3 jit_solution(2056964583187858145)
XLA Ops:
  0.6 3.0 %ask.1 = (f32[32,2,128]{2,1,0:T(2,128)}, f32[384,128]{1,0:T(8,128)S(1)}) custom-call(s32[3,128]{1,0:T(4,128)} %bitcast.12, s32[114,114]{1,0:T(8,128)} %refs_1_.2, s32[1,114]{1,0:T(1,128)} %bitcast.13, f32[4,512]{1,0:T(4,128)} %refs_3_.3, f32[4,32]{1,0:T(4,128)} %refs_4_.2, f32[512,128]{1,0:T(8,128)} %constant.19.clone.refs_5_, f32[32,128]{1,0:T(8,128)} %constant.20.clone.refs_6_), custom_call_target="tpu_custom_call" | custom-call | bytes 570584 | tf_op jit(solution)/shard_map/ask/pallas_call | solution.py:509
  3.6 12.0 %all-to-all-start = ((f32[32,2,128]{2,1,0:T(2,128)}), f32[32,2,128]{2,1,0:T(2,128)S(1)}, u32[]{:S(2)}, u32[]{:S(2)}) async-start(f32[32,2,128]{2,1,0:T(2,128)} %get-tuple-element.14), calls=%async_computation | async-start | bytes 65536 | tf_op jit(solution)/shard_map/all_to_all | solution.py:567
  15.7 0.0 copy-start
  15.7 0.0 copy-start.1
  15.7 0.0 copy-start.2
  15.7 6.7 %table.1 = (bf16[256,512]{1,0:T(8,128)(2,1)S(1)}, bf16[256,512]{1,0:T(8,128)(2,1)S(1)}, f32[128,256]{1,0:T(8,128)S(1)}, f32[16,32,256]{2,1,0:T(8,128)}) custom-call(f32[256,1024]{1,0:T(8,128)} %refs_0_.1, bf16[1024,256]{1,0:T(8,128)(2,1)} %constant.16.clone.refs_1_.hi_ref, bf16[1024,256]{1,0:T(8,128)(2,1)} %constant.17.clone.refs_2_.lo_ref, ...), custom_call_target="tpu_custom_call" | custom-call | flops 500000000 | bytes 11870208 | tf_op jit(solution)/shard_map/table/pallas_call | solution.py:509
  22.4 2.0 %all-to-all-done.came_ref = f32[32,2,128]{2,1,0:T(2,128)S(1)} async-done(((f32[32,2,128]{2,1,0:T(2,128)}), f32[32,2,128]{2,1,0:T(2,128)S(1)}, u32[]{:S(2)}, u32[]{:S(2)}) %all-to-all-start) | async-done | bytes 32800 | tf_op jit(solution)/shard_map/all_to_all | solution.py:567
  24.4 7.8 %share.1 = (f32[800,128]{1,0:T(8,128)}, f32[384,128]{1,0:T(8,128)S(1)}) custom-call(f32[32,2,128]{2,1,0:T(2,128)S(1)} %all-to-all-done.came_ref, bf16[256,512]{1,0:T(8,128)(2,1)S(1)} %get-tuple-element.15.hi_ref, bf16[256,512]{1,0:T(8,128)(2,1)S(1)} %get-tuple-element.16.lo_ref, bf16[128,32768]{1,0:T(8,128)(2,1)} %source_ref.3, ...), custom_call_target="tpu_custom_call" | custom-call | flops 1000000000 | bytes 10027008 | tf_op jit(solution)/shard_map/share/pallas_call | solution.py:509
  32.2 7.3 %all-to-all-start.1 = ((f32[32,25,1,128]{3,2,1,0:T(1,128)}), f32[32,25,1,128]{3,2,1,0:T(1,128)S(1)}, u32[]{:S(2)}, u32[]{:S(2)}) async-start(f32[32,25,1,128]{3,2,1,0:T(1,128)} %bitcast.2), calls=%async_computation.1 | async-start | bytes 819200 | tf_op jit(solution)/shard_map/all_to_all | solution.py:618
  39.5 0.0 copy-done
  39.5 0.0 copy-done.1
  39.5 0.0 copy-done.2
  39.5 8.4 %fit.1.far_in = f32[16,96,256]{2,1,0:T(8,128)} custom-call(bf16[128,32768]{1,0:T(8,128)(2,1)} %source_ref.3, bf16[1024,256]{1,0:T(8,128)(2,1)S(1)} %copy-done.1, bf16[1024,256]{1,0:T(8,128)(2,1)S(1)} %copy-done, bf16[256,256]{1,0:T(8,128)(2,1)S(1)} %copy-done.2), custom_call_target="tpu_custom_call" | custom-call | flops 5000000000 | bytes 11141120 | tf_op jit(solution)/shard_map/fit/pallas_call | solution.py:509
  47.9 2.5 %all-to-all-done.1 = f32[32,25,1,128]{3,2,1,0:T(1,128)S(1)} async-done(((f32[32,25,1,128]{3,2,1,0:T(1,128)}), f32[32,25,1,128]{3,2,1,0:T(1,128)S(1)}, u32[]{:S(2)}, u32[]{:S(2)}) %all-to-all-start.1) | async-done | bytes 409632 | tf_op jit(solution)/shard_map/all_to_all | solution.py:618
  50.4 0.6 own.1
  51.0 9.1 %all-to-all-start.2 = ((f32[8,1,128]{2,1,0:T(1,128)}), f32[8,1,128]{2,1,0:T(1,128)S(1)}, u32[]{:S(2)}, u32[]{:S(2)}) async-start(f32[8,1,128]{2,1,0:T(1,128)} %bitcast.6), calls=%async_computation.2 | async-start | bytes 8192 | tf_op jit(solution)/shard_map/all_to_all | solution.py:641
  60.1 4.3 %faces.1 = (bf16[128,4096]{1,0:T(8,128)(2,1)}, f32[1,128]{1,0:T(1,128)}) custom-call(f32[16,32,256]{2,1,0:T(8,128)} %get-tuple-element.13.near_in, f32[16,96,256]{2,1,0:T(8,128)} %fit.1.far_in, f32[800,128]{1,0:T(8,128)S(1)} %bitcast.10, f32[384,128]{1,0:T(8,128)S(1)} %get-tuple-element.19.known_ref, f32[384,128]{1,0:T(8,128)S(1)} %get-tuple-element.17.meta_ref), custom_call_target="tpu_custom_call" | custom-call | flops 1000000000 | bytes 3949056 | tf_op jit(solution)/shard_map/faces/pallas_call | solution.py:509
  64.4 0.2 all-to-all-done.2
  64.5 0.8 %integrals.1 = f32[4,256]{1,0:T(4,128)} custom-call(f32[8,128]{1,0:T(8,128)S(1)} %bitcast.11, f32[128,256]{1,0:T(8,128)S(1)} %get-tuple-element.22.integral_ref), custom_call_target="tpu_custom_call" | custom-call | bytes 139264 | tf_op jit(solution)/shard_map/integrals/pallas_call | solution.py:509
Async XLA Ops:
  3.6 20.8 %all-to-all-start = ((f32[32,2,128]{2,1,0:T(2,128)}), f32[32,2,128]{2,1,0:T(2,128)S(1)}, u32[]{:S(2)}, u32[]{:S(2)}) async-start(f32[32,2,128]{2,1,0:T(2,128)} %get-tuple-element.14), calls=%async_computation | async-start | bytes 65536 | tf_op jit(solution)/shard_map/all_to_all | solution.py:567
  15.7 23.9 %copy-start = (bf16[1024,256]{1,0:T(8,128)(2,1)S(1)}, bf16[1024,256]{1,0:T(8,128)(2,1)}, u32[]{:S(2)}) copy-start(bf16[1024,256]{1,0:T(8,128)(2,1)} %constant.17.clone.refs_2_.lo_ref) | copy-start | bytes 1572868
  15.7 23.9 %copy-start.1 = (bf16[1024,256]{1,0:T(8,128)(2,1)S(1)}, bf16[1024,256]{1,0:T(8,128)(2,1)}, u32[]{:S(2)}) copy-start(bf16[1024,256]{1,0:T(8,128)(2,1)} %constant.16.clone.refs_1_.hi_ref) | copy-start | bytes 1572868
  15.7 23.9 %copy-start.2 = (bf16[256,256]{1,0:T(8,128)(2,1)S(1)}, bf16[256,256]{1,0:T(8,128)(2,1)}, u32[]{:S(2)}) copy-start(bf16[256,256]{1,0:T(8,128)(2,1)} %constant.21.clone.refs_5_.first_ref) | copy-start | bytes 393220
  32.2 18.2 %all-to-all-start.1 = ((f32[32,25,1,128]{3,2,1,0:T(1,128)}), f32[32,25,1,128]{3,2,1,0:T(1,128)S(1)}, u32[]{:S(2)}, u32[]{:S(2)}) async-start(f32[32,25,1,128]{3,2,1,0:T(1,128)} %bitcast.2), calls=%async_computation.1 | async-start | bytes 819200 | tf_op jit(solution)/shard_map/all_to_all | solution.py:618
  51.0 13.6 %all-to-all-start.2 = ((f32[8,1,128]{2,1,0:T(1,128)}), f32[8,1,128]{2,1,0:T(1,128)S(1)}, u32[]{:S(2)}, u32[]{:S(2)}) async-start(f32[8,1,128]{2,1,0:T(1,128)} %bitcast.6), calls=%async_computation.2 | async-start | bytes 8192 | tf_op jit(solution)/shard_map/all_to_all | solution.py:641

commit v7 on v6

--- a/solution.py
+++ b/solution.py
@@ -150,18 +150,10 @@
     lo_ref,
     modal_ref,
     cosine_ref,
-    first_ref,
-    source_ref,
     table_hi_ref,
     table_lo_ref,
     integral_ref,
-    far_ref,
-    energy_ref,
-    fit_ref,
-    sem,
 ):
-    copy_in = pltpu.make_async_copy(source_ref.at[:FIT_TILE], energy_ref, sem)
-    copy_in.start()
     a_hi, a_lo = halves(pair_ref[...])
     k_hi, k_lo = hi_ref[...], lo_ref[...]
     terms = dot(a_hi, k_hi) + dot(a_hi, k_lo) + dot(a_lo, k_hi)
@@ -173,10 +165,6 @@
     table_lo_ref[:, :256] = t_lo
     table_hi_ref[:, 256:] = dot(t_hi, turn).astype(BF16)
     table_lo_ref[:, 256:] = dot(t_lo, turn).astype(BF16)
-    copy_in.wait()
-    fit_some(energy_ref, hi_ref, lo_ref, first_ref, fit_ref, 0)
-    copy_out = pltpu.make_async_copy(fit_ref, far_ref, sem)
-    copy_out.start()
     modal = modal_ref[...]
     own = modal.shape[0]
     row = iota((own * G, G * S), 0)
@@ -192,17 +180,14 @@
     left = dot(hi, to_left) + dot(lo, to_left)
     right = dot(hi, to_right) + dot(lo, to_right)
     integral_ref[...] = dot_exact(cosine_ref[...], left * right)
-    copy_out.wait()
 
 
 def fit_kernel(source_ref, hi_ref, lo_ref, first_ref, far_ref, energy_ref, out_ref, sems, out_sems):
-    skipped = source_ref.shape[0] - energy_ref.shape[0]
     tiles = energy_ref.shape[0] // FIT_TILE
 
     def copy(r):
         rows = pl.ds(pl.multiple_of(r * FIT_TILE, FIT_TILE), FIT_TILE)
-        there = pl.ds(pl.multiple_of(skipped + r * FIT_TILE, FIT_TILE), FIT_TILE)
-        return pltpu.make_async_copy(source_ref.at[there], energy_ref.at[rows], sems.at[r])
+        return pltpu.make_async_copy(source_ref.at[rows], energy_ref.at[rows], sems.at[r])
 
     def copy_out(r):
         rows = pl.ds(pl.multiple_of(r * FIT_TILE, FIT_TILE), FIT_TILE)
@@ -409,26 +394,20 @@
     peers = came_ref.shape[0] // 25
     each = 25
     rows = came_ref[pl.ds(each - 1, peers, stride=each), :]
-    total = jnp.sum(rows, axis=0, keepdims=True)
-    out_ref[...] = jnp.broadcast_to(total, out_ref.shape)
-
-
-def face_kernel(near_in, far_in, came_ref, known_ref, meta_ref, coef_ref, energy_ref, fit_ref, sems):
+    out_ref[...] = jnp.sum(rows, axis=0, keepdims=True)
+
+
+def face_kernel(far_ref, came_ref, known_ref, meta_ref, far_out, energy_ref, fit_ref, coef_ref, sems, out_sems):
     number = fit_ref.shape[1]
     some = 4
-    split = near_in.shape[1]
-    copies = []
+    copies, leaving = [], []
     for k in range(KEEP // some):
         these = slice(k * some, (k + 1) * some)
-        copies.append(
-            (
-                pltpu.make_async_copy(near_in.at[these], fit_ref.at[these, :split], sems.at[k, 0]),
-                pltpu.make_async_copy(far_in.at[these], fit_ref.at[these, split:], sems.at[k, 1]),
-            )
-        )
-    for pair in copies:
-        for copy in pair:
-            copy.start()
+        copies.append(pltpu.make_async_copy(far_ref.at[these], fit_ref.at[these], sems.at[k]))
+        cols = slice(k * some * 256, (k + 1) * some * 256)
+        leaving.append(pltpu.make_async_copy(coef_ref.at[:, cols], far_out.at[:, cols], out_sems.at[k]))
+    for copy in copies:
+        copy.start()
     place = meta_ref[:, 0:1]
     known = known_ref[...]
     one, two, three = (known[p * number : (p + 1) * number] for p in range(3))
@@ -453,8 +432,7 @@
     energy = jnp.zeros((number, 128), F32)
     for c in range(KEEP):
         if c % some == 0:
-            for copy in copies[c // some]:
-                copy.wait()
+            copies[c // some].wait()
         along = jnp.zeros((number, 128), F32)
         for h in range(2):
             moved = pltpu.roll(first_pair[h], 128 - c, 1) if c else first_pair[h]
@@ -469,15 +447,22 @@
             coef_ref[:, c * 256 + h * 128 : c * 256 + (h + 1) * 128] = value.astype(BF16)
             along = along + value * both[h]
         energy = energy + one[:, c : c + 1] * along
+        if c % some == some - 1:
+            leaving[c // some].start()
     energy_ref[...] = lax.dot_general(
         jnp.full((8, 128), 1.0, F32), energy, (((1,), (1,)), ((), ())), preferred_element_type=F32, precision=HIGHEST
     )[0:1]
-
-
-def integral_kernel(parts_ref, integral_ref, out_ref):
-    total = jnp.sum(parts_ref[...], axis=0, keepdims=True)
+    for copy in leaving:
+        copy.wait()
+
+
+def integral_kernel(*refs):
+    *parts, integral_ref, out_ref = refs
+    parts = [p[...] for p in parts]
+    while len(parts) > 1:
+        parts = [parts[i] + parts[i + 1] for i in range(0, len(parts), 2)]
     shape = (out_ref.shape[0], 128)
-    total = jnp.where((iota(shape, 1) >> 4) == iota(shape, 0), total, 0.0)
+    total = jnp.where((iota(shape, 1) >> 4) == iota(shape, 0), parts[0], 0.0)
     out_ref[...] = dot_exact(total, integral_ref[...])
 
 
@@ -520,6 +505,10 @@
         cost_estimate=pl.CostEstimate(flops=flops, bytes_accessed=moved, transcendentals=0),
         name=name,
     )(*(far(a) if i in outside else a for i, a in enumerate(args)))
+
+
+def across(a, k):
+    return lax.ppermute(a, "grp", [(i, i ^ k) for i in range(lax.axis_size("grp"))])
 
 
 def far(a):
@@ -568,24 +557,15 @@
     table = shaped((pair_surfaces.shape[0], 512), BF16)
     first_hi, first_lo = halves_np(np.kron(FITTER, np.eye(8)))
     first = jnp.asarray(np.concatenate([first_hi, first_lo], axis=0))
-    table_hi, table_lo, integral, fitted_first = call(
+    table_hi, table_lo, integral = call(
         table_kernel,
-        [table, table, shaped((128, S * S)), pltpu.HBM((KEEP, FIT_TILE, KEEP**2), F32)],
+        [table, table, shaped((128, S * S))],
         pair_surfaces,
         hi,
         lo,
         modals,
         jnp.asarray(cos_block),
-        first,
-        energies,
-        fetched=(0, 1, 2, 3, 4, 5),
-        apart=(6,),
-        outs_apart=(3,),
-        scratch=[
-            pltpu.VMEM((FIT_TILE, G**3), BF16),
-            pltpu.VMEM((KEEP, FIT_TILE, KEEP**2), F32),
-            pltpu.SemaphoreType.DMA,
-        ],
+        fetched=(0, 1, 2, 3, 4),
         name="table",
         flops=5 * 10**8,
     )
@@ -618,10 +598,9 @@
     terms = lax.all_to_all(
         answer.reshape(devices, each, 1, 128), "dev", 0, 0, tiled=True
     ).reshape(devices * each, 128)
-    others = number - FIT_TILE
-    (fitted_others,) = call(
+    (fitted,) = call(
         fit_kernel,
-        [pltpu.HBM((KEEP, others, KEEP**2), F32)],
+        [pltpu.HBM((KEEP, number, KEEP**2), F32)],
         energies,
         hi,
         lo,
@@ -629,33 +608,41 @@
         apart=(0,),
         outs_apart=(0,),
         scratch=[
-            pltpu.VMEM((others, G**3), BF16),
-            pltpu.VMEM((KEEP, others, KEEP**2), F32),
-            pltpu.SemaphoreType.DMA((others // FIT_TILE,)),
-            pltpu.SemaphoreType.DMA((others // FIT_TILE,)),
+            pltpu.VMEM(energies.shape, BF16),
+            pltpu.VMEM((KEEP, number, KEEP**2), F32),
+            pltpu.SemaphoreType.DMA((number // FIT_TILE,)),
+            pltpu.SemaphoreType.DMA((number // FIT_TILE,)),
         ],
         name="fit",
         flops=5 * 10**9,
     )
-    (mine,) = call(own_kernel, [shaped((groups, 128))], terms, name="own")
-    parts = lax.all_to_all(mine.reshape(groups, 1, 128), "grp", 0, 0, tiled=True)
+    terms, fitted = lax.optimization_barrier((terms, fitted))
+    (mine,) = call(own_kernel, [shaped((1, 128))], terms, name="own")
+    mine = mine + across(mine, 1)
+    parts = [mine] + [across(mine, k) for k in range(2, groups, 2)]
+    mine, known = lax.optimization_barrier((mine, known))
     coefficients, energy = call(
         face_kernel,
-        [shaped((number, KEEP**3), BF16), shaped((1, number))],
-        fitted_first,
-        fitted_others,
+        [pltpu.HBM((number, KEEP**3), BF16), shaped((1, number))],
+        fitted,
         terms,
         known,
         meta,
-        apart=(0, 1),
-        scratch=[pltpu.VMEM((KEEP, number, KEEP**2), F32), pltpu.SemaphoreType.DMA((4, 2))],
+        apart=(0,),
+        outs_apart=(0,),
+        scratch=[
+            pltpu.VMEM((KEEP, number, KEEP**2), F32),
+            pltpu.VMEM((number, KEEP**3), BF16),
+            pltpu.SemaphoreType.DMA((4,)),
+            pltpu.SemaphoreType.DMA((4,)),
+        ],
         name="faces",
         flops=10**9,
     )
     (mean_field,) = call(
         integral_kernel,
         [shaped((own, S * S))],
-        parts.reshape(groups, 128),
+        *parts,
         integral,
         name="integrals",
     )

time: 65.7 us -> 62.3 us (0.948)
  starting transfers between devices: 28.4 us -> 24.8 us
  waiting for transfers between devices: 4.64 us -> 6.53 us
  Pallas kernels: 31.5 us -> 29.8 us
    all_to_all x1 -> x0, starting transfers between devices: 9.06 us -> none  [body(): lax.all_to_all(mine.reshape(groups, 1, 128), 'grp', 0, 0, tiled=True)]
    ppermute x0 -> x4, starting transfers between devices: none -> 8.89 us  [across(): lax.ppermute(a, 'grp', [(i, i ^ k) for i in range(lax.axis_size('grp'))])]
    all_to_all x1, waiting for transfers between devices: 1.99 us -> 5.5 us  [body(): came = lax.all_to_all(send, 'dev', 0, 0, tiled=True)]
    all_to_all x1, starting transfers between devices: 7.27 us -> 3.9 us  [body(): lax.all_to_all(answer.reshape(devices, each, 1, 128), 'dev', 0, 0, tiled=...]
    all_to_all x1, waiting for transfers between devices: 2.47 us -> 0.2 us  [body(): lax.all_to_all(answer.reshape(devices, each, 1, 128), 'dev', 0, 0, tiled=...]
    pallas_call x7, Pallas kernels: 31.5 us -> 29.8 us  [call(): pl.pallas_call(fetching if fetched else kernel, out_shape=outs, in_specs=...]
    ppermute x0 -> x4, waiting for transfers between devices: none -> 0.83 us  [across(): lax.ppermute(a, 'grp', [(i, i ^ k) for i in range(lax.axis_size('grp'))])]
  transfers between devices with their start and end apart: 3 -> 6, of which waited for: 3 -> 3; matrix products, arithmetic and copies ran while one was open for 0% -> 0% of each run, Pallas kernels for 30% -> 29%
where the time goes in v7:
time: 62.3 us; the launch traced here: 61.9 us
  Pallas kernels  29.8 us (48%)
  starting transfers between devices  24.8 us (40%)
  waiting for transfers between devices  6.53 us (10%)
  between operations  0.76 us (1%)
    pallas_call x7, Pallas kernels, call(): pl.pallas_call(fetching if fetched else kernel, out_shape=outs, in_specs=...  29.8 us
    all_to_all x1, starting transfers between devices, body(): came = lax.all_to_all(send, 'dev', 0, 0, tiled=True)  12 us
    ppermute x4, starting transfers between devices, across(): lax.ppermute(a, 'grp', [(i, i ^ k) for i in range(lax.axis_size('grp'))])  8.89 us
    all_to_all x1, waiting for transfers between devices, body(): came = lax.all_to_all(send, 'dev', 0, 0, tiled=True)  5.5 us
    all_to_all x1, starting transfers between devices, body(): lax.all_to_all(answer.reshape(devices, each, 1, 128), 'dev', 0, 0, tiled=...  3.9 us
  transfers between devices with their start and end apart: 6, of which 3 were waited for; matrix products, arithmetic and copies ran while one was open for 0% of the time, Pallas kernels for 29%

profile of v7, /device:TPU:1, one launch (start us, length us, event | category | flops | bytes accessed | tf_op | source)
XLA Modules:
  0.0 61.9 jit_solution(17083722100019080078)
XLA Ops:
  0.6 0.0 copy-start
  0.6 0.0 copy-start.1
  0.7 0.0 copy-start.2
  0.7 3.0 %ask.1 = (f32[32,2,128]{2,1,0:T(2,128)}, f32[384,128]{1,0:T(8,128)S(1)}) custom-call(s32[3,128]{1,0:T(4,128)} %bitcast.7, s32[114,114]{1,0:T(8,128)} %refs_1_.2, s32[1,114]{1,0:T(1,128)} %bitcast.8, f32[4,512]{1,0:T(4,128)} %refs_3_.3, f32[4,32]{1,0:T(4,128)} %refs_4_.2, f32[512,128]{1,0:T(8,128)} %constant.19.clone.refs_5_, f32[32,128]{1,0:T(8,128)} %constant.20.clone.refs_6_), custom_call_target="tpu_custom_call" | custom-call | bytes 570584 | tf_op jit(solution)/shard_map/ask/pallas_call | solution.py:494
  3.7 12.0 %all-to-all-start = ((f32[32,2,128]{2,1,0:T(2,128)}), f32[32,2,128]{2,1,0:T(2,128)S(1)}, u32[]{:S(2)}, u32[]{:S(2)}) async-start(f32[32,2,128]{2,1,0:T(2,128)} %get-tuple-element.15), calls=%async_computation | async-start | bytes 65536 | tf_op jit(solution)/shard_map/all_to_all | solution.py:556
  15.8 3.3 %table.1 = (bf16[256,512]{1,0:T(8,128)(2,1)S(1)}, bf16[256,512]{1,0:T(8,128)(2,1)S(1)}, f32[128,256]{1,0:T(8,128)S(1)}) custom-call(f32[256,1024]{1,0:T(8,128)} %refs_0_.1, bf16[1024,256]{1,0:T(8,128)(2,1)} %constant.16.clone.refs_1_.hi_ref, bf16[1024,256]{1,0:T(8,128)(2,1)} %constant.17.clone.refs_2_.lo_ref, f32[4,512]{1,0:T(4,128)} %refs_3_.3, ...), custom_call_target="tpu_custom_call" | custom-call | flops 500000000 | bytes 2826240 | tf_op jit(solution)/shard_map/table/pallas_call | solution.py:494
  19.0 5.5 %all-to-all-done.came_ref = f32[32,2,128]{2,1,0:T(2,128)S(1)} async-done(((f32[32,2,128]{2,1,0:T(2,128)}), f32[32,2,128]{2,1,0:T(2,128)S(1)}, u32[]{:S(2)}, u32[]{:S(2)}) %all-to-all-start) | async-done | bytes 32800 | tf_op jit(solution)/shard_map/all_to_all | solution.py:556
  24.5 7.8 %share.1 = (f32[800,128]{1,0:T(8,128)}, f32[384,128]{1,0:T(8,128)S(1)}) custom-call(f32[32,2,128]{2,1,0:T(2,128)S(1)} %all-to-all-done.came_ref, bf16[256,512]{1,0:T(8,128)(2,1)S(1)} %get-tuple-element.16.hi_ref, bf16[256,512]{1,0:T(8,128)(2,1)S(1)} %get-tuple-element.17.lo_ref, bf16[128,32768]{1,0:T(8,128)(2,1)} %source_ref.3, ...), custom_call_target="tpu_custom_call" | custom-call | flops 1000000000 | bytes 10027008 | tf_op jit(solution)/shard_map/share/pallas_call | solution.py:494
  32.4 3.9 %all-to-all-start.1 = ((f32[32,25,1,128]{3,2,1,0:T(1,128)}), f32[32,25,1,128]{3,2,1,0:T(1,128)S(1)}, u32[]{:S(2)}, u32[]{:S(2)}) async-start(f32[32,25,1,128]{3,2,1,0:T(1,128)} %bitcast.2), calls=%async_computation.1 | async-start | bytes 819200 | tf_op jit(solution)/shard_map/all_to_all | solution.py:598
  36.3 0.0 copy-done
  36.3 0.0 copy-done.1
  36.3 0.0 copy-done.2
  36.3 10.4 %fit.1.far_ref = f32[16,128,256]{2,1,0:T(8,128)} custom-call(bf16[128,32768]{1,0:T(8,128)(2,1)} %source_ref.3, bf16[1024,256]{1,0:T(8,128)(2,1)S(1)} %copy-done, bf16[1024,256]{1,0:T(8,128)(2,1)S(1)} %copy-done.1, bf16[256,256]{1,0:T(8,128)(2,1)S(1)} %copy-done.2), custom_call_target="tpu_custom_call" | custom-call | flops 5000000000 | bytes 11665408 | tf_op jit(solution)/shard_map/fit/pallas_call | solution.py:494
  46.7 0.2 all-to-all-done.1
  46.9 5.0 %collective-permute-start = (f32[1,128]{1,0:T(1,128)S(1)}, f32[1,128]{1,0:T(1,128)S(1)}, u32[]{:S(2)}, u32[]{:S(2)}) collective-permute-start(f32[1,128]{1,0:T(1,128)S(1)} %own.1), channel_id=1, source_target_pairs={{0,32},{32,0},{64,96},{96,64},{128,160},{160,128},{192,224},{224,1... | collective-permute-start | bytes 1544 | tf_op jit(solution)/shard_map/ppermute | solution.py:511
  51.9 0.8 %collective-permute-done = f32[1,128]{1,0:T(1,128)S(1)} collective-permute-done((f32[1,128]{1,0:T(1,128)S(1)}, f32[1,128]{1,0:T(1,128)S(1)}, u32[]{:S(2)}, u32[]{:S(2)}) %collective-permute-start) | collective-permute-done | bytes 544 | tf_op jit(solution)/shard_map/ppermute | solution.py:511
  52.7 1.2 %collective-permute-start.1 = (f32[1,128]{1,0:T(1,128)S(1)}, f32[1,128]{1,0:T(1,128)S(1)}, u32[]{:S(2)}, u32[]{:S(2)}) collective-permute-start(f32[1,128]{1,0:T(1,128)S(1)} %add.3.refs_0_), channel_id=1, source_target_pairs={{0,64},{32,96},{64,0},{96,32},{128,192},{160,224},{192,128},{224,1... | collective-permute-start | bytes 1544 | tf_op jit(solution)/shard_map/ppermute | solution.py:511
  53.9 2.4 %collective-permute-start.2 = (f32[1,128]{1,0:T(1,128)S(1)}, f32[1,128]{1,0:T(1,128)S(1)}, u32[]{:S(2)}, u32[]{:S(2)}) collective-permute-start(f32[1,128]{1,0:T(1,128)S(1)} %add.3.refs_0_), channel_id=1, source_target_pairs={{0,128},{32,160},{64,192},{96,224},{128,0},{160,32},{192,64},{224,... | collective-permute-start | bytes 1544 | tf_op jit(solution)/shard_map/ppermute | solution.py:511
  56.4 0.2 collective-permute-start.3
  56.6 4.5 %faces.1 = (bf16[128,4096]{1,0:T(8,128)(2,1)}, f32[1,128]{1,0:T(1,128)}) custom-call(f32[16,128,256]{2,1,0:T(8,128)} %fit.1.far_ref, f32[800,128]{1,0:T(8,128)S(1)} %bitcast.6, f32[384,128]{1,0:T(8,128)S(1)} %get-tuple-element.23.known_ref, f32[384,128]{1,0:T(8,128)S(1)} %get-tuple-element.18.meta_ref), custom_call_target="tpu_custom_call" | custom-call | flops 1000000000 | bytes 3949056 | tf_op jit(solution)/shard_map/faces/pallas_call | solution.py:494
  61.1 0.0 collective-permute-done.1.refs_1_
  61.1 0.0 collective-permute-done.2.refs_2_
  61.1 0.0 collective-permute-done.3.refs_3_
  61.1 0.8 %integrals.1 = f32[4,256]{1,0:T(4,128)} custom-call(f32[1,128]{1,0:T(1,128)S(1)} %add.3.refs_0_, f32[1,128]{1,0:T(1,128)S(1)} %collective-permute-done.1.refs_1_, f32[1,128]{1,0:T(1,128)S(1)} %collective-permute-done.2.refs_2_, f32[1,128]{1,0:T(1,128)S(1)} %collective-permute-done.3.refs_3_, f32[128,256]{1,0:T(8,128)S(1)} %get-tuple-element.26.refs_4_), custom_call_target="tpu_custom_call" | custom-call | bytes 137216 | tf_op jit(solution)/shard_map/integrals/pallas_call | solution.py:494
  (2 shorter events, 0.0 us)
Async XLA Ops:
  0.6 35.6 %copy-start = (bf16[1024,256]{1,0:T(8,128)(2,1)S(1)}, bf16[1024,256]{1,0:T(8,128)(2,1)}, u32[]{:S(2)}) copy-start(bf16[1024,256]{1,0:T(8,128)(2,1)} %constant.16.clone.refs_1_.hi_ref) | copy-start | bytes 1572868
  0.6 35.6 %copy-start.1 = (bf16[1024,256]{1,0:T(8,128)(2,1)S(1)}, bf16[1024,256]{1,0:T(8,128)(2,1)}, u32[]{:S(2)}) copy-start(bf16[1024,256]{1,0:T(8,128)(2,1)} %constant.17.clone.refs_2_.lo_ref) | copy-start | bytes 1572868
  0.7 35.6 %copy-start.2 = (bf16[256,256]{1,0:T(8,128)(2,1)S(1)}, bf16[256,256]{1,0:T(8,128)(2,1)}, u32[]{:S(2)}) copy-start(bf16[256,256]{1,0:T(8,128)(2,1)} %constant.21.clone.first_ref) | copy-start | bytes 393220
  3.7 20.8 %all-to-all-start = ((f32[32,2,128]{2,1,0:T(2,128)}), f32[32,2,128]{2,1,0:T(2,128)S(1)}, u32[]{:S(2)}, u32[]{:S(2)}) async-start(f32[32,2,128]{2,1,0:T(2,128)} %get-tuple-element.15), calls=%async_computation | async-start | bytes 65536 | tf_op jit(solution)/shard_map/all_to_all | solution.py:556
  32.4 14.5 %all-to-all-start.1 = ((f32[32,25,1,128]{3,2,1,0:T(1,128)}), f32[32,25,1,128]{3,2,1,0:T(1,128)S(1)}, u32[]{:S(2)}, u32[]{:S(2)}) async-start(f32[32,25,1,128]{3,2,1,0:T(1,128)} %bitcast.2), calls=%async_computation.1 | async-start | bytes 819200 | tf_op jit(solution)/shard_map/all_to_all | solution.py:598
  46.9 5.8 %collective-permute-start = (f32[1,128]{1,0:T(1,128)S(1)}, f32[1,128]{1,0:T(1,128)S(1)}, u32[]{:S(2)}, u32[]{:S(2)}) collective-permute-start(f32[1,128]{1,0:T(1,128)S(1)} %own.1), channel_id=1, source_target_pairs={{0,32},{32,0},{64,96},{96,64},{128,160},{160,128},{192,224},{224,1... | collective-permute-start | bytes 1544 | tf_op jit(solution)/shard_map/ppermute | solution.py:511
  52.7 8.4 %collective-permute-start.1 = (f32[1,128]{1,0:T(1,128)S(1)}, f32[1,128]{1,0:T(1,128)S(1)}, u32[]{:S(2)}, u32[]{:S(2)}) collective-permute-start(f32[1,128]{1,0:T(1,128)S(1)} %add.3.refs_0_), channel_id=1, source_target_pairs={{0,64},{32,96},{64,0},{96,32},{128,192},{160,224},{192,128},{224,1... | collective-permute-start | bytes 1544 | tf_op jit(solution)/shard_map/ppermute | solution.py:511
  53.9 7.2 %collective-permute-start.2 = (f32[1,128]{1,0:T(1,128)S(1)}, f32[1,128]{1,0:T(1,128)S(1)}, u32[]{:S(2)}, u32[]{:S(2)}) collective-permute-start(f32[1,128]{1,0:T(1,128)S(1)} %add.3.refs_0_), channel_id=1, source_target_pairs={{0,128},{32,160},{64,192},{96,224},{128,0},{160,32},{192,64},{224,... | collective-permute-start | bytes 1544 | tf_op jit(solution)/shard_map/ppermute | solution.py:511
  56.4 4.7 %collective-permute-start.3 = (f32[1,128]{1,0:T(1,128)S(1)}, f32[1,128]{1,0:T(1,128)S(1)}, u32[]{:S(2)}, u32[]{:S(2)}) collective-permute-start(f32[1,128]{1,0:T(1,128)S(1)} %add.3.refs_0_), channel_id=1, source_target_pairs={{0,192},{32,224},{64,128},{96,160},{128,64},{160,96},{192,0},{224,... | collective-permute-start | bytes 1544 | tf_op jit(solution)/shard_map/ppermute | solution.py:511

commit v8 on v7

--- a/solution.py
+++ b/solution.py
@@ -122,9 +122,10 @@
 
 
 FIT_TILE = 32
-
-
-def fit_some(energy_ref, hi_ref, lo_ref, first_ref, out_ref, start):
+NEAR = 10
+
+
+def fit_some(energy_ref, hi_ref, lo_ref, first_ref, out_refs, start):
     cells = G * G
     few = 8
     rows = pl.ds(pl.multiple_of(start, FIT_TILE), FIT_TILE)
@@ -141,7 +142,7 @@
         all_three = large[:half] + large[half:] + dot(first_ref[:half], p_lo)
         some = pl.ds(pl.multiple_of(start + at, few), few)
         for c in range(KEEP):
-            out_ref[c, some, :] = all_three[c * few : (c + 1) * few]
+            out_refs[c][some, :] = all_three[c * few : (c + 1) * few]
 
 
 def table_kernel(
@@ -182,8 +183,11 @@
     integral_ref[...] = dot_exact(cosine_ref[...], left * right)
 
 
-def fit_kernel(source_ref, hi_ref, lo_ref, first_ref, far_ref, energy_ref, out_ref, sems, out_sems):
+def fit_kernel(source_ref, hi_ref, lo_ref, first_ref, *refs):
+    near_refs = list(refs[:NEAR])
+    far_ref, energy_ref, rest_ref, sems, out_sems = refs[NEAR:]
     tiles = energy_ref.shape[0] // FIT_TILE
+    out_refs = near_refs + [rest_ref.at[c] for c in range(KEEP - NEAR)]
 
     def copy(r):
         rows = pl.ds(pl.multiple_of(r * FIT_TILE, FIT_TILE), FIT_TILE)
@@ -191,7 +195,7 @@
 
     def copy_out(r):
         rows = pl.ds(pl.multiple_of(r * FIT_TILE, FIT_TILE), FIT_TILE)
-        return pltpu.make_async_copy(out_ref.at[:, rows], far_ref.at[:, rows], out_sems.at[r])
+        return pltpu.make_async_copy(rest_ref.at[:, rows], far_ref.at[:, rows], out_sems.at[r])
 
     for r in range(2):
         copy(r).start()
@@ -203,7 +207,7 @@
         def _():
             copy(r + 2).start()
 
-        fit_some(energy_ref, hi_ref, lo_ref, first_ref, out_ref, r * FIT_TILE)
+        fit_some(energy_ref, hi_ref, lo_ref, first_ref, out_refs, r * FIT_TILE)
         copy_out(r).start()
         return carry
 
@@ -397,17 +401,17 @@
     out_ref[...] = jnp.sum(rows, axis=0, keepdims=True)
 
 
-def face_kernel(far_ref, came_ref, known_ref, meta_ref, far_out, energy_ref, fit_ref, coef_ref, sems, out_sems):
-    number = fit_ref.shape[1]
+def face_kernel(*refs):
+    far_ref, came_ref, known_ref, meta_ref, far_out, energy_ref, coef_ref, rest_ref, out_sems, sem = refs[NEAR:]
+    fit_refs = list(refs[:NEAR]) + [rest_ref.at[c] for c in range(KEEP - NEAR)]
+    coming = pltpu.make_async_copy(far_ref, rest_ref, sem)
+    coming.start()
+    number = coef_ref.shape[0]
     some = 4
-    copies, leaving = [], []
+    leaving = []
     for k in range(KEEP // some):
-        these = slice(k * some, (k + 1) * some)
-        copies.append(pltpu.make_async_copy(far_ref.at[these], fit_ref.at[these], sems.at[k]))
         cols = slice(k * some * 256, (k + 1) * some * 256)
         leaving.append(pltpu.make_async_copy(coef_ref.at[:, cols], far_out.at[:, cols], out_sems.at[k]))
-    for copy in copies:
-        copy.start()
     place = meta_ref[:, 0:1]
     known = known_ref[...]
     one, two, three = (known[p * number : (p + 1) * number] for p in range(3))
@@ -431,12 +435,12 @@
     spaced = (lane & 15) == 0
     energy = jnp.zeros((number, 128), F32)
     for c in range(KEEP):
-        if c % some == 0:
-            copies[c // some].wait()
+        if c == NEAR:
+            coming.wait()
         along = jnp.zeros((number, 128), F32)
         for h in range(2):
             moved = pltpu.roll(first_pair[h], 128 - c, 1) if c else first_pair[h]
-            value = fit_ref[c, :, h * 128 : (h + 1) * 128] - jnp.where(spaced, moved, 0.0)
+            value = fit_refs[c][:, h * 128 : (h + 1) * 128] - jnp.where(spaced, moved, 0.0)
             if h == 0:
                 shift = (c % 8) * 16
                 moved = second_pair[c // 8]
@@ -598,18 +602,19 @@
     terms = lax.all_to_all(
         answer.reshape(devices, each, 1, 128), "dev", 0, 0, tiled=True
     ).reshape(devices * each, 128)
-    (fitted,) = call(
+    far_part = (KEEP - NEAR, number, KEEP**2)
+    fitted = call(
         fit_kernel,
-        [pltpu.HBM((KEEP, number, KEEP**2), F32)],
+        [shaped((number, KEEP**2))] * NEAR + [pltpu.HBM(far_part, F32)],
         energies,
         hi,
         lo,
         first,
         apart=(0,),
-        outs_apart=(0,),
+        outs_apart=(NEAR,),
         scratch=[
             pltpu.VMEM(energies.shape, BF16),
-            pltpu.VMEM((KEEP, number, KEEP**2), F32),
+            pltpu.VMEM(far_part, F32),
             pltpu.SemaphoreType.DMA((number // FIT_TILE,)),
             pltpu.SemaphoreType.DMA((number // FIT_TILE,)),
         ],
@@ -624,17 +629,17 @@
     coefficients, energy = call(
         face_kernel,
         [pltpu.HBM((number, KEEP**3), BF16), shaped((1, number))],
-        fitted,
+        *fitted,
         terms,
         known,
         meta,
-        apart=(0,),
+        apart=(NEAR,),
         outs_apart=(0,),
         scratch=[
-            pltpu.VMEM((KEEP, number, KEEP**2), F32),
             pltpu.VMEM((number, KEEP**3), BF16),
+            pltpu.VMEM(far_part, F32),
             pltpu.SemaphoreType.DMA((4,)),
-            pltpu.SemaphoreType.DMA((4,)),
+            pltpu.SemaphoreType.DMA,
         ],
         name="faces",
         flops=10**9,

time: 62.3 us -> 62.1 us (level)
  no operation moved by 1% of the time
where the time goes in v8:
time: 62.1 us; the launch traced here: 61.6 us
  Pallas kernels  29.3 us (47%)
  starting transfers between devices  24.8 us (40%)
  waiting for transfers between devices  6.67 us (11%)
  between operations  0.76 us (1%)
    pallas_call x7, Pallas kernels, call(): pl.pallas_call(fetching if fetched else kernel, out_shape=outs, in_specs=...  29.3 us
    all_to_all x1, starting transfers between devices, body(): came = lax.all_to_all(send, 'dev', 0, 0, tiled=True)  12 us
    ppermute x4, starting transfers between devices, across(): lax.ppermute(a, 'grp', [(i, i ^ k) for i in range(lax.axis_size('grp'))])  8.89 us
    all_to_all x1, waiting for transfers between devices, body(): came = lax.all_to_all(send, 'dev', 0, 0, tiled=True)  5.5 us
    all_to_all x1, starting transfers between devices, body(): lax.all_to_all(answer.reshape(devices, each, 1, 128), 'dev', 0, 0, tiled=...  3.9 us
  transfers between devices with their start and end apart: 6, of which 3 were waited for; matrix products, arithmetic and copies ran while one was open for 0% of the time, Pallas kernels for 29%

profile of v8, /device:TPU:1, one launch (start us, length us, event | category | flops | bytes accessed | tf_op | source)
XLA Modules:
  0.0 61.6 jit_solution(8341226072219487679)
XLA Ops:
  0.6 0.0 copy-start
  0.6 0.0 copy-start.1
  0.7 0.0 copy-start.2
  0.7 3.0 %ask.1 = (f32[32,2,128]{2,1,0:T(2,128)}, f32[384,128]{1,0:T(8,128)S(1)}) custom-call(s32[3,128]{1,0:T(4,128)} %bitcast.7, s32[114,114]{1,0:T(8,128)} %refs_1_.2, s32[1,114]{1,0:T(1,128)} %bitcast.8, f32[4,512]{1,0:T(4,128)} %refs_3_.3, f32[4,32]{1,0:T(4,128)} %refs_4_.2, f32[512,128]{1,0:T(8,128)} %constant.19.clone.refs_5_, f32[32,128]{1,0:T(8,128)} %constant.20.clone.refs_6_), custom_call_target="tpu_custom_call" | custom-call | bytes 570584 | tf_op jit(solution)/shard_map/ask/pallas_call | solution.py:498
  3.7 12.0 %all-to-all-start = ((f32[32,2,128]{2,1,0:T(2,128)}), f32[32,2,128]{2,1,0:T(2,128)S(1)}, u32[]{:S(2)}, u32[]{:S(2)}) async-start(f32[32,2,128]{2,1,0:T(2,128)} %get-tuple-element.36), calls=%async_computation | async-start | bytes 65536 | tf_op jit(solution)/shard_map/all_to_all | solution.py:560
  15.8 3.3 %table.1 = (bf16[256,512]{1,0:T(8,128)(2,1)S(1)}, bf16[256,512]{1,0:T(8,128)(2,1)S(1)}, f32[128,256]{1,0:T(8,128)S(1)}) custom-call(f32[256,1024]{1,0:T(8,128)} %refs_0_.1, bf16[1024,256]{1,0:T(8,128)(2,1)} %constant.16.clone.refs_1_.hi_ref, bf16[1024,256]{1,0:T(8,128)(2,1)} %constant.17.clone.refs_2_.lo_ref, f32[4,512]{1,0:T(4,128)} %refs_3_.3, ...), custom_call_target="tpu_custom_call" | custom-call | flops 500000000 | bytes 2826240 | tf_op jit(solution)/shard_map/table/pallas_call | solution.py:498
  19.0 5.5 %all-to-all-done.came_ref = f32[32,2,128]{2,1,0:T(2,128)S(1)} async-done(((f32[32,2,128]{2,1,0:T(2,128)}), f32[32,2,128]{2,1,0:T(2,128)S(1)}, u32[]{:S(2)}, u32[]{:S(2)}) %all-to-all-start) | async-done | bytes 32800 | tf_op jit(solution)/shard_map/all_to_all | solution.py:560
  24.5 7.8 %share.1 = (f32[800,128]{1,0:T(8,128)}, f32[384,128]{1,0:T(8,128)S(1)}) custom-call(f32[32,2,128]{2,1,0:T(2,128)S(1)} %all-to-all-done.came_ref, bf16[256,512]{1,0:T(8,128)(2,1)S(1)} %get-tuple-element.37.hi_ref, bf16[256,512]{1,0:T(8,128)(2,1)S(1)} %get-tuple-element.38.lo_ref, bf16[128,32768]{1,0:T(8,128)(2,1)} %source_ref.3, ...), custom_call_target="tpu_custom_call" | custom-call | flops 1000000000 | bytes 10027008 | tf_op jit(solution)/shard_map/share/pallas_call | solution.py:498
  32.4 3.9 %all-to-all-start.1 = ((f32[32,25,1,128]{3,2,1,0:T(1,128)}), f32[32,25,1,128]{3,2,1,0:T(1,128)S(1)}, u32[]{:S(2)}, u32[]{:S(2)}) async-start(f32[32,25,1,128]{3,2,1,0:T(1,128)} %bitcast.2), calls=%async_computation.1 | async-start | bytes 819200 | tf_op jit(solution)/shard_map/all_to_all | solution.py:602
  36.3 0.0 copy-done
  36.3 0.0 copy-done.1
  36.3 0.0 copy-done.2
  36.3 10.2 %fit.1 = (f32[128,256]{1,0:T(8,128)S(1)}, f32[128,256]{1,0:T(8,128)S(1)}, f32[128,256]{1,0:T(8,128)S(1)}, f32[128,256]{1,0:T(8,128)S(1)}, f32[128,256]{1,0:T(8,1...) custom-call(bf16[128,32768]{1,0:T(8,128)(2,1)} %source_ref.3, ...), custom_call_target="tpu_custom_call" | custom-call | flops 5000000000 | bytes 11665408 | tf_op jit(solution)/shard_map/fit/pallas_call | solution.py:498
  46.5 0.3 all-to-all-done.1
  46.9 5.0 %collective-permute-start = (f32[1,128]{1,0:T(1,128)S(1)}, f32[1,128]{1,0:T(1,128)S(1)}, u32[]{:S(2)}, u32[]{:S(2)}) collective-permute-start(f32[1,128]{1,0:T(1,128)S(1)} %own.1), channel_id=1, source_target_pairs={{0,32},{32,0},{64,96},{96,64},{128,160},{160,128},{192,224},{224,1... | collective-permute-start | bytes 1544 | tf_op jit(solution)/shard_map/ppermute | solution.py:515
  51.9 0.8 %collective-permute-done = f32[1,128]{1,0:T(1,128)S(1)} collective-permute-done((f32[1,128]{1,0:T(1,128)S(1)}, f32[1,128]{1,0:T(1,128)S(1)}, u32[]{:S(2)}, u32[]{:S(2)}) %collective-permute-start) | collective-permute-done | bytes 544 | tf_op jit(solution)/shard_map/ppermute | solution.py:515
  52.7 1.2 %collective-permute-start.1 = (f32[1,128]{1,0:T(1,128)S(1)}, f32[1,128]{1,0:T(1,128)S(1)}, u32[]{:S(2)}, u32[]{:S(2)}) collective-permute-start(f32[1,128]{1,0:T(1,128)S(1)} %add.3.refs_0_), channel_id=1, source_target_pairs={{0,64},{32,96},{64,0},{96,32},{128,192},{160,224},{192,128},{224,1... | collective-permute-start | bytes 1544 | tf_op jit(solution)/shard_map/ppermute | solution.py:515
  53.9 2.4 %collective-permute-start.2 = (f32[1,128]{1,0:T(1,128)S(1)}, f32[1,128]{1,0:T(1,128)S(1)}, u32[]{:S(2)}, u32[]{:S(2)}) collective-permute-start(f32[1,128]{1,0:T(1,128)S(1)} %add.3.refs_0_), channel_id=1, source_target_pairs={{0,128},{32,160},{64,192},{96,224},{128,0},{160,32},{192,64},{224,... | collective-permute-start | bytes 1544 | tf_op jit(solution)/shard_map/ppermute | solution.py:515
  56.4 0.2 collective-permute-start.3
  56.6 4.2 %faces.1 = (bf16[128,4096]{1,0:T(8,128)(2,1)}, f32[1,128]{1,0:T(1,128)}) custom-call(f32[128,256]{1,0:T(8,128)S(1)} %get-tuple-element.52.refs_0_, f32[128,256]{1,0:T(8,128)S(1)} %get-tuple-element.53.refs_1_, f32[128,256]{1,0:T(8,128)S(1)} %get-tuple-element.54.refs_2_, f32[128,256]{1,0:T(8,128)S(1)} %get-tuple-element.55.refs_3_, ...), custom_call_target="tpu_custom_call" | custom-call | flops 1000000000 | bytes 3949056 | tf_op jit(solution)/shard_map/faces/pallas_call | solution.py:498
  60.8 0.0 collective-permute-done.1.refs_1_
  60.9 0.0 collective-permute-done.2.refs_2_
  60.9 0.0 collective-permute-done.3.refs_3_
  60.9 0.8 %integrals.1 = f32[4,256]{1,0:T(4,128)} custom-call(f32[1,128]{1,0:T(1,128)S(1)} %add.3.refs_0_, f32[1,128]{1,0:T(1,128)S(1)} %collective-permute-done.1.refs_1_, f32[1,128]{1,0:T(1,128)S(1)} %collective-permute-done.2.refs_2_, f32[1,128]{1,0:T(1,128)S(1)} %collective-permute-done.3.refs_3_, f32[128,256]{1,0:T(8,128)S(1)} %get-tuple-element.68.refs_4_), custom_call_target="tpu_custom_call" | custom-call | bytes 137216 | tf_op jit(solution)/shard_map/integrals/pallas_call | solution.py:498
  (2 shorter events, 0.0 us)
Async XLA Ops:
  0.6 35.6 %copy-start = (bf16[1024,256]{1,0:T(8,128)(2,1)S(1)}, bf16[1024,256]{1,0:T(8,128)(2,1)}, u32[]{:S(2)}) copy-start(bf16[1024,256]{1,0:T(8,128)(2,1)} %constant.16.clone.refs_1_.hi_ref) | copy-start | bytes 1572868
  0.6 35.6 %copy-start.1 = (bf16[1024,256]{1,0:T(8,128)(2,1)S(1)}, bf16[1024,256]{1,0:T(8,128)(2,1)}, u32[]{:S(2)}) copy-start(bf16[1024,256]{1,0:T(8,128)(2,1)} %constant.17.clone.refs_2_.lo_ref) | copy-start | bytes 1572868
  0.7 35.6 %copy-start.2 = (bf16[256,256]{1,0:T(8,128)(2,1)S(1)}, bf16[256,256]{1,0:T(8,128)(2,1)}, u32[]{:S(2)}) copy-start(bf16[256,256]{1,0:T(8,128)(2,1)} %constant.21.clone.first_ref) | copy-start | bytes 393220
  3.7 20.8 %all-to-all-start = ((f32[32,2,128]{2,1,0:T(2,128)}), f32[32,2,128]{2,1,0:T(2,128)S(1)}, u32[]{:S(2)}, u32[]{:S(2)}) async-start(f32[32,2,128]{2,1,0:T(2,128)} %get-tuple-element.36), calls=%async_computation | async-start | bytes 65536 | tf_op jit(solution)/shard_map/all_to_all | solution.py:560
  32.4 14.5 %all-to-all-start.1 = ((f32[32,25,1,128]{3,2,1,0:T(1,128)}), f32[32,25,1,128]{3,2,1,0:T(1,128)S(1)}, u32[]{:S(2)}, u32[]{:S(2)}) async-start(f32[32,25,1,128]{3,2,1,0:T(1,128)} %bitcast.2), calls=%async_computation.1 | async-start | bytes 819200 | tf_op jit(solution)/shard_map/all_to_all | solution.py:602
  46.9 5.8 %collective-permute-start = (f32[1,128]{1,0:T(1,128)S(1)}, f32[1,128]{1,0:T(1,128)S(1)}, u32[]{:S(2)}, u32[]{:S(2)}) collective-permute-start(f32[1,128]{1,0:T(1,128)S(1)} %own.1), channel_id=1, source_target_pairs={{0,32},{32,0},{64,96},{96,64},{128,160},{160,128},{192,224},{224,1... | collective-permute-start | bytes 1544 | tf_op jit(solution)/shard_map/ppermute | solution.py:515
  52.7 8.1 %collective-permute-start.1 = (f32[1,128]{1,0:T(1,128)S(1)}, f32[1,128]{1,0:T(1,128)S(1)}, u32[]{:S(2)}, u32[]{:S(2)}) collective-permute-start(f32[1,128]{1,0:T(1,128)S(1)} %add.3.refs_0_), channel_id=1, source_target_pairs={{0,64},{32,96},{64,0},{96,32},{128,192},{160,224},{192,128},{224,1... | collective-permute-start | bytes 1544 | tf_op jit(solution)/shard_map/ppermute | solution.py:515
  53.9 6.9 %collective-permute-start.2 = (f32[1,128]{1,0:T(1,128)S(1)}, f32[1,128]{1,0:T(1,128)S(1)}, u32[]{:S(2)}, u32[]{:S(2)}) collective-permute-start(f32[1,128]{1,0:T(1,128)S(1)} %add.3.refs_0_), channel_id=1, source_target_pairs={{0,128},{32,160},{64,192},{96,224},{128,0},{160,32},{192,64},{224,... | collective-permute-start | bytes 1544 | tf_op jit(solution)/shard_map/ppermute | solution.py:515
  56.4 4.5 %collective-permute-start.3 = (f32[1,128]{1,0:T(1,128)S(1)}, f32[1,128]{1,0:T(1,128)S(1)}, u32[]{:S(2)}, u32[]{:S(2)}) collective-permute-start(f32[1,128]{1,0:T(1,128)S(1)} %add.3.refs_0_), channel_id=1, source_target_pairs={{0,192},{32,224},{64,128},{96,160},{128,64},{160,96},{192,0},{224,... | collective-permute-start | bytes 1544 | tf_op jit(solution)/shard_map/ppermute | solution.py:515

commit v9 on v8

--- a/solution.py
+++ b/solution.py
@@ -112,7 +112,9 @@
         said = said + jnp.where(off == 16.0 * (k + 1), value, 0.0)
     asked = lax.dot_general(hit_b, said.astype(BF16), (((0,), (0,)), ((), ())), preferred_element_type=F32)
     square = modal_ref[...] * modal_ref[...]
-    mine = dot_exact(square, cos_ref[...]) + dot_exact(single_ref[...], fit_ref[...])
+    spread = jnp.broadcast_to(cos_ref[...][:, None, :], (G, S, 128)).reshape(G * S, 128)
+    spread = jnp.where((iota((G * S, 128), 0) & 15) == 0, spread, 0.0)
+    mine = dot_exact(square, spread) + dot_exact(single_ref[...], fit_ref[...])
     four = mine.shape
     mine = jnp.sum(jnp.where((iota(four, 1) >> 5) == iota(four, 0), mine, 0.0), axis=0, keepdims=True)
     peers = out_ref.shape[0]
@@ -189,23 +191,28 @@
     tiles = energy_ref.shape[0] // FIT_TILE
     out_refs = near_refs + [rest_ref.at[c] for c in range(KEEP - NEAR)]
 
-    def copy(r):
-        rows = pl.ds(pl.multiple_of(r * FIT_TILE, FIT_TILE), FIT_TILE)
-        return pltpu.make_async_copy(source_ref.at[rows], energy_ref.at[rows], sems.at[r])
+    def copies(r):
+        few = FIT_TILE // 4
+        for k in range(4):
+            rows = pl.ds(pl.multiple_of(r * FIT_TILE + k * few, few), few)
+            yield pltpu.make_async_copy(source_ref.at[rows], energy_ref.at[rows], sems.at[r, k])
 
     def copy_out(r):
         rows = pl.ds(pl.multiple_of(r * FIT_TILE, FIT_TILE), FIT_TILE)
         return pltpu.make_async_copy(rest_ref.at[:, rows], far_ref.at[:, rows], out_sems.at[r])
 
     for r in range(2):
-        copy(r).start()
+        for copy in copies(r):
+            copy.start()
 
     def over_rows(r, carry):
-        copy(r).wait()
+        for copy in copies(r):
+            copy.wait()
 
         @pl.when(r + 2 < tiles)
         def _():
-            copy(r + 2).start()
+            for copy in copies(r + 2):
+                copy.start()
 
         fit_some(energy_ref, hi_ref, lo_ref, first_ref, out_refs, r * FIT_TILE)
         copy_out(r).start()
@@ -475,13 +482,17 @@
         int(np.prod(o.shape)) * o.dtype.itemsize for o in outs
     )
     count = len(args) + len(outs) + len(scratch)
+    pieces = {i: 4 if args[i].size * args[i].dtype.itemsize >= 2**18 else 1 for i in fetched}
 
     def fetching(*refs):
         refs, held, sems = list(refs[:count]), refs[count:-1], refs[-1]
-        copies = [
-            pltpu.make_async_copy(refs[i], buffer, sems.at[k])
-            for k, (i, buffer) in enumerate(zip(fetched, held, strict=True))
-        ]
+        copies = []
+        for i, buffer in zip(fetched, held, strict=True):
+            rows = args[i].shape[0] // pieces[i]
+            for k in range(pieces[i]):
+                some = slice(k * rows, (k + 1) * rows)
+                ends = (refs[i].at[some], buffer.at[some]) if pieces[i] > 1 else (refs[i], buffer)
+                copies.append(pltpu.make_async_copy(*ends, sems.at[len(copies)]))
         for copy in copies:
             copy.start()
         for copy in copies:
@@ -493,7 +504,7 @@
     extra = []
     if fetched:
         extra = [pltpu.VMEM(args[i].shape, args[i].dtype) for i in fetched]
-        extra.append(pltpu.SemaphoreType.DMA((len(fetched),)))
+        extra.append(pltpu.SemaphoreType.DMA((sum(pieces.values()),)))
     outside = set(apart) | set(fetched)
     return pl.pallas_call(
         fetching if fetched else kernel,
@@ -529,11 +540,11 @@
     number = triples.shape[0]
     own = modals.shape[0]
     capacity = 3 * number // devices
-    cos_wide = np.zeros((G * S, 128), np.float32)
+    cos_wide = np.zeros((G, 128), np.float32)
     fit_wide = np.zeros((G, 128), np.float32)
     cos_block = np.zeros((128, own * G), np.float32)
     for m in range(own):
-        cos_wide[::S, m * 32 : m * 32 + KEEP] = COSINES.T
+        cos_wide[:, m * 32 : m * 32 + KEEP] = COSINES.T
         fit_wide[:, m * 32 + KEEP : m * 32 + 2 * KEEP] = FITTER.T
         cos_block[m * KEEP : (m + 1) * KEEP, m * G : (m + 1) * G] = COSINES
     kron = np.einsum("dh,el->hlde", FITTER, FITTER).reshape(G * G, KEEP * KEEP)
@@ -615,7 +626,7 @@
         scratch=[
             pltpu.VMEM(energies.shape, BF16),
             pltpu.VMEM(far_part, F32),
-            pltpu.SemaphoreType.DMA((number // FIT_TILE,)),
+            pltpu.SemaphoreType.DMA((number // FIT_TILE, 4)),
             pltpu.SemaphoreType.DMA((number // FIT_TILE,)),
         ],
         name="fit",

time: 62.1 us -> 61.7 us (level)
  no operation moved by 1% of the time
where the time goes in v9:
time: 61.7 us; the launch traced here: 61.3 us
  Pallas kernels  29.1 us (47%)
  starting transfers between devices  24.8 us (40%)
  waiting for transfers between devices  6.57 us (11%)
  between operations  0.76 us (1%)
    pallas_call x7, Pallas kernels, call(): pl.pallas_call(fetching if fetched else kernel, out_shape=outs, in_specs=...  29.1 us
    all_to_all x1, starting transfers between devices, body(): came = lax.all_to_all(send, 'dev', 0, 0, tiled=True)  12 us
    ppermute x4, starting transfers between devices, across(): lax.ppermute(a, 'grp', [(i, i ^ k) for i in range(lax.axis_size('grp'))])  8.89 us
    all_to_all x1, waiting for transfers between devices, body(): came = lax.all_to_all(send, 'dev', 0, 0, tiled=True)  5.44 us
    all_to_all x1, starting transfers between devices, body(): lax.all_to_all(answer.reshape(devices, each, 1, 128), 'dev', 0, 0, tiled=...  3.9 us
  transfers between devices with their start and end apart: 6, of which 3 were waited for; matrix products, arithmetic and copies ran while one was open for 0% of the time, Pallas kernels for 29%

profile of v9, /device:TPU:1, one launch (start us, length us, event | category | flops | bytes accessed | tf_op | source)
XLA Modules:
  0.0 61.3 jit_solution(4829883316742973957)
XLA Ops:
  0.6 0.0 copy-start
  0.6 0.0 copy-start.1
  0.7 0.0 copy-start.2
  0.7 2.7 %ask.1 = (f32[32,2,128]{2,1,0:T(2,128)}, f32[384,128]{1,0:T(8,128)S(1)}) custom-call(s32[3,128]{1,0:T(4,128)} %bitcast.7, s32[114,114]{1,0:T(8,128)} %refs_1_.2, s32[1,114]{1,0:T(1,128)} %bitcast.8, f32[4,512]{1,0:T(4,128)} %refs_3_.3, f32[4,32]{1,0:T(4,128)} %refs_4_.2, f32[32,128]{1,0:T(8,128)} %constant.19.clone.refs_5_, f32[32,128]{1,0:T(8,128)} %constant.20.clone.refs_6_), custom_call_target="tpu_custom_call" | custom-call | bytes 324824 | tf_op jit(solution)/shard_map/ask/pallas_call | solution.py:509
  3.3 12.0 %all-to-all-start = ((f32[32,2,128]{2,1,0:T(2,128)}), f32[32,2,128]{2,1,0:T(2,128)S(1)}, u32[]{:S(2)}, u32[]{:S(2)}) async-start(f32[32,2,128]{2,1,0:T(2,128)} %get-tuple-element.36), calls=%async_computation | async-start | bytes 65536 | tf_op jit(solution)/shard_map/all_to_all | solution.py:571
  15.4 3.3 %table.1 = (bf16[256,512]{1,0:T(8,128)(2,1)S(1)}, bf16[256,512]{1,0:T(8,128)(2,1)S(1)}, f32[128,256]{1,0:T(8,128)S(1)}) custom-call(f32[256,1024]{1,0:T(8,128)} %refs_0_.1, bf16[1024,256]{1,0:T(8,128)(2,1)} %constant.16.clone.refs_1_.hi_ref, bf16[1024,256]{1,0:T(8,128)(2,1)} %constant.17.clone.refs_2_.lo_ref, f32[4,512]{1,0:T(4,128)} %refs_3_.3, ...), custom_call_target="tpu_custom_call" | custom-call | flops 500000000 | bytes 2826240 | tf_op jit(solution)/shard_map/table/pallas_call | solution.py:509
  18.7 5.4 %all-to-all-done.came_ref = f32[32,2,128]{2,1,0:T(2,128)S(1)} async-done(((f32[32,2,128]{2,1,0:T(2,128)}), f32[32,2,128]{2,1,0:T(2,128)S(1)}, u32[]{:S(2)}, u32[]{:S(2)}) %all-to-all-start) | async-done | bytes 32800 | tf_op jit(solution)/shard_map/all_to_all | solution.py:571
  24.2 7.8 %share.1 = (f32[800,128]{1,0:T(8,128)}, f32[384,128]{1,0:T(8,128)S(1)}) custom-call(f32[32,2,128]{2,1,0:T(2,128)S(1)} %all-to-all-done.came_ref, bf16[256,512]{1,0:T(8,128)(2,1)S(1)} %get-tuple-element.37.hi_ref, bf16[256,512]{1,0:T(8,128)(2,1)S(1)} %get-tuple-element.38.lo_ref, bf16[128,32768]{1,0:T(8,128)(2,1)} %source_ref.3, ...), custom_call_target="tpu_custom_call" | custom-call | flops 1000000000 | bytes 10027008 | tf_op jit(solution)/shard_map/share/pallas_call | solution.py:509
  32.0 3.9 %all-to-all-start.1 = ((f32[32,25,1,128]{3,2,1,0:T(1,128)}), f32[32,25,1,128]{3,2,1,0:T(1,128)S(1)}, u32[]{:S(2)}, u32[]{:S(2)}) async-start(f32[32,25,1,128]{3,2,1,0:T(1,128)} %bitcast.2), calls=%async_computation.1 | async-start | bytes 819200 | tf_op jit(solution)/shard_map/all_to_all | solution.py:613
  35.9 0.0 copy-done
  35.9 0.0 copy-done.1
  35.9 0.0 copy-done.2
  35.9 10.3 %fit.1 = (f32[128,256]{1,0:T(8,128)S(1)}, f32[128,256]{1,0:T(8,128)S(1)}, f32[128,256]{1,0:T(8,128)S(1)}, f32[128,256]{1,0:T(8,128)S(1)}, f32[128,256]{1,0:T(8,1...) custom-call(bf16[128,32768]{1,0:T(8,128)(2,1)} %source_ref.3, ...), custom_call_target="tpu_custom_call" | custom-call | flops 5000000000 | bytes 11665408 | tf_op jit(solution)/shard_map/fit/pallas_call | solution.py:509
  46.2 0.3 all-to-all-done.1
  46.5 5.0 %collective-permute-start = (f32[1,128]{1,0:T(1,128)S(1)}, f32[1,128]{1,0:T(1,128)S(1)}, u32[]{:S(2)}, u32[]{:S(2)}) collective-permute-start(f32[1,128]{1,0:T(1,128)S(1)} %own.1), channel_id=1, source_target_pairs={{0,32},{32,0},{64,96},{96,64},{128,160},{160,128},{192,224},{224,1... | collective-permute-start | bytes 1544 | tf_op jit(solution)/shard_map/ppermute | solution.py:526
  51.5 0.8 %collective-permute-done = f32[1,128]{1,0:T(1,128)S(1)} collective-permute-done((f32[1,128]{1,0:T(1,128)S(1)}, f32[1,128]{1,0:T(1,128)S(1)}, u32[]{:S(2)}, u32[]{:S(2)}) %collective-permute-start) | collective-permute-done | bytes 544 | tf_op jit(solution)/shard_map/ppermute | solution.py:526
  52.3 1.2 %collective-permute-start.1 = (f32[1,128]{1,0:T(1,128)S(1)}, f32[1,128]{1,0:T(1,128)S(1)}, u32[]{:S(2)}, u32[]{:S(2)}) collective-permute-start(f32[1,128]{1,0:T(1,128)S(1)} %add.3.refs_0_), channel_id=1, source_target_pairs={{0,64},{32,96},{64,0},{96,32},{128,192},{160,224},{192,128},{224,1... | collective-permute-start | bytes 1544 | tf_op jit(solution)/shard_map/ppermute | solution.py:526
  53.6 2.4 %collective-permute-start.2 = (f32[1,128]{1,0:T(1,128)S(1)}, f32[1,128]{1,0:T(1,128)S(1)}, u32[]{:S(2)}, u32[]{:S(2)}) collective-permute-start(f32[1,128]{1,0:T(1,128)S(1)} %add.3.refs_0_), channel_id=1, source_target_pairs={{0,128},{32,160},{64,192},{96,224},{128,0},{160,32},{192,64},{224,... | collective-permute-start | bytes 1544 | tf_op jit(solution)/shard_map/ppermute | solution.py:526
  56.0 0.2 collective-permute-start.3
  56.2 4.3 %faces.1 = (bf16[128,4096]{1,0:T(8,128)(2,1)}, f32[1,128]{1,0:T(1,128)}) custom-call(f32[128,256]{1,0:T(8,128)S(1)} %get-tuple-element.52.refs_0_, f32[128,256]{1,0:T(8,128)S(1)} %get-tuple-element.53.refs_1_, f32[128,256]{1,0:T(8,128)S(1)} %get-tuple-element.54.refs_2_, f32[128,256]{1,0:T(8,128)S(1)} %get-tuple-element.55.refs_3_, ...), custom_call_target="tpu_custom_call" | custom-call | flops 1000000000 | bytes 3949056 | tf_op jit(solution)/shard_map/faces/pallas_call | solution.py:509
  60.5 0.0 collective-permute-done.1.refs_1_
  60.5 0.0 collective-permute-done.2.refs_2_
  60.5 0.0 collective-permute-done.3.refs_3_
  60.5 0.8 %integrals.1 = f32[4,256]{1,0:T(4,128)} custom-call(f32[1,128]{1,0:T(1,128)S(1)} %add.3.refs_0_, f32[1,128]{1,0:T(1,128)S(1)} %collective-permute-done.1.refs_1_, f32[1,128]{1,0:T(1,128)S(1)} %collective-permute-done.2.refs_2_, f32[1,128]{1,0:T(1,128)S(1)} %collective-permute-done.3.refs_3_, f32[128,256]{1,0:T(8,128)S(1)} %get-tuple-element.68.refs_4_), custom_call_target="tpu_custom_call" | custom-call | bytes 137216 | tf_op jit(solution)/shard_map/integrals/pallas_call | solution.py:509
  (2 shorter events, 0.0 us)
Async XLA Ops:
  0.6 35.2 %copy-start = (bf16[1024,256]{1,0:T(8,128)(2,1)S(1)}, bf16[1024,256]{1,0:T(8,128)(2,1)}, u32[]{:S(2)}) copy-start(bf16[1024,256]{1,0:T(8,128)(2,1)} %constant.16.clone.refs_1_.hi_ref) | copy-start | bytes 1572868
  0.6 35.2 %copy-start.1 = (bf16[1024,256]{1,0:T(8,128)(2,1)S(1)}, bf16[1024,256]{1,0:T(8,128)(2,1)}, u32[]{:S(2)}) copy-start(bf16[1024,256]{1,0:T(8,128)(2,1)} %constant.17.clone.refs_2_.lo_ref) | copy-start | bytes 1572868
  0.7 35.2 %copy-start.2 = (bf16[256,256]{1,0:T(8,128)(2,1)S(1)}, bf16[256,256]{1,0:T(8,128)(2,1)}, u32[]{:S(2)}) copy-start(bf16[256,256]{1,0:T(8,128)(2,1)} %constant.21.clone.first_ref) | copy-start | bytes 393220
  3.3 20.8 %all-to-all-start = ((f32[32,2,128]{2,1,0:T(2,128)}), f32[32,2,128]{2,1,0:T(2,128)S(1)}, u32[]{:S(2)}, u32[]{:S(2)}) async-start(f32[32,2,128]{2,1,0:T(2,128)} %get-tuple-element.36), calls=%async_computation | async-start | bytes 65536 | tf_op jit(solution)/shard_map/all_to_all | solution.py:571
  32.0 14.5 %all-to-all-start.1 = ((f32[32,25,1,128]{3,2,1,0:T(1,128)}), f32[32,25,1,128]{3,2,1,0:T(1,128)S(1)}, u32[]{:S(2)}, u32[]{:S(2)}) async-start(f32[32,25,1,128]{3,2,1,0:T(1,128)} %bitcast.2), calls=%async_computation.1 | async-start | bytes 819200 | tf_op jit(solution)/shard_map/all_to_all | solution.py:613
  46.5 5.8 %collective-permute-start = (f32[1,128]{1,0:T(1,128)S(1)}, f32[1,128]{1,0:T(1,128)S(1)}, u32[]{:S(2)}, u32[]{:S(2)}) collective-permute-start(f32[1,128]{1,0:T(1,128)S(1)} %own.1), channel_id=1, source_target_pairs={{0,32},{32,0},{64,96},{96,64},{128,160},{160,128},{192,224},{224,1... | collective-permute-start | bytes 1544 | tf_op jit(solution)/shard_map/ppermute | solution.py:526
  52.3 8.1 %collective-permute-start.1 = (f32[1,128]{1,0:T(1,128)S(1)}, f32[1,128]{1,0:T(1,128)S(1)}, u32[]{:S(2)}, u32[]{:S(2)}) collective-permute-start(f32[1,128]{1,0:T(1,128)S(1)} %add.3.refs_0_), channel_id=1, source_target_pairs={{0,64},{32,96},{64,0},{96,32},{128,192},{160,224},{192,128},{224,1... | collective-permute-start | bytes 1544 | tf_op jit(solution)/shard_map/ppermute | solution.py:526
  53.6 6.9 %collective-permute-start.2 = (f32[1,128]{1,0:T(1,128)S(1)}, f32[1,128]{1,0:T(1,128)S(1)}, u32[]{:S(2)}, u32[]{:S(2)}) collective-permute-start(f32[1,128]{1,0:T(1,128)S(1)} %add.3.refs_0_), channel_id=1, source_target_pairs={{0,128},{32,160},{64,192},{96,224},{128,0},{160,32},{192,64},{224,... | collective-permute-start | bytes 1544 | tf_op jit(solution)/shard_map/ppermute | solution.py:526
  56.0 4.5 %collective-permute-start.3 = (f32[1,128]{1,0:T(1,128)S(1)}, f32[1,128]{1,0:T(1,128)S(1)}, u32[]{:S(2)}, u32[]{:S(2)}) collective-permute-start(f32[1,128]{1,0:T(1,128)S(1)} %add.3.refs_0_), channel_id=1, source_target_pairs={{0,192},{32,224},{64,128},{96,160},{128,64},{160,96},{192,0},{224,... | collective-permute-start | bytes 1544 | tf_op jit(solution)/shard_map/ppermute | solution.py:526

commit v10 on v9

--- a/solution.py
+++ b/solution.py
@@ -341,7 +341,7 @@
             return tuple(fresh)
 
         none = jnp.zeros((tile, 128), F32)
-        lead = lax.fori_loop(0, G, over_points, (none,) * lanes, unroll=8)
+        lead = lax.fori_loop(0, G, over_points, (none,) * lanes, unroll=16)
         for k in range(lanes):
             lead_ref[rows_r, k * 128 : (k + 1) * 128] = lead[k]
         return carry
@@ -408,8 +408,16 @@
     out_ref[...] = jnp.sum(rows, axis=0, keepdims=True)
 
 
+def gather_kernel(came_ref, meta_ref, out_ref):
+    place = meta_ref[:, 0:1]
+    hi, lo = halves(came_ref[...])
+    slots = came_ref.shape[0]
+    for h in range(2):
+        out_ref[:, h * 128 : (h + 1) * 128] = pick_two(one_hot(place + 12.0 * h, slots), hi, lo)
+
+
 def face_kernel(*refs):
-    far_ref, came_ref, known_ref, meta_ref, far_out, energy_ref, coef_ref, rest_ref, out_sems, sem = refs[NEAR:]
+    far_ref, got_ref, known_ref, far_out, energy_ref, coef_ref, rest_ref, out_sems, sem = refs[NEAR:]
     fit_refs = list(refs[:NEAR]) + [rest_ref.at[c] for c in range(KEEP - NEAR)]
     coming = pltpu.make_async_copy(far_ref, rest_ref, sem)
     coming.start()
@@ -419,12 +427,9 @@
     for k in range(KEEP // some):
         cols = slice(k * some * 256, (k + 1) * some * 256)
         leaving.append(pltpu.make_async_copy(coef_ref.at[:, cols], far_out.at[:, cols], out_sems.at[k]))
-    place = meta_ref[:, 0:1]
     known = known_ref[...]
     one, two, three = (known[p * number : (p + 1) * number] for p in range(3))
-    hi, lo = halves(came_ref[...])
-    slots = came_ref.shape[0]
-    got = [pick_two(one_hot(place + 12.0 * h, slots), hi, lo) for h in range(2)]
+    got = [got_ref[:, h * 128 : (h + 1) * 128] for h in range(2)]
     lane = iota((number, 128), 1)
     k, n = iota((128, 256), 0), iota((128, 256), 1)
     two_wide = dot_two(two, (k == (n >> 4)).astype(F32).astype(BF16))
@@ -635,15 +640,19 @@
     terms, fitted = lax.optimization_barrier((terms, fitted))
     (mine,) = call(own_kernel, [shaped((1, 128))], terms, name="own")
     mine = mine + across(mine, 1)
-    parts = [mine] + [across(mine, k) for k in range(2, groups, 2)]
-    mine, known = lax.optimization_barrier((mine, known))
+    mine, terms = lax.optimization_barrier((mine, terms))
+    neighbour = across(mine, 2)
+    (got,) = call(gather_kernel, [shaped((3 * number, KEEP**2))], terms, meta, name="gather", flops=3 * 10**8)
+    neighbour, got = lax.optimization_barrier((neighbour, got))
+    mine = mine + neighbour
+    parts = [mine, across(mine, 4)]
+    mine, known, got = lax.optimization_barrier((mine, known, got))
     coefficients, energy = call(
         face_kernel,
         [pltpu.HBM((number, KEEP**3), BF16), shaped((1, number))],
         *fitted,
-        terms,
+        got,
         known,
-        meta,
         apart=(NEAR,),
         outs_apart=(0,),
         scratch=[

time: 61.7 us -> 62.9 us (1.019)
    pallas_call x7 -> x8, Pallas kernels: 29.1 us -> 29.4 us  [call(): pl.pallas_call(fetching if fetched else kernel, out_shape=outs, in_specs=...]
    ppermute x4 -> x3, starting transfers between devices: 8.89 us -> 9 us  [across(): lax.ppermute(a, 'grp', [(i, i ^ k) for i in range(lax.axis_size('grp'))])]
  transfers between devices with their start and end apart: 6 -> 5, of which waited for: 3 -> 4; matrix products, arithmetic and copies ran while one was open for 0% -> 0% of each run, Pallas kernels for 29% -> 30%
where the time goes in v10:
time: 62.9 us; the launch traced here: 61.9 us
  Pallas kernels  29.4 us (47%)
  starting transfers between devices  24.9 us (40%)
  waiting for transfers between devices  6.74 us (11%)
  between operations  0.75 us (1%)
    pallas_call x8, Pallas kernels, call(): pl.pallas_call(fetching if fetched else kernel, out_shape=outs, in_specs=...  29.4 us
    all_to_all x1, starting transfers between devices, body(): came = lax.all_to_all(send, 'dev', 0, 0, tiled=True)  12 us
    ppermute x3, starting transfers between devices, across(): lax.ppermute(a, 'grp', [(i, i ^ k) for i in range(lax.axis_size('grp'))])  9 us
    all_to_all x1, waiting for transfers between devices, body(): came = lax.all_to_all(send, 'dev', 0, 0, tiled=True)  5.44 us
    all_to_all x1, starting transfers between devices, body(): lax.all_to_all(answer.reshape(devices, each, 1, 128), 'dev', 0, 0, tiled=...  3.9 us
  transfers between devices with their start and end apart: 5, of which 4 were waited for; matrix products, arithmetic and copies ran while one was open for 0% of the time, Pallas kernels for 30%

profile of v10, /device:TPU:1, one launch (start us, length us, event | category | flops | bytes accessed | tf_op | source)
XLA Modules:
  0.0 61.9 jit_solution(1308096736207135696)
XLA Ops:
  0.6 0.0 copy-start
  0.6 0.0 copy-start.1
  0.7 0.0 copy-start.2
  0.7 2.7 %ask.1 = (f32[32,2,128]{2,1,0:T(2,128)}, f32[384,128]{1,0:T(8,128)S(1)}) custom-call(s32[3,128]{1,0:T(4,128)} %bitcast.7, s32[114,114]{1,0:T(8,128)} %refs_1_.2, s32[1,114]{1,0:T(1,128)} %bitcast.8, f32[4,512]{1,0:T(4,128)} %refs_3_.3, f32[4,32]{1,0:T(4,128)} %refs_4_.2, f32[32,128]{1,0:T(8,128)} %constant.19.clone.refs_5_, f32[32,128]{1,0:T(8,128)} %constant.20.clone.refs_6_), custom_call_target="tpu_custom_call" | custom-call | bytes 324824 | tf_op jit(solution)/shard_map/ask/pallas_call | solution.py:514
  3.3 12.0 %all-to-all-start = ((f32[32,2,128]{2,1,0:T(2,128)}), f32[32,2,128]{2,1,0:T(2,128)S(1)}, u32[]{:S(2)}, u32[]{:S(2)}) async-start(f32[32,2,128]{2,1,0:T(2,128)} %get-tuple-element.41), calls=%async_computation | async-start | bytes 65536 | tf_op jit(solution)/shard_map/all_to_all | solution.py:576
  15.4 3.3 %table.1 = (bf16[256,512]{1,0:T(8,128)(2,1)S(1)}, bf16[256,512]{1,0:T(8,128)(2,1)S(1)}, f32[128,256]{1,0:T(8,128)S(1)}) custom-call(f32[256,1024]{1,0:T(8,128)} %refs_0_.1, bf16[1024,256]{1,0:T(8,128)(2,1)} %constant.16.clone.refs_1_.hi_ref, bf16[1024,256]{1,0:T(8,128)(2,1)} %constant.17.clone.refs_2_.lo_ref, f32[4,512]{1,0:T(4,128)} %refs_3_.3, ...), custom_call_target="tpu_custom_call" | custom-call | flops 500000000 | bytes 2826240 | tf_op jit(solution)/shard_map/table/pallas_call | solution.py:514
  18.7 5.4 %all-to-all-done.came_ref = f32[32,2,128]{2,1,0:T(2,128)S(1)} async-done(((f32[32,2,128]{2,1,0:T(2,128)}), f32[32,2,128]{2,1,0:T(2,128)S(1)}, u32[]{:S(2)}, u32[]{:S(2)}) %all-to-all-start) | async-done | bytes 32800 | tf_op jit(solution)/shard_map/all_to_all | solution.py:576
  24.2 7.7 %share.1 = (f32[800,128]{1,0:T(8,128)}, f32[384,128]{1,0:T(8,128)S(1)}) custom-call(f32[32,2,128]{2,1,0:T(2,128)S(1)} %all-to-all-done.came_ref, bf16[256,512]{1,0:T(8,128)(2,1)S(1)} %get-tuple-element.42.hi_ref, bf16[256,512]{1,0:T(8,128)(2,1)S(1)} %get-tuple-element.43.lo_ref, bf16[128,32768]{1,0:T(8,128)(2,1)} %source_ref.3, ...), custom_call_target="tpu_custom_call" | custom-call | flops 1000000000 | bytes 10027008 | tf_op jit(solution)/shard_map/share/pallas_call | solution.py:514
  31.8 3.9 %all-to-all-start.1 = ((f32[32,25,1,128]{3,2,1,0:T(1,128)}), f32[32,25,1,128]{3,2,1,0:T(1,128)S(1)}, u32[]{:S(2)}, u32[]{:S(2)}) async-start(f32[32,25,1,128]{3,2,1,0:T(1,128)} %bitcast.2), calls=%async_computation.1 | async-start | bytes 819200 | tf_op jit(solution)/shard_map/all_to_all | solution.py:618
  35.7 0.0 copy-done
  35.7 0.0 copy-done.1
  35.8 0.0 copy-done.2
  35.8 10.3 %fit.1 = (f32[128,256]{1,0:T(8,128)S(1)}, f32[128,256]{1,0:T(8,128)S(1)}, f32[128,256]{1,0:T(8,128)S(1)}, f32[128,256]{1,0:T(8,128)S(1)}, f32[128,256]{1,0:T(8,1...) custom-call(bf16[128,32768]{1,0:T(8,128)(2,1)} %source_ref.3, ...), custom_call_target="tpu_custom_call" | custom-call | flops 5000000000 | bytes 11665408 | tf_op jit(solution)/shard_map/fit/pallas_call | solution.py:514
  46.1 0.3 all-to-all-done.1
  46.4 5.0 %collective-permute-start = (f32[1,128]{1,0:T(1,128)S(1)}, f32[1,128]{1,0:T(1,128)S(1)}, u32[]{:S(2)}, u32[]{:S(2)}) collective-permute-start(f32[1,128]{1,0:T(1,128)S(1)} %own.1), channel_id=1, source_target_pairs={{0,32},{32,0},{64,96},{96,64},{128,160},{160,128},{192,224},{224,1... | collective-permute-start | bytes 1544 | tf_op jit(solution)/shard_map/ppermute | solution.py:531
  51.4 0.8 %collective-permute-done = f32[1,128]{1,0:T(1,128)S(1)} collective-permute-done((f32[1,128]{1,0:T(1,128)S(1)}, f32[1,128]{1,0:T(1,128)S(1)}, u32[]{:S(2)}, u32[]{:S(2)}) %collective-permute-start) | collective-permute-done | bytes 544 | tf_op jit(solution)/shard_map/ppermute | solution.py:531
  52.2 1.2 %collective-permute-start.1 = (f32[1,128]{1,0:T(1,128)S(1)}, f32[1,128]{1,0:T(1,128)S(1)}, u32[]{:S(2)}, u32[]{:S(2)}) collective-permute-start(f32[1,128]{1,0:T(1,128)S(1)} %add.6), channel_id=1, source_target_pairs={{0,64},{32,96},{64,0},{96,32},{128,192},{160,224},{192,128},{224,1... | collective-permute-start | bytes 1544 | tf_op jit(solution)/shard_map/ppermute | solution.py:531
  53.4 1.0 %gather.1.refs_11_ = f32[384,256]{1,0:T(8,128)S(1)} custom-call(f32[800,128]{1,0:T(8,128)S(1)} %bitcast.6, f32[384,128]{1,0:T(8,128)S(1)} %get-tuple-element.44.meta_ref), custom_call_target="tpu_custom_call" | custom-call | flops 300000000 | bytes 999424 | tf_op jit(solution)/shard_map/gather/pallas_call | solution.py:514
  54.4 0.2 collective-permute-done.1
  54.6 2.8 %collective-permute-start.2 = (f32[1,128]{1,0:T(1,128)S(1)}, f32[1,128]{1,0:T(1,128)S(1)}, u32[]{:S(2)}, u32[]{:S(2)}) collective-permute-start(f32[1,128]{1,0:T(1,128)S(1)} %add.7.refs_0_), channel_id=1, source_target_pairs={{0,128},{32,160},{64,192},{96,224},{128,0},{160,32},{192,64},{224,... | collective-permute-start | bytes 1544 | tf_op jit(solution)/shard_map/ppermute | solution.py:531
  57.4 3.7 %faces.1 = (bf16[128,4096]{1,0:T(8,128)(2,1)}, f32[1,128]{1,0:T(1,128)}) custom-call(f32[128,256]{1,0:T(8,128)S(1)} %get-tuple-element.57.refs_0_, f32[128,256]{1,0:T(8,128)S(1)} %get-tuple-element.58.refs_1_, f32[128,256]{1,0:T(8,128)S(1)} %get-tuple-element.59.refs_2_, f32[128,256]{1,0:T(8,128)S(1)} %get-tuple-element.60.refs_3_, ...), custom_call_target="tpu_custom_call" | custom-call | flops 1000000000 | bytes 3736064 | tf_op jit(solution)/shard_map/faces/pallas_call | solution.py:514
  61.1 0.0 collective-permute-done.2.refs_1_
  61.1 0.8 %integrals.1 = f32[4,256]{1,0:T(4,128)} custom-call(f32[1,128]{1,0:T(1,128)S(1)} %add.7.refs_0_, f32[1,128]{1,0:T(1,128)S(1)} %collective-permute-done.2.refs_1_, f32[128,256]{1,0:T(8,128)S(1)} %get-tuple-element.78.refs_2_), custom_call_target="tpu_custom_call" | custom-call | bytes 136192 | tf_op jit(solution)/shard_map/integrals/pallas_call | solution.py:514
  (3 shorter events, 0.0 us)
Async XLA Ops:
  0.6 35.1 %copy-start = (bf16[1024,256]{1,0:T(8,128)(2,1)S(1)}, bf16[1024,256]{1,0:T(8,128)(2,1)}, u32[]{:S(2)}) copy-start(bf16[1024,256]{1,0:T(8,128)(2,1)} %constant.16.clone.refs_1_.hi_ref) | copy-start | bytes 1572868
  0.6 35.1 %copy-start.1 = (bf16[1024,256]{1,0:T(8,128)(2,1)S(1)}, bf16[1024,256]{1,0:T(8,128)(2,1)}, u32[]{:S(2)}) copy-start(bf16[1024,256]{1,0:T(8,128)(2,1)} %constant.17.clone.refs_2_.lo_ref) | copy-start | bytes 1572868
  0.7 35.1 %copy-start.2 = (bf16[256,256]{1,0:T(8,128)(2,1)S(1)}, bf16[256,256]{1,0:T(8,128)(2,1)}, u32[]{:S(2)}) copy-start(bf16[256,256]{1,0:T(8,128)(2,1)} %constant.21.clone.first_ref) | copy-start | bytes 393220
  3.3 20.8 %all-to-all-start = ((f32[32,2,128]{2,1,0:T(2,128)}), f32[32,2,128]{2,1,0:T(2,128)S(1)}, u32[]{:S(2)}, u32[]{:S(2)}) async-start(f32[32,2,128]{2,1,0:T(2,128)} %get-tuple-element.41), calls=%async_computation | async-start | bytes 65536 | tf_op jit(solution)/shard_map/all_to_all | solution.py:576
  31.8 14.5 %all-to-all-start.1 = ((f32[32,25,1,128]{3,2,1,0:T(1,128)}), f32[32,25,1,128]{3,2,1,0:T(1,128)S(1)}, u32[]{:S(2)}, u32[]{:S(2)}) async-start(f32[32,25,1,128]{3,2,1,0:T(1,128)} %bitcast.2), calls=%async_computation.1 | async-start | bytes 819200 | tf_op jit(solution)/shard_map/all_to_all | solution.py:618
  46.4 5.8 %collective-permute-start = (f32[1,128]{1,0:T(1,128)S(1)}, f32[1,128]{1,0:T(1,128)S(1)}, u32[]{:S(2)}, u32[]{:S(2)}) collective-permute-start(f32[1,128]{1,0:T(1,128)S(1)} %own.1), channel_id=1, source_target_pairs={{0,32},{32,0},{64,96},{96,64},{128,160},{160,128},{192,224},{224,1... | collective-permute-start | bytes 1544 | tf_op jit(solution)/shard_map/ppermute | solution.py:531
  52.2 2.4 %collective-permute-start.1 = (f32[1,128]{1,0:T(1,128)S(1)}, f32[1,128]{1,0:T(1,128)S(1)}, u32[]{:S(2)}, u32[]{:S(2)}) collective-permute-start(f32[1,128]{1,0:T(1,128)S(1)} %add.6), channel_id=1, source_target_pairs={{0,64},{32,96},{64,0},{96,32},{128,192},{160,224},{192,128},{224,1... | collective-permute-start | bytes 1544 | tf_op jit(solution)/shard_map/ppermute | solution.py:531
  54.6 6.5 %collective-permute-start.2 = (f32[1,128]{1,0:T(1,128)S(1)}, f32[1,128]{1,0:T(1,128)S(1)}, u32[]{:S(2)}, u32[]{:S(2)}) collective-permute-start(f32[1,128]{1,0:T(1,128)S(1)} %add.7.refs_0_), channel_id=1, source_target_pairs={{0,128},{32,160},{64,192},{96,224},{128,0},{160,32},{192,64},{224,... | collective-permute-start | bytes 1544 | tf_op jit(solution)/shard_map/ppermute | solution.py:531

commit v11 on v9

--- a/solution.py
+++ b/solution.py
@@ -341,7 +341,7 @@
             return tuple(fresh)
 
         none = jnp.zeros((tile, 128), F32)
-        lead = lax.fori_loop(0, G, over_points, (none,) * lanes, unroll=8)
+        lead = lax.fori_loop(0, G, over_points, (none,) * lanes, unroll=16)
         for k in range(lanes):
             lead_ref[rows_r, k * 128 : (k + 1) * 128] = lead[k]
         return carry

time: 61.7 us -> 61.6 us (level)
  no operation moved by 1% of the time
where the time goes in v11:
time: 61.6 us; the launch traced here: 61.1 us
  Pallas kernels  28.9 us (47%)
  starting transfers between devices  24.8 us (40%)
  waiting for transfers between devices  6.57 us (11%)
  between operations  0.76 us (1%)
    pallas_call x7, Pallas kernels, call(): pl.pallas_call(fetching if fetched else kernel, out_shape=outs, in_specs=...  28.9 us
    all_to_all x1, starting transfers between devices, body(): came = lax.all_to_all(send, 'dev', 0, 0, tiled=True)  12 us
    ppermute x4, starting transfers between devices, across(): lax.ppermute(a, 'grp', [(i, i ^ k) for i in range(lax.axis_size('grp'))])  8.89 us
    all_to_all x1, waiting for transfers between devices, body(): came = lax.all_to_all(send, 'dev', 0, 0, tiled=True)  5.44 us
    all_to_all x1, starting transfers between devices, body(): lax.all_to_all(answer.reshape(devices, each, 1, 128), 'dev', 0, 0, tiled=...  3.9 us
  transfers between devices with their start and end apart: 6, of which 3 were waited for; matrix products, arithmetic and copies ran while one was open for 0% of the time, Pallas kernels for 29%

profile of v11, /device:TPU:1, one launch (start us, length us, event | category | flops | bytes accessed | tf_op | source)
XLA Modules:
  0.0 61.1 jit_solution(11800630963028303855)
XLA Ops:
  0.6 0.0 copy-start
  0.6 0.0 copy-start.1
  0.7 0.0 copy-start.2
  0.7 2.7 %ask.1 = (f32[32,2,128]{2,1,0:T(2,128)}, f32[384,128]{1,0:T(8,128)S(1)}) custom-call(s32[3,128]{1,0:T(4,128)} %bitcast.7, s32[114,114]{1,0:T(8,128)} %refs_1_.2, s32[1,114]{1,0:T(1,128)} %bitcast.8, f32[4,512]{1,0:T(4,128)} %refs_3_.3, f32[4,32]{1,0:T(4,128)} %refs_4_.2, f32[32,128]{1,0:T(8,128)} %constant.19.clone.refs_5_, f32[32,128]{1,0:T(8,128)} %constant.20.clone.refs_6_), custom_call_target="tpu_custom_call" | custom-call | bytes 324824 | tf_op jit(solution)/shard_map/ask/pallas_call | solution.py:509
  3.3 12.0 %all-to-all-start = ((f32[32,2,128]{2,1,0:T(2,128)}), f32[32,2,128]{2,1,0:T(2,128)S(1)}, u32[]{:S(2)}, u32[]{:S(2)}) async-start(f32[32,2,128]{2,1,0:T(2,128)} %get-tuple-element.36), calls=%async_computation | async-start | bytes 65536 | tf_op jit(solution)/shard_map/all_to_all | solution.py:571
  15.4 3.3 %table.1 = (bf16[256,512]{1,0:T(8,128)(2,1)S(1)}, bf16[256,512]{1,0:T(8,128)(2,1)S(1)}, f32[128,256]{1,0:T(8,128)S(1)}) custom-call(f32[256,1024]{1,0:T(8,128)} %refs_0_.1, bf16[1024,256]{1,0:T(8,128)(2,1)} %constant.16.clone.refs_1_.hi_ref, bf16[1024,256]{1,0:T(8,128)(2,1)} %constant.17.clone.refs_2_.lo_ref, f32[4,512]{1,0:T(4,128)} %refs_3_.3, ...), custom_call_target="tpu_custom_call" | custom-call | flops 500000000 | bytes 2826240 | tf_op jit(solution)/shard_map/table/pallas_call | solution.py:509
  18.7 5.4 %all-to-all-done.came_ref = f32[32,2,128]{2,1,0:T(2,128)S(1)} async-done(((f32[32,2,128]{2,1,0:T(2,128)}), f32[32,2,128]{2,1,0:T(2,128)S(1)}, u32[]{:S(2)}, u32[]{:S(2)}) %all-to-all-start) | async-done | bytes 32800 | tf_op jit(solution)/shard_map/all_to_all | solution.py:571
  24.2 7.7 %share.1 = (f32[800,128]{1,0:T(8,128)}, f32[384,128]{1,0:T(8,128)S(1)}) custom-call(f32[32,2,128]{2,1,0:T(2,128)S(1)} %all-to-all-done.came_ref, bf16[256,512]{1,0:T(8,128)(2,1)S(1)} %get-tuple-element.37.hi_ref, bf16[256,512]{1,0:T(8,128)(2,1)S(1)} %get-tuple-element.38.lo_ref, bf16[128,32768]{1,0:T(8,128)(2,1)} %source_ref.3, ...), custom_call_target="tpu_custom_call" | custom-call | flops 1000000000 | bytes 10027008 | tf_op jit(solution)/shard_map/share/pallas_call | solution.py:509
  31.8 3.9 %all-to-all-start.1 = ((f32[32,25,1,128]{3,2,1,0:T(1,128)}), f32[32,25,1,128]{3,2,1,0:T(1,128)S(1)}, u32[]{:S(2)}, u32[]{:S(2)}) async-start(f32[32,25,1,128]{3,2,1,0:T(1,128)} %bitcast.2), calls=%async_computation.1 | async-start | bytes 819200 | tf_op jit(solution)/shard_map/all_to_all | solution.py:613
  35.7 0.0 copy-done
  35.7 0.0 copy-done.1
  35.8 0.0 copy-done.2
  35.8 10.3 %fit.1 = (f32[128,256]{1,0:T(8,128)S(1)}, f32[128,256]{1,0:T(8,128)S(1)}, f32[128,256]{1,0:T(8,128)S(1)}, f32[128,256]{1,0:T(8,128)S(1)}, f32[128,256]{1,0:T(8,1...) custom-call(bf16[128,32768]{1,0:T(8,128)(2,1)} %source_ref.3, ...), custom_call_target="tpu_custom_call" | custom-call | flops 5000000000 | bytes 11665408 | tf_op jit(solution)/shard_map/fit/pallas_call | solution.py:509
  46.0 0.3 all-to-all-done.1
  46.4 5.0 %collective-permute-start = (f32[1,128]{1,0:T(1,128)S(1)}, f32[1,128]{1,0:T(1,128)S(1)}, u32[]{:S(2)}, u32[]{:S(2)}) collective-permute-start(f32[1,128]{1,0:T(1,128)S(1)} %own.1), channel_id=1, source_target_pairs={{0,32},{32,0},{64,96},{96,64},{128,160},{160,128},{192,224},{224,1... | collective-permute-start | bytes 1544 | tf_op jit(solution)/shard_map/ppermute | solution.py:526
  51.4 0.8 %collective-permute-done = f32[1,128]{1,0:T(1,128)S(1)} collective-permute-done((f32[1,128]{1,0:T(1,128)S(1)}, f32[1,128]{1,0:T(1,128)S(1)}, u32[]{:S(2)}, u32[]{:S(2)}) %collective-permute-start) | collective-permute-done | bytes 544 | tf_op jit(solution)/shard_map/ppermute | solution.py:526
  52.2 1.2 %collective-permute-start.1 = (f32[1,128]{1,0:T(1,128)S(1)}, f32[1,128]{1,0:T(1,128)S(1)}, u32[]{:S(2)}, u32[]{:S(2)}) collective-permute-start(f32[1,128]{1,0:T(1,128)S(1)} %add.3.refs_0_), channel_id=1, source_target_pairs={{0,64},{32,96},{64,0},{96,32},{128,192},{160,224},{192,128},{224,1... | collective-permute-start | bytes 1544 | tf_op jit(solution)/shard_map/ppermute | solution.py:526
  53.4 2.4 %collective-permute-start.2 = (f32[1,128]{1,0:T(1,128)S(1)}, f32[1,128]{1,0:T(1,128)S(1)}, u32[]{:S(2)}, u32[]{:S(2)}) collective-permute-start(f32[1,128]{1,0:T(1,128)S(1)} %add.3.refs_0_), channel_id=1, source_target_pairs={{0,128},{32,160},{64,192},{96,224},{128,0},{160,32},{192,64},{224,... | collective-permute-start | bytes 1544 | tf_op jit(solution)/shard_map/ppermute | solution.py:526
  55.9 0.2 collective-permute-start.3
  56.1 4.3 %faces.1 = (bf16[128,4096]{1,0:T(8,128)(2,1)}, f32[1,128]{1,0:T(1,128)}) custom-call(f32[128,256]{1,0:T(8,128)S(1)} %get-tuple-element.52.refs_0_, f32[128,256]{1,0:T(8,128)S(1)} %get-tuple-element.53.refs_1_, f32[128,256]{1,0:T(8,128)S(1)} %get-tuple-element.54.refs_2_, f32[128,256]{1,0:T(8,128)S(1)} %get-tuple-element.55.refs_3_, ...), custom_call_target="tpu_custom_call" | custom-call | flops 1000000000 | bytes 3949056 | tf_op jit(solution)/shard_map/faces/pallas_call | solution.py:509
  60.3 0.0 collective-permute-done.1.refs_1_
  60.3 0.0 collective-permute-done.2.refs_2_
  60.4 0.0 collective-permute-done.3.refs_3_
  60.4 0.8 %integrals.1 = f32[4,256]{1,0:T(4,128)} custom-call(f32[1,128]{1,0:T(1,128)S(1)} %add.3.refs_0_, f32[1,128]{1,0:T(1,128)S(1)} %collective-permute-done.1.refs_1_, f32[1,128]{1,0:T(1,128)S(1)} %collective-permute-done.2.refs_2_, f32[1,128]{1,0:T(1,128)S(1)} %collective-permute-done.3.refs_3_, f32[128,256]{1,0:T(8,128)S(1)} %get-tuple-element.68.refs_4_), custom_call_target="tpu_custom_call" | custom-call | bytes 137216 | tf_op jit(solution)/shard_map/integrals/pallas_call | solution.py:509
  (2 shorter events, 0.0 us)
Async XLA Ops:
  0.6 35.1 %copy-start = (bf16[1024,256]{1,0:T(8,128)(2,1)S(1)}, bf16[1024,256]{1,0:T(8,128)(2,1)}, u32[]{:S(2)}) copy-start(bf16[1024,256]{1,0:T(8,128)(2,1)} %constant.16.clone.refs_1_.hi_ref) | copy-start | bytes 1572868
  0.6 35.1 %copy-start.1 = (bf16[1024,256]{1,0:T(8,128)(2,1)S(1)}, bf16[1024,256]{1,0:T(8,128)(2,1)}, u32[]{:S(2)}) copy-start(bf16[1024,256]{1,0:T(8,128)(2,1)} %constant.17.clone.refs_2_.lo_ref) | copy-start | bytes 1572868
  0.7 35.1 %copy-start.2 = (bf16[256,256]{1,0:T(8,128)(2,1)S(1)}, bf16[256,256]{1,0:T(8,128)(2,1)}, u32[]{:S(2)}) copy-start(bf16[256,256]{1,0:T(8,128)(2,1)} %constant.21.clone.first_ref) | copy-start | bytes 393220
  3.3 20.8 %all-to-all-start = ((f32[32,2,128]{2,1,0:T(2,128)}), f32[32,2,128]{2,1,0:T(2,128)S(1)}, u32[]{:S(2)}, u32[]{:S(2)}) async-start(f32[32,2,128]{2,1,0:T(2,128)} %get-tuple-element.36), calls=%async_computation | async-start | bytes 65536 | tf_op jit(solution)/shard_map/all_to_all | solution.py:571
  31.8 14.5 %all-to-all-start.1 = ((f32[32,25,1,128]{3,2,1,0:T(1,128)}), f32[32,25,1,128]{3,2,1,0:T(1,128)S(1)}, u32[]{:S(2)}, u32[]{:S(2)}) async-start(f32[32,25,1,128]{3,2,1,0:T(1,128)} %bitcast.2), calls=%async_computation.1 | async-start | bytes 819200 | tf_op jit(solution)/shard_map/all_to_all | solution.py:613
  46.4 5.8 %collective-permute-start = (f32[1,128]{1,0:T(1,128)S(1)}, f32[1,128]{1,0:T(1,128)S(1)}, u32[]{:S(2)}, u32[]{:S(2)}) collective-permute-start(f32[1,128]{1,0:T(1,128)S(1)} %own.1), channel_id=1, source_target_pairs={{0,32},{32,0},{64,96},{96,64},{128,160},{160,128},{192,224},{224,1... | collective-permute-start | bytes 1544 | tf_op jit(solution)/shard_map/ppermute | solution.py:526
  52.2 8.1 %collective-permute-start.1 = (f32[1,128]{1,0:T(1,128)S(1)}, f32[1,128]{1,0:T(1,128)S(1)}, u32[]{:S(2)}, u32[]{:S(2)}) collective-permute-start(f32[1,128]{1,0:T(1,128)S(1)} %add.3.refs_0_), channel_id=1, source_target_pairs={{0,64},{32,96},{64,0},{96,32},{128,192},{160,224},{192,128},{224,1... | collective-permute-start | bytes 1544 | tf_op jit(solution)/shard_map/ppermute | solution.py:526
  53.4 6.9 %collective-permute-start.2 = (f32[1,128]{1,0:T(1,128)S(1)}, f32[1,128]{1,0:T(1,128)S(1)}, u32[]{:S(2)}, u32[]{:S(2)}) collective-permute-start(f32[1,128]{1,0:T(1,128)S(1)} %add.3.refs_0_), channel_id=1, source_target_pairs={{0,128},{32,160},{64,192},{96,224},{128,0},{160,32},{192,64},{224,... | collective-permute-start | bytes 1544 | tf_op jit(solution)/shard_map/ppermute | solution.py:526
  55.9 4.5 %collective-permute-start.3 = (f32[1,128]{1,0:T(1,128)S(1)}, f32[1,128]{1,0:T(1,128)S(1)}, u32[]{:S(2)}, u32[]{:S(2)}) collective-permute-start(f32[1,128]{1,0:T(1,128)S(1)} %add.3.refs_0_), channel_id=1, source_target_pairs={{0,192},{32,224},{64,128},{96,160},{128,64},{160,96},{192,0},{224,... | collective-permute-start | bytes 1544 | tf_op jit(solution)/shard_map/ppermute | solution.py:526

commit v12 on v11

--- a/solution.py
+++ b/solution.py
@@ -124,7 +124,7 @@
 
 
 FIT_TILE = 32
-NEAR = 10
+NEAR = 11
 
 
 def fit_some(energy_ref, hi_ref, lo_ref, first_ref, out_refs, start):

time: 61.6 us -> 61.5 us (level)
  no operation moved by 1% of the time
where the time goes in v12:
time: 61.5 us; the launch traced here: 61.1 us
  Pallas kernels  28.9 us (47%)
  starting transfers between devices  24.8 us (40%)
  waiting for transfers between devices  6.58 us (11%)
  between operations  0.76 us (1%)
    pallas_call x7, Pallas kernels, call(): pl.pallas_call(fetching if fetched else kernel, out_shape=outs, in_specs=...  28.9 us
    all_to_all x1, starting transfers between devices, body(): came = lax.all_to_all(send, 'dev', 0, 0, tiled=True)  12 us
    ppermute x4, starting transfers between devices, across(): lax.ppermute(a, 'grp', [(i, i ^ k) for i in range(lax.axis_size('grp'))])  8.89 us
    all_to_all x1, waiting for transfers between devices, body(): came = lax.all_to_all(send, 'dev', 0, 0, tiled=True)  5.44 us
    all_to_all x1, starting transfers between devices, body(): lax.all_to_all(answer.reshape(devices, each, 1, 128), 'dev', 0, 0, tiled=...  3.9 us
  transfers between devices with their start and end apart: 6, of which 3 were waited for; matrix products, arithmetic and copies ran while one was open for 0% of the time, Pallas kernels for 29%

profile of v12, /device:TPU:1, one launch (start us, length us, event | category | flops | bytes accessed | tf_op | source)
XLA Modules:
  0.0 61.1 jit_solution(8589090398636337657)
XLA Ops:
  0.6 0.0 copy-start
  0.6 0.0 copy-start.1
  0.7 0.0 copy-start.2
  0.7 2.7 %ask.1 = (f32[32,2,128]{2,1,0:T(2,128)}, f32[384,128]{1,0:T(8,128)S(1)}) custom-call(s32[3,128]{1,0:T(4,128)} %bitcast.7, s32[114,114]{1,0:T(8,128)} %refs_1_.2, s32[1,114]{1,0:T(1,128)} %bitcast.8, f32[4,512]{1,0:T(4,128)} %refs_3_.3, f32[4,32]{1,0:T(4,128)} %refs_4_.2, f32[32,128]{1,0:T(8,128)} %constant.19.clone.refs_5_, f32[32,128]{1,0:T(8,128)} %constant.20.clone.refs_6_), custom_call_target="tpu_custom_call" | custom-call | bytes 324824 | tf_op jit(solution)/shard_map/ask/pallas_call | solution.py:509
  3.3 12.0 %all-to-all-start = ((f32[32,2,128]{2,1,0:T(2,128)}), f32[32,2,128]{2,1,0:T(2,128)S(1)}, u32[]{:S(2)}, u32[]{:S(2)}) async-start(f32[32,2,128]{2,1,0:T(2,128)} %get-tuple-element.38), calls=%async_computation | async-start | bytes 65536 | tf_op jit(solution)/shard_map/all_to_all | solution.py:571
  15.4 3.3 %table.1 = (bf16[256,512]{1,0:T(8,128)(2,1)S(1)}, bf16[256,512]{1,0:T(8,128)(2,1)S(1)}, f32[128,256]{1,0:T(8,128)S(1)}) custom-call(f32[256,1024]{1,0:T(8,128)} %refs_0_.1, bf16[1024,256]{1,0:T(8,128)(2,1)} %constant.16.clone.refs_1_.hi_ref, bf16[1024,256]{1,0:T(8,128)(2,1)} %constant.17.clone.refs_2_.lo_ref, f32[4,512]{1,0:T(4,128)} %refs_3_.3, ...), custom_call_target="tpu_custom_call" | custom-call | flops 500000000 | bytes 2826240 | tf_op jit(solution)/shard_map/table/pallas_call | solution.py:509
  18.7 5.4 %all-to-all-done.came_ref = f32[32,2,128]{2,1,0:T(2,128)S(1)} async-done(((f32[32,2,128]{2,1,0:T(2,128)}), f32[32,2,128]{2,1,0:T(2,128)S(1)}, u32[]{:S(2)}, u32[]{:S(2)}) %all-to-all-start) | async-done | bytes 32800 | tf_op jit(solution)/shard_map/all_to_all | solution.py:571
  24.2 7.7 %share.1 = (f32[800,128]{1,0:T(8,128)}, f32[384,128]{1,0:T(8,128)S(1)}) custom-call(f32[32,2,128]{2,1,0:T(2,128)S(1)} %all-to-all-done.came_ref, bf16[256,512]{1,0:T(8,128)(2,1)S(1)} %get-tuple-element.39.hi_ref, bf16[256,512]{1,0:T(8,128)(2,1)S(1)} %get-tuple-element.40.lo_ref, bf16[128,32768]{1,0:T(8,128)(2,1)} %source_ref.3, ...), custom_call_target="tpu_custom_call" | custom-call | flops 1000000000 | bytes 10027008 | tf_op jit(solution)/shard_map/share/pallas_call | solution.py:509
  31.8 3.9 %all-to-all-start.1 = ((f32[32,25,1,128]{3,2,1,0:T(1,128)}), f32[32,25,1,128]{3,2,1,0:T(1,128)S(1)}, u32[]{:S(2)}, u32[]{:S(2)}) async-start(f32[32,25,1,128]{3,2,1,0:T(1,128)} %bitcast.2), calls=%async_computation.1 | async-start | bytes 819200 | tf_op jit(solution)/shard_map/all_to_all | solution.py:613
  35.7 0.0 copy-done
  35.7 0.0 copy-done.1
  35.8 0.0 copy-done.2
  35.8 10.3 %fit.1 = (f32[128,256]{1,0:T(8,128)S(1)}, f32[128,256]{1,0:T(8,128)S(1)}, f32[128,256]{1,0:T(8,128)S(1)}, f32[128,256]{1,0:T(8,128)S(1)}, f32[128,256]{1,0:T(8,1...) custom-call(bf16[128,32768]{1,0:T(8,128)(2,1)} %source_ref.3, ...), custom_call_target="tpu_custom_call" | custom-call | flops 5000000000 | bytes 11665408 | tf_op jit(solution)/shard_map/fit/pallas_call | solution.py:509
  46.0 0.3 all-to-all-done.1
  46.4 5.0 %collective-permute-start = (f32[1,128]{1,0:T(1,128)S(1)}, f32[1,128]{1,0:T(1,128)S(1)}, u32[]{:S(2)}, u32[]{:S(2)}) collective-permute-start(f32[1,128]{1,0:T(1,128)S(1)} %own.1), channel_id=1, source_target_pairs={{0,32},{32,0},{64,96},{96,64},{128,160},{160,128},{192,224},{224,1... | collective-permute-start | bytes 1544 | tf_op jit(solution)/shard_map/ppermute | solution.py:526
  51.4 0.8 %collective-permute-done = f32[1,128]{1,0:T(1,128)S(1)} collective-permute-done((f32[1,128]{1,0:T(1,128)S(1)}, f32[1,128]{1,0:T(1,128)S(1)}, u32[]{:S(2)}, u32[]{:S(2)}) %collective-permute-start) | collective-permute-done | bytes 544 | tf_op jit(solution)/shard_map/ppermute | solution.py:526
  52.2 1.2 %collective-permute-start.1 = (f32[1,128]{1,0:T(1,128)S(1)}, f32[1,128]{1,0:T(1,128)S(1)}, u32[]{:S(2)}, u32[]{:S(2)}) collective-permute-start(f32[1,128]{1,0:T(1,128)S(1)} %add.3.refs_0_), channel_id=1, source_target_pairs={{0,64},{32,96},{64,0},{96,32},{128,192},{160,224},{192,128},{224,1... | collective-permute-start | bytes 1544 | tf_op jit(solution)/shard_map/ppermute | solution.py:526
  53.4 2.4 %collective-permute-start.2 = (f32[1,128]{1,0:T(1,128)S(1)}, f32[1,128]{1,0:T(1,128)S(1)}, u32[]{:S(2)}, u32[]{:S(2)}) collective-permute-start(f32[1,128]{1,0:T(1,128)S(1)} %add.3.refs_0_), channel_id=1, source_target_pairs={{0,128},{32,160},{64,192},{96,224},{128,0},{160,32},{192,64},{224,... | collective-permute-start | bytes 1544 | tf_op jit(solution)/shard_map/ppermute | solution.py:526
  55.9 0.2 collective-permute-start.3
  56.1 4.2 %faces.1 = (bf16[128,4096]{1,0:T(8,128)(2,1)}, f32[1,128]{1,0:T(1,128)}) custom-call(f32[128,256]{1,0:T(8,128)S(1)} %get-tuple-element.55.refs_0_, f32[128,256]{1,0:T(8,128)S(1)} %get-tuple-element.56.refs_1_, f32[128,256]{1,0:T(8,128)S(1)} %get-tuple-element.57.refs_2_, f32[128,256]{1,0:T(8,128)S(1)} %get-tuple-element.58.refs_3_, ...), custom_call_target="tpu_custom_call" | custom-call | flops 1000000000 | bytes 3949056 | tf_op jit(solution)/shard_map/faces/pallas_call | solution.py:509
  60.3 0.0 collective-permute-done.1.refs_1_
  60.3 0.0 collective-permute-done.2.refs_2_
  60.3 0.0 collective-permute-done.3.refs_3_
  60.3 0.8 %integrals.1 = f32[4,256]{1,0:T(4,128)} custom-call(f32[1,128]{1,0:T(1,128)S(1)} %add.3.refs_0_, f32[1,128]{1,0:T(1,128)S(1)} %collective-permute-done.1.refs_1_, f32[1,128]{1,0:T(1,128)S(1)} %collective-permute-done.2.refs_2_, f32[1,128]{1,0:T(1,128)S(1)} %collective-permute-done.3.refs_3_, f32[128,256]{1,0:T(8,128)S(1)} %get-tuple-element.72.refs_4_), custom_call_target="tpu_custom_call" | custom-call | bytes 137216 | tf_op jit(solution)/shard_map/integrals/pallas_call | solution.py:509
  (2 shorter events, 0.0 us)
Async XLA Ops:
  0.6 35.1 %copy-start = (bf16[1024,256]{1,0:T(8,128)(2,1)S(1)}, bf16[1024,256]{1,0:T(8,128)(2,1)}, u32[]{:S(2)}) copy-start(bf16[1024,256]{1,0:T(8,128)(2,1)} %constant.16.clone.refs_1_.hi_ref) | copy-start | bytes 1572868
  0.6 35.1 %copy-start.1 = (bf16[1024,256]{1,0:T(8,128)(2,1)S(1)}, bf16[1024,256]{1,0:T(8,128)(2,1)}, u32[]{:S(2)}) copy-start(bf16[1024,256]{1,0:T(8,128)(2,1)} %constant.17.clone.refs_2_.lo_ref) | copy-start | bytes 1572868
  0.7 35.1 %copy-start.2 = (bf16[256,256]{1,0:T(8,128)(2,1)S(1)}, bf16[256,256]{1,0:T(8,128)(2,1)}, u32[]{:S(2)}) copy-start(bf16[256,256]{1,0:T(8,128)(2,1)} %constant.21.clone.first_ref) | copy-start | bytes 393220
  3.3 20.8 %all-to-all-start = ((f32[32,2,128]{2,1,0:T(2,128)}), f32[32,2,128]{2,1,0:T(2,128)S(1)}, u32[]{:S(2)}, u32[]{:S(2)}) async-start(f32[32,2,128]{2,1,0:T(2,128)} %get-tuple-element.38), calls=%async_computation | async-start | bytes 65536 | tf_op jit(solution)/shard_map/all_to_all | solution.py:571
  31.8 14.5 %all-to-all-start.1 = ((f32[32,25,1,128]{3,2,1,0:T(1,128)}), f32[32,25,1,128]{3,2,1,0:T(1,128)S(1)}, u32[]{:S(2)}, u32[]{:S(2)}) async-start(f32[32,25,1,128]{3,2,1,0:T(1,128)} %bitcast.2), calls=%async_computation.1 | async-start | bytes 819200 | tf_op jit(solution)/shard_map/all_to_all | solution.py:613
  46.4 5.8 %collective-permute-start = (f32[1,128]{1,0:T(1,128)S(1)}, f32[1,128]{1,0:T(1,128)S(1)}, u32[]{:S(2)}, u32[]{:S(2)}) collective-permute-start(f32[1,128]{1,0:T(1,128)S(1)} %own.1), channel_id=1, source_target_pairs={{0,32},{32,0},{64,96},{96,64},{128,160},{160,128},{192,224},{224,1... | collective-permute-start | bytes 1544 | tf_op jit(solution)/shard_map/ppermute | solution.py:526
  52.2 8.1 %collective-permute-start.1 = (f32[1,128]{1,0:T(1,128)S(1)}, f32[1,128]{1,0:T(1,128)S(1)}, u32[]{:S(2)}, u32[]{:S(2)}) collective-permute-start(f32[1,128]{1,0:T(1,128)S(1)} %add.3.refs_0_), channel_id=1, source_target_pairs={{0,64},{32,96},{64,0},{96,32},{128,192},{160,224},{192,128},{224,1... | collective-permute-start | bytes 1544 | tf_op jit(solution)/shard_map/ppermute | solution.py:526
  53.4 6.8 %collective-permute-start.2 = (f32[1,128]{1,0:T(1,128)S(1)}, f32[1,128]{1,0:T(1,128)S(1)}, u32[]{:S(2)}, u32[]{:S(2)}) collective-permute-start(f32[1,128]{1,0:T(1,128)S(1)} %add.3.refs_0_), channel_id=1, source_target_pairs={{0,128},{32,160},{64,192},{96,224},{128,0},{160,32},{192,64},{224,... | collective-permute-start | bytes 1544 | tf_op jit(solution)/shard_map/ppermute | solution.py:526
  55.9 4.4 %collective-permute-start.3 = (f32[1,128]{1,0:T(1,128)S(1)}, f32[1,128]{1,0:T(1,128)S(1)}, u32[]{:S(2)}, u32[]{:S(2)}) collective-permute-start(f32[1,128]{1,0:T(1,128)S(1)} %add.3.refs_0_), channel_id=1, source_target_pairs={{0,192},{32,224},{64,128},{96,160},{128,64},{160,96},{192,0},{224,... | collective-permute-start | bytes 1544 | tf_op jit(solution)/shard_map/ppermute | solution.py:526
